TPU v7x, 256 devices: a whole 4x4x8 slice. The times are simulated.
256 devices in a mesh: ctx: 32 (over x, z), ch: 8 (over y, core).
Axes of the slice: x: 4, y: 4, z: 8, core: 2. Of those that a mesh axis runs over, the one named last changes fastest.
Arguments:
- query_gate: bfloat16 [16384, 4096], P('ctx', 'ch'), may hold values from -6 to 6
- key_gate: bfloat16 [16384, 4096], P('ctx', 'ch'), may hold values from -6 to 6
- value_in: bfloat16 [16384, 4096], P('ctx', 'ch'), may hold values from -6 to 6
- filter_taps: float32 [4096, 4096], P(None, 'ch'), may hold values from -0.09375 to 0.09375
- skip_gain: float32 [4096], P('ch'), may hold values from -4 to 4
- out_weight: bfloat16 [4096, 4096], P('ch'), may hold values from -0.09375 to 0.09375
Outputs:
- mixed_out: bfloat16 [16384, 4096], P('ctx', 'ch')
All inputs are finite; a program needn't handle non-finite values.
Results may differ from a plain program's by a relative error of at most 0.017.
Values may be sent and summed in bfloat16 or wider, within the bound.
No kernel may reach another device: no remote copies, remote signals or barrier semaphores. Data moves between devices by JAX's collectives and lax.ppermute only.
A program may use at most 128 MiB of HBM per device.

v0:
```python
import math

import jax
import jax.numpy as jnp
from jax import lax
from jax.sharding import PartitionSpec as P

WIN = 8


def passed_along(block, axis, distance):
    devices = range(lax.axis_size(axis))
    route = [(i - distance, i) for i in devices if i - distance in devices]
    return lax.ppermute(block, axis, route)


def forward_tables(length):
    freq_rows = jnp.arange(length + 1, dtype=jnp.int32)[:, None]
    time_cols = jnp.arange(length, dtype=jnp.int32)[None, :]
    turns = freq_rows * time_cols % (2 * length)
    angle = turns.astype(jnp.float32) * (math.pi / length)
    return (jnp.cos(angle), jnp.sin(angle))


def inverse_tables(length):
    out_rows = jnp.arange(length, dtype=jnp.int32)[:, None]
    freq_cols = jnp.arange(length + 1, dtype=jnp.int32)[None, :]
    turns = freq_cols * (out_rows + length) % (2 * length)
    angle = turns.astype(jnp.float32) * (math.pi / length)
    edge = jnp.logical_or(freq_cols == 0, freq_cols == length)
    factor = jnp.where(edge, 1.0, 2.0).astype(jnp.float32) / (2.0 * length)
    return (factor * jnp.cos(angle), factor * jnp.sin(angle))


def split_table(table):
    upper = table.astype(jnp.bfloat16)
    lower = (table - upper.astype(jnp.float32)).astype(jnp.bfloat16)
    return (upper, lower)


def table_product(parts, block):
    first = jnp.einsum("mn,knc->kmc", parts[0], block, preferred_element_type=jnp.float32)
    second = jnp.einsum("mn,knc->kmc", parts[1], block, preferred_element_type=jnp.float32)
    return first + second


def data_spectrum(block, cos_parts, sin_parts):
    return (table_product(cos_parts, block), -table_product(sin_parts, block))


def taps_spectrum(block, cos_table, sin_table):
    cos_part = jnp.einsum("mn,knc->kmc", cos_table, block, precision=lax.Precision.HIGH)
    sin_part = jnp.einsum("mn,knc->kmc", sin_table, block, precision=lax.Precision.HIGH)
    return (cos_part, -sin_part)


def lag_stack(payload):
    pieces = [payload]
    current = payload
    for lag_index in range(WIN):
        current = passed_along(current, "ctx", 1)
        pieces.append(current)
    return jnp.concatenate(pieces, axis=0)


def body(query_gate, key_gate, value_in, filter_taps, skip_gain, out_weight):
    length, width = query_gate.shape
    mixed_in = (key_gate.astype(jnp.float32) * value_in.astype(jnp.float32)).astype(jnp.bfloat16)
    cos_table, sin_table = forward_tables(length)
    cos_parts = split_table(cos_table)
    sin_parts = split_table(sin_table)
    tap_blocks = filter_taps.reshape(WIN, length, width)
    block_real, block_imag = taps_spectrum(tap_blocks, cos_table, sin_table)
    parity = 1.0 - 2.0 * (jnp.arange(length + 1, dtype=jnp.int32) % 2).astype(jnp.float32)
    parity = parity[None, :, None]
    zero_block = jnp.zeros((1, length + 1, width), jnp.float32)
    kernel_real = jnp.concatenate([zero_block, block_real], axis=0) + parity * jnp.concatenate(
        [block_real, zero_block], axis=0
    )
    kernel_imag = jnp.concatenate([zero_block, block_imag], axis=0) + parity * jnp.concatenate(
        [block_imag, zero_block], axis=0
    )
    own_real, own_imag = data_spectrum(mixed_in[None], cos_parts, sin_parts)
    packed = jnp.stack([own_real, own_imag], axis=1).astype(jnp.bfloat16)
    lagged = lag_stack(packed)
    span_real = lagged[:, 0].astype(jnp.float32)
    span_imag = lagged[:, 1].astype(jnp.float32)
    total_real = jnp.sum(kernel_real * span_real - kernel_imag * span_imag, axis=0)
    total_imag = jnp.sum(kernel_real * span_imag + kernel_imag * span_real, axis=0)
    inverse_cos, inverse_sin = inverse_tables(length)
    conv_out = jnp.dot(inverse_cos, total_real, precision=lax.Precision.HIGH) - jnp.dot(
        inverse_sin, total_imag, precision=lax.Precision.HIGH
    )
    combined = conv_out + skip_gain[None, :] * mixed_in.astype(jnp.float32)
    gated = (query_gate.astype(jnp.float32) * combined).astype(jnp.bfloat16)
    partial_value = jnp.dot(gated, out_weight, preferred_element_type=jnp.float32)
    return lax.psum_scatter(
        partial_value.astype(jnp.bfloat16), "ch", scatter_dimension=1, tiled=True
    )


def solution(mesh):
    in_specs = (
        P("ctx", "ch"),
        P("ctx", "ch"),
        P("ctx", "ch"),
        P(None, "ch"),
        P("ch"),
        P("ch", None),
    )
    out_specs = P("ctx", "ch")
    return jax.shard_map(body, mesh=mesh, in_specs=in_specs, out_specs=out_specs, check_vma=False)
```

profile of v0, /device:TPU:32, one launch (start us, length us, event | category | flops | bytes accessed | tf_op | source)
XLA Modules:
  0.0 323.2 jit_solution(1079235855472592371)
XLA Ops:
  7.9 4.0 %fusion.46 = f32[512,513]{0,1:T(8,128)S(1)} fusion(bf16[512,512]{1,0:T(8,128)(2,1)S(1)} %multiply_convert_fusion), kind=kOutput, calls=%fused_computation.69 | convolution fusion | flops 272899584 | bytes 1574912 | tf_op jit(solution)/shard_map/mn,knc->kmc/dot_general | solution.py:42
  11.9 4.0 %fusion.49 = f32[512,513]{0,1:T(8,128)S(1)} fusion(bf16[512,512]{1,0:T(8,128)(2,1)S(1)} %multiply_convert_fusion), kind=kOutput, calls=%fused_computation.70 | convolution fusion | flops 272899584 | bytes 1574912 | tf_op jit(solution)/shard_map/mn,knc->kmc/dot_general | solution.py:42
  15.9 16.3 %fusion.23 = bf16[1,1,513,512]{3,2,0,1:T(8,128)(2,1)S(1)} fusion(f32[512,513]{0,1:T(8,128)S(1)} %fusion.46, bf16[512,512]{1,0:T(8,128)(2,1)S(1)} %multiply_convert_fusion), kind=kOutput, calls=%fused_computation.41 | convolution fusion | flops 274475520 | bytes 2100224 | tf_op jit(solution)/shard_map/mn,knc->kmc/dot_general | solution.py:43
  32.2 4.4 %fusion.24 = bf16[1,1,513,512]{3,2,0,1:T(8,128)(2,1)S(1)} fusion(f32[512,513]{0,1:T(8,128)S(1)} %fusion.49, bf16[512,512]{1,0:T(8,128)(2,1)S(1)} %multiply_convert_fusion), kind=kOutput, calls=%fused_computation.42 | convolution fusion | flops 274212864 | bytes 2100224 | tf_op jit(solution)/shard_map/mn,knc->kmc/dot_general | solution.py:43
  42.3 23.0 %collective-permute-done = bf16[1,2,513,512]{3,1,2,0:T(2,128)(2,1)S(1)} collective-permute-done((bf16[1,2,513,512]{3,1,2,0:T(2,128)(2,1)S(1)}, bf16[1,2,513,512]{3,1,2,0:T(2,128)(2,1)S(1)}, u32[]{:S(2)}, u32[]{:S(2)}) %collective-permute-start) | collective-permute-done | bytes 1050656 | tf_op jit(solution)/shard_map/ppermute | solution.py:14
  69.2 22.1 %collective-permute-done.1 = bf16[1,2,513,512]{3,1,2,0:T(2,128)(2,1)S(1)} collective-permute-done((bf16[1,2,513,512]{3,1,2,0:T(2,128)(2,1)S(1)}, bf16[1,2,513,512]{3,1,2,0:T(2,128)(2,1)S(1)}, u32[]{:S(2)}, u32[]{:S(2)}) %collective-permute-start.1) | collective-permute-done | bytes 1050656 | tf_op jit(solution)/shard_map/ppermute | solution.py:14
  91.3 3.9 %collective-permute-start.2 = (bf16[1,2,513,512]{3,1,2,0:T(2,128)(2,1)S(1)}, bf16[1,2,513,512]{3,1,2,0:T(2,128)(2,1)S(1)}, u32[]{:S(2)}, u32[]{:S(2)}) collective-permute-start(bf16[1,2,513,512]{3,1,2,0:T(2,128)(2,1)S(1)} %collective-permute-done.1), channel_id=1, source_target_pairs={{0,8},{8,16},{16,24},{24,32},{32,40},{40,48},{48,56},{56,64},{64,7... | collective-permute-start | bytes 3151880 | tf_op jit(solution)/shard_map/ppermute | solution.py:14
  95.2 21.2 %collective-permute-done.2 = bf16[1,2,513,512]{3,1,2,0:T(2,128)(2,1)S(1)} collective-permute-done((bf16[1,2,513,512]{3,1,2,0:T(2,128)(2,1)S(1)}, bf16[1,2,513,512]{3,1,2,0:T(2,128)(2,1)S(1)}, u32[]{:S(2)}, u32[]{:S(2)}) %collective-permute-start.2) | collective-permute-done | bytes 1050656 | tf_op jit(solution)/shard_map/ppermute | solution.py:14
  116.4 5.1 %collective-permute-start.3 = (bf16[1,2,513,512]{3,1,2,0:T(2,128)(2,1)S(1)}, bf16[1,2,513,512]{3,1,2,0:T(2,128)(2,1)S(1)}, u32[]{:S(2)}, u32[]{:S(2)}) collective-permute-start(bf16[1,2,513,512]{3,1,2,0:T(2,128)(2,1)S(1)} %collective-permute-done.2), channel_id=1, source_target_pairs={{0,8},{8,16},{16,24},{24,32},{32,40},{40,48},{48,56},{56,64},{64,7... | collective-permute-start | bytes 3151880 | tf_op jit(solution)/shard_map/ppermute | solution.py:14
  121.5 19.9 %collective-permute-done.3 = bf16[1,2,513,512]{3,1,2,0:T(2,128)(2,1)S(1)} collective-permute-done((bf16[1,2,513,512]{3,1,2,0:T(2,128)(2,1)S(1)}, bf16[1,2,513,512]{3,1,2,0:T(2,128)(2,1)S(1)}, u32[]{:S(2)}, u32[]{:S(2)}) %collective-permute-start.3) | collective-permute-done | bytes 1050656 | tf_op jit(solution)/shard_map/ppermute | solution.py:14
  141.4 5.6 %collective-permute-start.4 = (bf16[1,2,513,512]{3,1,2,0:T(2,128)(2,1)S(1)}, bf16[1,2,513,512]{3,1,2,0:T(2,128)(2,1)}, u32[]{:S(2)}, u32[]{:S(2)}) collective-permute-start(bf16[1,2,513,512]{3,1,2,0:T(2,128)(2,1)S(1)} %collective-permute-done.3), channel_id=1, source_target_pairs={{0,8},{8,16},{16,24},{24,32},{32,40},{40,48},{48,56},{56,64},{64,7... | collective-permute-start | bytes 3151880 | tf_op jit(solution)/shard_map/ppermute | solution.py:14
  147.0 19.0 %collective-permute-done.4 = bf16[1,2,513,512]{3,1,2,0:T(2,128)(2,1)} collective-permute-done((bf16[1,2,513,512]{3,1,2,0:T(2,128)(2,1)S(1)}, bf16[1,2,513,512]{3,1,2,0:T(2,128)(2,1)}, u32[]{:S(2)}, u32[]{:S(2)}) %collective-permute-start.4) | collective-permute-done | bytes 1050656 | tf_op jit(solution)/shard_map/ppermute | solution.py:14
  166.0 5.6 %collective-permute-start.5 = (bf16[1,2,513,512]{3,1,2,0:T(2,128)(2,1)}, bf16[1,2,513,512]{3,1,2,0:T(2,128)(2,1)}, u32[]{:S(2)}, u32[]{:S(2)}) collective-permute-start(bf16[1,2,513,512]{3,1,2,0:T(2,128)(2,1)} %collective-permute-done.4), channel_id=1, source_target_pairs={{0,8},{8,16},{16,24},{24,32},{32,40},{40,48},{48,56},{56,64},{64,7... | collective-permute-start | bytes 3151880 | tf_op jit(solution)/shard_map/ppermute | solution.py:14
  171.7 11.5 %convolution_bitcast_fusion = f32[8,513,512]{2,1,0:T(8,128)S(1)} fusion(f32[8,512,512]{2,1,0:T(8,128)S(1)} %bitcast.49), kind=kOutput, calls=%fused_computation.14 | convolution fusion | flops 6458711040 | bytes 16793600 | tf_op jit(solution)/shard_map/mn,knc->kmc/dot_general | solution.py:52
  183.2 11.9 %negate_bitcast_fusion = f32[8,513,512]{2,1,0:T(8,128)S(1)} fusion(f32[8,512,512]{2,1,0:T(8,128)S(1)} %bitcast.50), kind=kOutput, calls=%fused_computation.10 | convolution fusion | flops 6460812288 | bytes 16793600 | tf_op jit(solution)/shard_map/mn,knc->kmc/dot_general | solution.py:53
  195.1 5.6 %collective-permute-start.6 = (bf16[1,2,513,512]{3,1,2,0:T(2,128)(2,1)}, bf16[1,2,513,512]{3,1,2,0:T(2,128)(2,1)S(1)}, u32[]{:S(2)}, u32[]{:S(2)}) collective-permute-start(bf16[1,2,513,512]{3,1,2,0:T(2,128)(2,1)} %collective-permute-done.5), channel_id=1, source_target_pairs={{0,8},{8,16},{16,24},{24,32},{32,40},{40,48},{48,56},{56,64},{64,7... | collective-permute-start | bytes 3151880 | tf_op jit(solution)/shard_map/ppermute | solution.py:14
  204.3 14.6 %collective-permute-done.6 = bf16[1,2,513,512]{3,1,2,0:T(2,128)(2,1)S(1)} collective-permute-done((bf16[1,2,513,512]{3,1,2,0:T(2,128)(2,1)}, bf16[1,2,513,512]{3,1,2,0:T(2,128)(2,1)S(1)}, u32[]{:S(2)}, u32[]{:S(2)}) %collective-permute-start.6) | collective-permute-done | bytes 1050656 | tf_op jit(solution)/shard_map/ppermute | solution.py:14
  218.9 6.8 %collective-permute-start.7 = (bf16[1,2,513,512]{3,1,2,0:T(2,128)(2,1)S(1)}, bf16[1,2,513,512]{3,1,2,0:T(2,128)(2,1)S(1)}, u32[]{:S(2)}, u32[]{:S(2)}) collective-permute-start(bf16[1,2,513,512]{3,1,2,0:T(2,128)(2,1)S(1)} %collective-permute-done.6), channel_id=1, source_target_pairs={{0,8},{8,16},{16,24},{24,32},{32,40},{40,48},{48,56},{56,64},{64,7... | collective-permute-start | bytes 3151880 | tf_op jit(solution)/shard_map/ppermute | solution.py:14
  233.0 8.7 %collective-permute-done.7 = bf16[1,2,513,512]{3,1,2,0:T(2,128)(2,1)S(1)} collective-permute-done((bf16[1,2,513,512]{3,1,2,0:T(2,128)(2,1)S(1)}, bf16[1,2,513,512]{3,1,2,0:T(2,128)(2,1)S(1)}, u32[]{:S(2)}, u32[]{:S(2)}) %collective-permute-start.7) | collective-permute-done | bytes 1050656 | tf_op jit(solution)/shard_map/ppermute | solution.py:14
  242.8 8.7 %fusion.1 = (f32[513,512]{1,0:T(8,128)S(1)}, f32[513,512]{1,0:T(8,128)S(1)}) fusion(f32[8,513,512]{2,1,0:T(8,128)S(1)} %convolution_bitcast_fusion, f32[8,513,512]{2,1,0:T(8,128)S(1)} %negate_bitcast_fusion, f32[513]{0:T(1024)S(1)} %fusion.53, bf16[9,2,513,512]{3,2,0,1:T(8,128)(2,1)} %copy_dynamic-update-slice_fusion), kind=kLoop, calls=%fused_computation.5 | loop fusion | flops 32569344 | bytes 28368900 | tf_op jit(solution)/shard_map/reduce_sum | solution.py:88
  251.6 6.1 %fusion.10 = f32[512,512]{1,0:T(8,128)S(1)} fusion(f32[513,512]{1,0:T(8,128)S(1)} %get-tuple-element.6, s32[512]{0:T(512)S(1)} %iota_add_fusion, f32[513]{0:T(1024)S(1)} %select_multiply_fusion), kind=kOutput, calls=%fused_computation.30 | convolution fusion | flops 810819072 | bytes 2103300 | tf_op jit(solution)/shard_map/dot_general | solution.py:91
  257.7 6.5 %fusion.20 = bf16[512,512]{1,0:T(8,128)(2,1)S(1)} fusion(f32[512,512]{1,0:T(8,128)S(1)} %fusion.10, f32[513,512]{1,0:T(8,128)S(1)} %get-tuple-element.5, bf16[512,512]{1,0:T(8,128)(2,1)S(1)} %copy-done.1, bf16[512,512]{1,0:T(8,128)(2,1)S(1)} %copy-done.3, s32[512]{0:T(512)S(1)} %iota_add_fusion, f32[513]{0:T(1024)S(1)} %select_multiply_fusion, ...), kind=kOutput, calls=%fused_computation.40 | convolution fusion | flops 812654080 | bytes 3678212 | tf_op jit(solution)/shard_map/dot_general | solution.py:91
  264.3 4.3 %convolution_convert_fusion = bf16[512,4096]{1,0:T(8,128)(2,1)} fusion(bf16[512,512]{1,0:T(8,128)(2,1)S(1)} %fusion.20, bf16[512,4096]{1,0:T(8,128)(2,1)S(1)} %copy-done.2), kind=kOutput, calls=%fused_computation.11 | convolution fusion | flops 2149580800 | bytes 8912896 | tf_op jit(solution)/shard_map/dot_general | solution.py:96
  268.6 47.6 %reduce-scatter.2.cloned.1.call-done = bf16[512,512]{1,0:T(8,128)(2,1)} async-done(((bf16[512,4096]{1,0:T(8,128)(2,1)}), bf16[512,512]{1,0:T(8,128)(2,1)}) %reduce-scatter.2.cloned.1.call-update) | async-done | bytes 524304 | tf_op jit(solution)/shard_map/reduce_scatter | solution.py:97
  (34 shorter events, 22.9 us)
Async XLA Ops:
  6.5 309.6 %reduce-scatter.2.cloned.1.call-start = ((), (), s32[]{:S(2)}) async-start(), calls=%async_computation.1 | async-start | bytes 4718592 | tf_op jit(solution)/shard_map/reduce_scatter | solution.py:97
  7.9 24.3 %copy-start = (bf16[512,512]{1,0:T(8,128)(2,1)}, bf16[512,512]{1,0:T(8,128)(2,1)S(1)}, u32[]{:S(2)}) copy-start(bf16[512,512]{1,0:T(8,128)(2,1)S(1)} %multiply_convert_fusion) | copy-start | bytes 1572868
  15.9 155.8 %slice-start = ((s8[8388608]{0:T(1024)(128)(4,1)}), s8[4194304]{0:T(1024)(128)(4,1)S(1)}, s32[]{:S(2)}) async-start(s8[8388608]{0:T(1024)(128)(4,1)} %bitcast.47), calls=%async_computation.2 | async-start | bytes 8388608
  32.2 139.5 %slice-start.1 = ((s8[8388608]{0:T(1024)(128)(4,1)}), s8[4194304]{0:T(1024)(128)(4,1)S(1)}, s32[]{:S(2)}) async-start(s8[8388608]{0:T(1024)(128)(4,1)} %bitcast.47), calls=%async_computation.3 | async-start | bytes 8388608
  38.5 26.8 %collective-permute-start = (bf16[1,2,513,512]{3,1,2,0:T(2,128)(2,1)S(1)}, bf16[1,2,513,512]{3,1,2,0:T(2,128)(2,1)S(1)}, u32[]{:S(2)}, u32[]{:S(2)}) collective-permute-start(bf16[1,2,513,512]{3,1,2,0:T(2,128)(2,1)S(1)} %copy.7), channel_id=1, source_target_pairs={{0,8},{8,16},{16,24},{24,32},{32,40},{40,48},{48,56},{56,64},{64,7... | collective-permute-start | bytes 3151880 | tf_op jit(solution)/shard_map/ppermute | solution.py:14
  65.3 26.0 %collective-permute-start.1 = (bf16[1,2,513,512]{3,1,2,0:T(2,128)(2,1)S(1)}, bf16[1,2,513,512]{3,1,2,0:T(2,128)(2,1)S(1)}, u32[]{:S(2)}, u32[]{:S(2)}) collective-permute-start(bf16[1,2,513,512]{3,1,2,0:T(2,128)(2,1)S(1)} %collective-permute-done), channel_id=1, source_target_pairs={{0,8},{8,16},{16,24},{24,32},{32,40},{40,48},{48,56},{56,64},{64,7... | collective-permute-start | bytes 3151880 | tf_op jit(solution)/shard_map/ppermute | solution.py:14
  91.3 25.1 %collective-permute-start.2 = (bf16[1,2,513,512]{3,1,2,0:T(2,128)(2,1)S(1)}, bf16[1,2,513,512]{3,1,2,0:T(2,128)(2,1)S(1)}, u32[]{:S(2)}, u32[]{:S(2)}) collective-permute-start(bf16[1,2,513,512]{3,1,2,0:T(2,128)(2,1)S(1)} %collective-permute-done.1), channel_id=1, source_target_pairs={{0,8},{8,16},{16,24},{24,32},{32,40},{40,48},{48,56},{56,64},{64,7... | collective-permute-start | bytes 3151880 | tf_op jit(solution)/shard_map/ppermute | solution.py:14
  116.4 25.0 %collective-permute-start.3 = (bf16[1,2,513,512]{3,1,2,0:T(2,128)(2,1)S(1)}, bf16[1,2,513,512]{3,1,2,0:T(2,128)(2,1)S(1)}, u32[]{:S(2)}, u32[]{:S(2)}) collective-permute-start(bf16[1,2,513,512]{3,1,2,0:T(2,128)(2,1)S(1)} %collective-permute-done.2), channel_id=1, source_target_pairs={{0,8},{8,16},{16,24},{24,32},{32,40},{40,48},{48,56},{56,64},{64,7... | collective-permute-start | bytes 3151880 | tf_op jit(solution)/shard_map/ppermute | solution.py:14
  141.4 24.6 %collective-permute-start.4 = (bf16[1,2,513,512]{3,1,2,0:T(2,128)(2,1)S(1)}, bf16[1,2,513,512]{3,1,2,0:T(2,128)(2,1)}, u32[]{:S(2)}, u32[]{:S(2)}) collective-permute-start(bf16[1,2,513,512]{3,1,2,0:T(2,128)(2,1)S(1)} %collective-permute-done.3), channel_id=1, source_target_pairs={{0,8},{8,16},{16,24},{24,32},{32,40},{40,48},{48,56},{56,64},{64,7... | collective-permute-start | bytes 3151880 | tf_op jit(solution)/shard_map/ppermute | solution.py:14
  166.0 29.1 %collective-permute-start.5 = (bf16[1,2,513,512]{3,1,2,0:T(2,128)(2,1)}, bf16[1,2,513,512]{3,1,2,0:T(2,128)(2,1)}, u32[]{:S(2)}, u32[]{:S(2)}) collective-permute-start(bf16[1,2,513,512]{3,1,2,0:T(2,128)(2,1)} %collective-permute-done.4), channel_id=1, source_target_pairs={{0,8},{8,16},{16,24},{24,32},{32,40},{40,48},{48,56},{56,64},{64,7... | collective-permute-start | bytes 3151880 | tf_op jit(solution)/shard_map/ppermute | solution.py:14
  195.1 23.8 %collective-permute-start.6 = (bf16[1,2,513,512]{3,1,2,0:T(2,128)(2,1)}, bf16[1,2,513,512]{3,1,2,0:T(2,128)(2,1)S(1)}, u32[]{:S(2)}, u32[]{:S(2)}) collective-permute-start(bf16[1,2,513,512]{3,1,2,0:T(2,128)(2,1)} %collective-permute-done.5), channel_id=1, source_target_pairs={{0,8},{8,16},{16,24},{24,32},{32,40},{40,48},{48,56},{56,64},{64,7... | collective-permute-start | bytes 3151880 | tf_op jit(solution)/shard_map/ppermute | solution.py:14
  218.9 22.7 %collective-permute-start.7 = (bf16[1,2,513,512]{3,1,2,0:T(2,128)(2,1)S(1)}, bf16[1,2,513,512]{3,1,2,0:T(2,128)(2,1)S(1)}, u32[]{:S(2)}, u32[]{:S(2)}) collective-permute-start(bf16[1,2,513,512]{3,1,2,0:T(2,128)(2,1)S(1)} %collective-permute-done.6), channel_id=1, source_target_pairs={{0,8},{8,16},{16,24},{24,32},{32,40},{40,48},{48,56},{56,64},{64,7... | collective-permute-start | bytes 3151880 | tf_op jit(solution)/shard_map/ppermute | solution.py:14
  251.5 6.1 %copy-start.1 = (bf16[512,512]{1,0:T(8,128)(2,1)S(1)}, bf16[512,512]{1,0:T(8,128)(2,1)}, u32[]{:S(2)}) copy-start(bf16[512,512]{1,0:T(8,128)(2,1)} %copy-done) | copy-start | bytes 1572868
  251.6 6.1 %copy-start.3 = (bf16[512,512]{1,0:T(8,128)(2,1)S(1)}, bf16[512,512]{1,0:T(8,128)(2,1)}, u32[]{:S(2)}) copy-start(bf16[512,512]{1,0:T(8,128)(2,1)} %param.6) | copy-start | bytes 1572868
  251.6 6.1 %copy-start.4 = (f32[512]{0:T(512)S(1)}, f32[512]{0:T(512)}, u32[]{:S(2)}) copy-start(f32[512]{0:T(512)} %param.10) | copy-start | bytes 6148
  257.7 6.6 %copy-start.2 = (bf16[512,4096]{1,0:T(8,128)(2,1)S(1)}, bf16[512,4096]{1,0:T(8,128)(2,1)}, u32[]{:S(2)}) copy-start(bf16[512,4096]{1,0:T(8,128)(2,1)} %param.11) | copy-start | bytes 12582916
Sparse Core Ops, SparseCore 0:
  268.7 47.4 reduce-scatter.1
where the time goes:
time: 324 us; the launch traced here: 323 us
  waiting for transfers between devices  176 us (54%)
  matrix products  69 us (21%)
  starting transfers between devices  40.2 us (12%)
  between operations  13.8 us (4%)
  local copies, waits for them, and re-layouts  12.8 us (4%)
  other arithmetic  11.2 us (3%)
    ppermute x8, waiting for transfers between devices, passed_along(): return lax.ppermute(block, axis, route)  129 us
    reduce_scatter x1, waiting for transfers between devices, body(): lax.psum_scatter(partial_value.astype(jnp.bfloat16), 'ch', scatter_dimens...  47.6 us
    ppermute x8, starting transfers between devices, passed_along(): return lax.ppermute(block, axis, route)  40.2 us
    dot_general x2, matrix products, table_product(): jnp.einsum('mn,knc->kmc', parts[1], block, preferred_element_type=jnp.flo...  20.7 us
    dot_general x1, matrix products, taps_spectrum(): jnp.einsum('mn,knc->kmc', sin_table, block, precision=lax.Precision.HIGH)  11.9 us
    dot_general x1, matrix products, taps_spectrum(): jnp.einsum('mn,knc->kmc', cos_table, block, precision=lax.Precision.HIGH)  11.5 us
    unnamed x21, local copies, waits for them, and re-layouts  10.8 us
    reduce_sum x1, other arithmetic, body(): jnp.sum(kernel_real * span_real - kernel_imag * span_imag, axis=0)  8.7 us
  transfers between devices with their start and end apart: 9, of which 8 were waited for; matrix products, arithmetic and copies ran while one was open for 11% of the time, Pallas kernels for 0%

commit v1 on v0

v1 whole, which is shorter than its diff:
```python
import functools

import jax
import jax.numpy as jnp
import numpy as np
from jax import lax
from jax.experimental import pallas as pl
from jax.experimental.pallas import tpu as pltpu
from jax.sharding import PartitionSpec as P

WIN = 8
LANES = 128
CORES = 2


def odd_tables(length):
    order = np.concatenate([np.arange(0, length, 2), np.arange(1, length, 2)])
    turns = (np.arange(length)[:, None] * (2 * order[None, :] + 1)) % (4 * length)
    angle = turns * (np.pi / (2 * length))
    tiles = length // LANES
    cos_part = np.cos(angle).reshape(length, tiles, LANES)
    sin_part = -np.sin(angle).reshape(length, tiles, LANES)
    table = np.concatenate([cos_part, sin_part], axis=2).transpose(1, 0, 2)
    return table.astype(jnp.bfloat16)


def mix_kernel(key_ref, value_ref, mixed_ref, turned_ref):
    product = (key_ref[...].astype(jnp.float32) * value_ref[...].astype(jnp.float32)).astype(jnp.bfloat16)
    mixed_ref[...] = product
    turned_ref[...] = product.T


def mix(key_gate, value_in):
    length, width = key_gate.shape
    return pl.pallas_call(
        mix_kernel,
        grid=(width // LANES,),
        in_specs=[pl.BlockSpec((length, LANES), lambda i: (0, i))] * 2,
        out_specs=[
            pl.BlockSpec((length, LANES), lambda i: (0, i)),
            pl.BlockSpec((LANES, length), lambda i: (i, 0)),
        ],
        out_shape=[
            jax.ShapeDtypeStruct((length, width), jnp.bfloat16),
            jax.ShapeDtypeStruct((width, length), jnp.bfloat16),
        ],
        cost_estimate=pl.CostEstimate(flops=length * width, bytes_accessed=8 * length * width, transcendentals=0),
        name="mix",
    )(key_gate, value_in)


def taps_kernel(few, place_ref, taps_ref, table_ref, out_ref, turned):
    step = pl.program_id(0)
    length = table_ref.shape[1]
    first = place_ref[1] * few
    rows = lax.broadcasted_iota(jnp.int32, (few, LANES), 0)
    lanes = lax.broadcasted_iota(jnp.int32, (few, LANES), 1)
    pick = (lanes == rows + first).astype(jnp.bfloat16)
    picked = lax.dot_general(
        pick, taps_ref[...].astype(jnp.bfloat16), (((1,), (1,)), ((), ())), preferred_element_type=jnp.float32
    ).astype(jnp.bfloat16)
    for half in range(2):
        start = pl.multiple_of((2 * step + half) * few, few)
        turned[pl.ds(start, few), :] = picked[:, half * length : (half + 1) * length]

    @pl.when(step == pl.num_programs(0) - 1)
    def _():
        for tile in range(table_ref.shape[0]):
            out_ref[tile] = jnp.dot(turned[...], table_ref[tile], preferred_element_type=jnp.float32)


def taps_spectrum(place, filter_taps, table, few):
    tiles, length, pair = table.shape
    rows = WIN * few
    return pl.pallas_call(
        functools.partial(taps_kernel, few),
        grid_spec=pltpu.PrefetchScalarGridSpec(
            num_scalar_prefetch=1,
            grid=(WIN // 2,),
            in_specs=[
                pl.BlockSpec((2 * length, LANES), lambda i, place: (i, place[0])),
                pl.BlockSpec((tiles, length, pair), lambda i, place: (0, 0, 0)),
            ],
            out_specs=pl.BlockSpec((tiles, rows, pair), lambda i, place: (0, 0, 0)),
            scratch_shapes=[pltpu.VMEM((rows, length), jnp.bfloat16)],
        ),
        out_shape=jax.ShapeDtypeStruct((tiles, rows, pair), jnp.float32),
        cost_estimate=pl.CostEstimate(
            flops=2 * rows * length * tiles * pair, bytes_accessed=3 << 20, transcendentals=0
        ),
        name="taps_spectrum",
    )(place, filter_taps, table)


def conv_kernel(few, x_ref, h_ref, table_ref, out_ref, window, total, product, gathered):
    tile = pl.program_id(0)
    tiles = pl.num_programs(0)
    count, length = x_ref.shape
    spans = count // few
    spectrum = jnp.dot(x_ref[...], table_ref[0], preferred_element_type=jnp.float32)
    real, imag = spectrum[:, :LANES], spectrum[:, LANES:]
    sign = jnp.where(tile < tiles // 2, 1.0, -1.0).astype(jnp.float32)
    zero = jnp.zeros((few, LANES), jnp.float32)
    before_real = jnp.concatenate([zero, real[:-few]], axis=0)
    before_imag = jnp.concatenate([zero, imag[:-few]], axis=0)
    window_real = before_real + sign * imag
    window_imag = before_imag - sign * real
    window[0] = window_real
    window[1] = window_imag
    window[2] = window_real + window_imag
    for part in range(few // 8):
        low = part * 8
        first, plus, minus = [], [], []
        for lag in range(WIN):
            h_real = h_ref[0, lag * few + low : lag * few + low + 8, :LANES]
            h_imag = h_ref[0, lag * few + low : lag * few + low + 8, LANES:]
            first.append(h_real)
            plus.append(h_real + h_imag)
            minus.append(h_imag - h_real)
        for span in range(spans):
            one = two = three = None
            for lag in range(min(WIN, span + 1)):
                at = (span - lag) * few + low
                term_one = first[lag] * window[2, at : at + 8, :]
                term_two = plus[lag] * window[1, at : at + 8, :]
                term_three = minus[lag] * window[0, at : at + 8, :]
                one = term_one if one is None else one + term_one
                two = term_two if two is None else two + term_two
                three = term_three if three is None else three + term_three
            at = span * few + low
            total[0, at : at + 8, :] = one + three
            total[1, at : at + 8, :] = one - two
    scale = sign * (1.0 / length)
    product[:, :LANES] = (-scale * total[0]).astype(jnp.bfloat16)
    product[:, LANES:] = (scale * total[1]).astype(jnp.bfloat16)
    part_out = lax.dot_general(
        product[...], table_ref[0], (((1,), (1,)), ((), ())), preferred_element_type=jnp.float32
    )

    @pl.when(tile == 0)
    def _():
        gathered[...] = part_out

    @pl.when(tile > 0)
    def _():
        gathered[...] += part_out

    @pl.when(tile == tiles - 1)
    def _():
        out_ref[...] = gathered[...].astype(jnp.bfloat16)


def convolve(turned, spectrum, table, few):
    count, length = turned.shape
    tiles, _, pair = table.shape
    rows = WIN * few
    return pl.pallas_call(
        functools.partial(conv_kernel, few),
        grid=(tiles,),
        in_specs=[
            pl.BlockSpec((count, length), lambda i: (0, 0)),
            pl.BlockSpec((1, rows, pair), lambda i: (i, 0, 0)),
            pl.BlockSpec((1, length, pair), lambda i: (i, 0, 0)),
        ],
        out_specs=pl.BlockSpec((count, length), lambda i: (0, 0)),
        out_shape=jax.ShapeDtypeStruct((count, length), jnp.bfloat16),
        scratch_shapes=[
            pltpu.VMEM((3, count, LANES), jnp.float32),
            pltpu.VMEM((2, count, LANES), jnp.float32),
            pltpu.VMEM((count, pair), jnp.bfloat16),
            pltpu.VMEM((count, length), jnp.float32),
        ],
        cost_estimate=pl.CostEstimate(
            flops=4 * count * length * tiles * pair, bytes_accessed=3 << 20, transcendentals=0
        ),
        name="convolve",
    )(turned, spectrum, table)


def project_kernel(place_ref, conv_ref, mixed_ref, query_ref, skip_ref, weight_ref, out_ref, gated):
    @pl.when(pl.program_id(0) == 0)
    def _():
        conv = conv_ref[...].T.astype(jnp.float32)
        combined = conv + skip_ref[...] * mixed_ref[...].astype(jnp.float32)
        gated[...] = (query_ref[...].astype(jnp.float32) * combined).astype(jnp.bfloat16)

    out_ref[0] = jnp.dot(gated[...], weight_ref[...], preferred_element_type=jnp.float32).astype(jnp.bfloat16)


def project(blocks, conv_turned, mixed, query_gate, skip_gain, out_weight):
    length, width = mixed.shape
    number = blocks.shape[0]
    return pl.pallas_call(
        project_kernel,
        grid_spec=pltpu.PrefetchScalarGridSpec(
            num_scalar_prefetch=1,
            grid=(number,),
            in_specs=[
                pl.BlockSpec((width, length), lambda i, blocks: (0, 0)),
                pl.BlockSpec((length, width), lambda i, blocks: (0, 0)),
                pl.BlockSpec((length, width), lambda i, blocks: (0, 0)),
                pl.BlockSpec((1, width), lambda i, blocks: (0, 0)),
                pl.BlockSpec((width, width), lambda i, blocks: (0, blocks[i])),
            ],
            out_specs=pl.BlockSpec((1, length, width), lambda i, blocks: (i, 0, 0)),
            scratch_shapes=[pltpu.VMEM((length, width), jnp.bfloat16)],
        ),
        out_shape=jax.ShapeDtypeStruct((number, length, width), jnp.bfloat16),
        cost_estimate=pl.CostEstimate(
            flops=2 * length * width * width * number, bytes_accessed=10 << 20, transcendentals=0
        ),
        name="project",
    )(blocks, conv_turned, mixed, query_gate, skip_gain.reshape(1, width), out_weight)


def added(*terms):
    total = terms[0].astype(jnp.float32)
    for term in terms[1:]:
        total = total + term.astype(jnp.float32)
    return total.astype(jnp.bfloat16)


def body(query_gate, key_gate, value_in, filter_taps, skip_gain, out_weight):
    length, width = query_gate.shape
    ctx, groups = lax.axis_size("ctx"), lax.axis_size("ch")
    ring = groups // CORES
    few = width // ctx
    here, group = lax.axis_index("ctx"), lax.axis_index("ch")
    y, core = group // CORES, group % CORES
    per_tile = LANES // few
    table = jnp.asarray(odd_tables(length))

    mixed, turned = mix(key_gate, value_in)
    place = jnp.stack([here // per_tile, here % per_tile]).astype(jnp.int32)
    spectrum = taps_spectrum(place, filter_taps, table, few)
    long_rows = lax.all_to_all(turned.reshape(ctx, few, length), "ctx", 0, 0)
    conv_rows = convolve(long_rows.reshape(ctx * few, length), spectrum, table, few)
    conv_turned = lax.all_to_all(conv_rows.reshape(ctx, few, length), "ctx", 0, 0).reshape(width, length)

    ahead = (y + jnp.array([2, 1, 3, 0], jnp.int32)) % ring
    blocks = jnp.concatenate([ahead * CORES + (1 - core), ahead * CORES + core]).astype(jnp.int32)
    parts = project(blocks, conv_turned, mixed, query_gate, skip_gain, out_weight)

    def ch_shift(block, dy, dcore):
        route = [(i, ((i // CORES + dy) % ring) * CORES + (i % CORES + dcore) % CORES) for i in range(groups)]
        return lax.ppermute(block, "ch", route)

    partner = ch_shift(parts[:ring], 0, 1)
    half = length // 2
    across_low = added(parts[ring, :half], partner[0, :half])
    across_high = added(parts[ring, half:], partner[0, half:])
    got_across_low = ch_shift(across_low, 1, 0)
    got_across_high = ch_shift(across_high, -1, 0)
    up_high = ch_shift(added(parts[ring + 1, half:], partner[1, half:]), 1, 0)
    down_low = ch_shift(added(parts[ring + 2, :half], partner[2, :half]), -1, 0)
    up_low = ch_shift(added(parts[ring + 1, :half], partner[1, :half], got_across_low), 1, 0)
    down_high = ch_shift(added(parts[ring + 2, half:], partner[2, half:], got_across_high), -1, 0)
    low = added(parts[ring + 3, :half], partner[3, :half], down_low, up_low)
    high = added(parts[ring + 3, half:], partner[3, half:], up_high, down_high)
    return jnp.concatenate([low, high], axis=0)


def solution(mesh):
    in_specs = (
        P("ctx", "ch"),
        P("ctx", "ch"),
        P("ctx", "ch"),
        P(None, "ch"),
        P("ch"),
        P("ch", None),
    )
    out_specs = P("ctx", "ch")
    return jax.shard_map(body, mesh=mesh, in_specs=in_specs, out_specs=out_specs, check_vma=False)
```

time: 324 us -> 107 us (0.33)
  waiting for transfers between devices: 176 us -> 51.6 us
  matrix products: 69 us -> 0 us
  Pallas kernels: 0 us -> 24.8 us
  starting transfers between devices: 40.2 us -> 23.8 us
  between operations: 13.8 us -> 0.12 us
  local copies, waits for them, and re-layouts: 12.8 us -> 3.51 us
  other arithmetic: 11.2 us -> 2.8 us
    ppermute x8 -> x7, waiting for transfers between devices: 129 us -> 23.1 us  [ch_shift(): return lax.ppermute(block, 'ch', route)]
    dot_general x9 -> x0, matrix products: 69 us -> none  [the longest x2 20.7 us: table_product(): jnp.einsum('mn,knc->kmc', parts[1], block, preferred_element_type=jnp.flo...]
    reduce_scatter x1 -> x0, waiting for transfers between devices: 47.6 us -> none  [body(): lax.psum_scatter(partial_value.astype(jnp.bfloat16), 'ch', scatter_dimens...]
    ppermute x8 -> x7, starting transfers between devices: 40.2 us -> 7.77 us  [ch_shift(): return lax.ppermute(block, 'ch', route)]
    all_to_all x0 -> x2, waiting for transfers between devices: none -> 28.5 us  [the longest x1 16.3 us: body(): lax.all_to_all(conv_rows.reshape(ctx, few, length), 'ctx', 0, 0)]
    pallas_call x0 -> x4, Pallas kernels: none -> 24.8 us  [the longest x1 9.48 us: project(): pl.pallas_call(project_kernel, grid_spec=pltpu.PrefetchScalarGridSpec(num...]
    all_to_all x0 -> x2, starting transfers between devices: none -> 16 us  [the longest x1 11.2 us: body(): long_rows = lax.all_to_all(turned.reshape(ctx, few, length), 'ctx', 0, 0)]
    unnamed x21 -> x8, local copies, waits for them, and re-layouts: 10.8 us -> 1.63 us
  transfers between devices with their start and end apart: 9 -> 9, of which waited for: 8 -> 8; matrix products, arithmetic and copies ran while one was open for 11% -> 1% of each run, Pallas kernels for 0% -> 4%
where the time goes in v1:
time: 107 us
  waiting for transfers between devices  51.6 us (48%)
  Pallas kernels  24.8 us (23%)
  starting transfers between devices  23.8 us (22%)
  local copies, waits for them, and re-layouts  3.51 us (3%)
  other arithmetic  2.8 us (3%)
    ppermute x7, waiting for transfers between devices, ch_shift(): return lax.ppermute(block, 'ch', route)  23.1 us
    all_to_all x1, waiting for transfers between devices, body(): lax.all_to_all(conv_rows.reshape(ctx, few, length), 'ctx', 0, 0)  16.3 us
    all_to_all x1, waiting for transfers between devices, body(): long_rows = lax.all_to_all(turned.reshape(ctx, few, length), 'ctx', 0, 0)  12.2 us
    all_to_all x1, starting transfers between devices, body(): long_rows = lax.all_to_all(turned.reshape(ctx, few, length), 'ctx', 0, 0)  11.2 us
    pallas_call x1, Pallas kernels, project(): pl.pallas_call(project_kernel, grid_spec=pltpu.PrefetchScalarGridSpec(num...  9.48 us
    ppermute x7, starting transfers between devices, ch_shift(): return lax.ppermute(block, 'ch', route)  7.77 us
    pallas_call x1, Pallas kernels, convolve(): pl.pallas_call(functools.partial(conv_kernel, few), grid=(tiles,), in_spe...  7.08 us
    all_to_all x1, starting transfers between devices, body(): lax.all_to_all(conv_rows.reshape(ctx, few, length), 'ctx', 0, 0)  4.86 us
  transfers between devices with their start and end apart: 9, of which 8 were waited for; matrix products, arithmetic and copies ran while one was open for 1% of the time, Pallas kernels for 4%

profile of v1, /device:TPU:32, one launch (start us, length us, event | category | flops | bytes accessed | tf_op | source)
XLA Modules:
  0.0 106.6 jit_solution(11894537132726801488)
XLA Ops:
  0.0 3.5 %mix.1 = (bf16[512,512]{1,0:T(8,128)(2,1)}, bf16[512,512]{1,0:T(8,128)(2,1)}) custom-call(bf16[512,512]{1,0:T(8,128)(2,1)} %key_ref.1, bf16[512,512]{1,0:T(8,128)(2,1)} %value_ref.1), custom_call_target="tpu_custom_call" | custom-call | flops 262144 | bytes 2097152 | tf_op jit(solution)/shard_map/mix/pallas_call | solution.py:35
  3.5 11.2 %all-to-all-start = ((bf16[32,16,512]{2,1,0:T(8,128)(2,1)}), bf16[32,16,512]{2,1,0:T(8,128)(2,1)S(1)}, u32[]{:S(2)}, u32[]{:S(2)}) async-start(bf16[32,16,512]{2,1,0:T(8,128)(2,1)} %bitcast.38), calls=%async_computation | async-start | bytes 1048576 | tf_op jit(solution)/shard_map/all_to_all | solution.py:236
  14.7 0.6 pad_add_fusion.1.place_ref
  15.3 4.8 %taps_spectrum.1.h_ref = f32[4,128,256]{2,1,0:T(8,128)} custom-call(s32[2]{0:T(128)} %pad_add_fusion.1.place_ref, f32[4096,512]{1,0:T(8,128)} %taps_ref.1, bf16[4,512,256]{2,1,0:T(8,128)(2,1)} %constant.71.clone.table_ref), custom_call_target="tpu_custom_call" | custom-call | flops 134217728 | bytes 3145728 | tf_op jit(solution)/shard_map/taps_spectrum/pallas_call | solution.py:75
  20.1 12.2 %all-to-all-done = bf16[32,16,512]{2,1,0:T(8,128)(2,1)S(1)} async-done(((bf16[32,16,512]{2,1,0:T(8,128)(2,1)}), bf16[32,16,512]{2,1,0:T(8,128)(2,1)S(1)}, u32[]{:S(2)}, u32[]{:S(2)}) %all-to-all-start) | async-done | bytes 524320 | tf_op jit(solution)/shard_map/all_to_all | solution.py:236
  32.3 0.8 copy-done.2
  33.1 7.1 %convolve.1 = bf16[512,512]{1,0:T(8,128)(2,1)} custom-call(bf16[512,512]{1,0:T(8,128)(2,1)} %bitcast.37, f32[4,128,256]{2,1,0:T(8,128)} %taps_spectrum.1.h_ref, bf16[4,512,256]{2,1,0:T(8,128)(2,1)} %constant.71.clone.table_ref), custom_call_target="tpu_custom_call" | custom-call | flops 1073741824 | bytes 3145728 | tf_op jit(solution)/shard_map/convolve/pallas_call | solution.py:157
  40.2 4.9 %all-to-all-start.1 = ((bf16[32,16,512]{2,1,0:T(8,128)(2,1)}), bf16[32,16,512]{2,1,0:T(8,128)(2,1)S(1)}, u32[]{:S(2)}, u32[]{:S(2)}) async-start(bf16[32,16,512]{2,1,0:T(8,128)(2,1)} %bitcast.36), calls=%async_computation.1 | async-start | bytes 1048576 | tf_op jit(solution)/shard_map/all_to_all | solution.py:238
  45.7 16.3 %all-to-all-done.1 = bf16[32,16,512]{2,1,0:T(8,128)(2,1)S(1)} async-done(((bf16[32,16,512]{2,1,0:T(8,128)(2,1)}), bf16[32,16,512]{2,1,0:T(8,128)(2,1)S(1)}, u32[]{:S(2)}, u32[]{:S(2)}) %all-to-all-start.1) | async-done | bytes 524320 | tf_op jit(solution)/shard_map/all_to_all | solution.py:238
  62.0 0.8 copy-done.1
  62.8 9.5 %project.1 = bf16[8,512,512]{2,1,0:T(8,128)(2,1)} custom-call(s32[8]{0:T(128)} %pad_add_fusion.place_ref, bf16[512,512]{1,0:T(8,128)(2,1)} %bitcast.35, bf16[512,512]{1,0:T(8,128)(2,1)} %get-tuple-element.8.mixed_ref, bf16[512,512]{1,0:T(8,128)(2,1)} %query_ref.1, f32[1,512]{1,0:T(1,128)} %bitcast.39, bf16[512,4096]{1,0:T(8,128)(2,1)} %weight_ref.1), custom_call_target="tpu_custom_call" | custom-call | flops 2147483648 | bytes 10485760 | tf_op jit(solution)/shard_map/project/pallas_call | solution.py:193
  72.3 1.9 %slice.69 = bf16[4,512,512]{2,1,0:T(8,128)(2,1)S(1)} slice(bf16[8,512,512]{2,1,0:T(8,128)(2,1)} %project.1), slice={[0:4], [0:512], [0:512]} | slice | bytes 4194304 | tf_op jit(solution)/shard_map/slice | solution.py:248
  74.2 4.1 %collective-permute-done = bf16[4,512,512]{2,1,0:T(8,128)(2,1)S(1)} collective-permute-done((bf16[4,512,512]{2,1,0:T(8,128)(2,1)S(1)}, bf16[4,512,512]{2,1,0:T(8,128)(2,1)S(1)}, u32[]{:S(2)}, u32[]{:S(2)}) %collective-permute-start) | collective-permute-done | bytes 2097184 | tf_op jit(solution)/shard_map/ppermute | solution.py:246
  78.7 1.7 %collective-permute-start.2 = (bf16[256,512]{1,0:T(8,128)(2,1)S(1)}, bf16[256,512]{1,0:T(8,128)(2,1)S(1)}, u32[]{:S(2)}, u32[]{:S(2)}) collective-permute-start(bf16[256,512]{1,0:T(8,128)(2,1)S(1)} %get-tuple-element.16), channel_id=1, source_target_pairs={{0,2},{1,3},{2,4},{3,5},{4,6},{5,7},{6,0},{7,1},{8,10},{9,11},{10,... | collective-permute-start | bytes 786440 | tf_op jit(solution)/shard_map/ppermute | solution.py:246
  80.3 1.7 %collective-permute-start.1 = (bf16[256,512]{1,0:T(8,128)(2,1)S(1)}, bf16[256,512]{1,0:T(8,128)(2,1)S(1)}, u32[]{:S(2)}, u32[]{:S(2)}) collective-permute-start(bf16[256,512]{1,0:T(8,128)(2,1)S(1)} %get-tuple-element.13), channel_id=1, source_target_pairs={{0,6},{1,7},{2,0},{3,1},{4,2},{5,3},{6,4},{7,5},{8,14},{9,15},{10,... | collective-permute-start | bytes 786440 | tf_op jit(solution)/shard_map/ppermute | solution.py:246
  82.0 1.8 %collective-permute-start.5 = (bf16[256,512]{1,0:T(8,128)(2,1)S(1)}, bf16[256,512]{1,0:T(8,128)(2,1)S(1)}, u32[]{:S(2)}, u32[]{:S(2)}) collective-permute-start(bf16[256,512]{1,0:T(8,128)(2,1)S(1)} %get-tuple-element.14), channel_id=1, source_target_pairs={{0,6},{1,7},{2,0},{3,1},{4,2},{5,3},{6,4},{7,5},{8,14},{9,15},{10,... | collective-permute-start | bytes 786440 | tf_op jit(solution)/shard_map/ppermute | solution.py:246
  83.8 4.6 %collective-permute-done.2 = bf16[256,512]{1,0:T(8,128)(2,1)S(1)} collective-permute-done((bf16[256,512]{1,0:T(8,128)(2,1)S(1)}, bf16[256,512]{1,0:T(8,128)(2,1)S(1)}, u32[]{:S(2)}, u32[]{:S(2)}) %collective-permute-start.2) | collective-permute-done | bytes 262176 | tf_op jit(solution)/shard_map/ppermute | solution.py:246
  88.9 1.6 %collective-permute-start.4 = (bf16[256,512]{1,0:T(8,128)(2,1)S(1)}, bf16[256,512]{1,0:T(8,128)(2,1)S(1)}, u32[]{:S(2)}, u32[]{:S(2)}) collective-permute-start(bf16[256,512]{1,0:T(8,128)(2,1)S(1)} %get-tuple-element.15), channel_id=1, source_target_pairs={{0,2},{1,3},{2,4},{3,5},{4,6},{5,7},{6,0},{7,1},{8,10},{9,11},{10,... | collective-permute-start | bytes 786440 | tf_op jit(solution)/shard_map/ppermute | solution.py:246
  90.5 3.6 %collective-permute-done.5 = bf16[256,512]{1,0:T(8,128)(2,1)S(1)} collective-permute-done((bf16[256,512]{1,0:T(8,128)(2,1)S(1)}, bf16[256,512]{1,0:T(8,128)(2,1)S(1)}, u32[]{:S(2)}, u32[]{:S(2)}) %collective-permute-start.5) | collective-permute-done | bytes 262176 | tf_op jit(solution)/shard_map/ppermute | solution.py:246
  94.0 4.9 %collective-permute-done.3 = bf16[256,512]{1,0:T(8,128)(2,1)S(1)} collective-permute-done((bf16[256,512]{1,0:T(8,128)(2,1)S(1)}, bf16[256,512]{1,0:T(8,128)(2,1)S(1)}, u32[]{:S(2)}, u32[]{:S(2)}) %collective-permute-start.3) | collective-permute-done | bytes 262176 | tf_op jit(solution)/shard_map/ppermute | solution.py:246
  99.2 0.6 collective-permute-start.6
  99.8 3.1 %collective-permute-done.4 = bf16[256,512]{1,0:T(8,128)(2,1)S(1)} collective-permute-done((bf16[256,512]{1,0:T(8,128)(2,1)S(1)}, bf16[256,512]{1,0:T(8,128)(2,1)S(1)}, u32[]{:S(2)}, u32[]{:S(2)}) %collective-permute-start.4) | collective-permute-done | bytes 262176 | tf_op jit(solution)/shard_map/ppermute | solution.py:246
  103.0 2.7 %collective-permute-done.6 = bf16[256,512]{1,0:T(8,128)(2,1)S(1)} collective-permute-done((bf16[256,512]{1,0:T(8,128)(2,1)S(1)}, bf16[256,512]{1,0:T(8,128)(2,1)S(1)}, u32[]{:S(2)}, u32[]{:S(2)}) %collective-permute-start.6) | collective-permute-done | bytes 262176 | tf_op jit(solution)/shard_map/ppermute | solution.py:246
  105.8 0.8 pad_maximum_fusion
  (16 shorter events, 1.9 us)
Async XLA Ops:
  3.5 28.8 %all-to-all-start = ((bf16[32,16,512]{2,1,0:T(8,128)(2,1)}), bf16[32,16,512]{2,1,0:T(8,128)(2,1)S(1)}, u32[]{:S(2)}, u32[]{:S(2)}) async-start(bf16[32,16,512]{2,1,0:T(8,128)(2,1)} %bitcast.38), calls=%async_computation | async-start | bytes 1048576 | tf_op jit(solution)/shard_map/all_to_all | solution.py:236
  20.1 25.0 %copy-start.3 = (s32[4]{0:T(128)S(1)}, s32[4]{0:T(128)}, u32[]{:S(2)}) copy-start(s32[4]{0:T(128)} %constant.72.clone) | copy-start | bytes 52
  32.3 0.8 copy-start.2
  40.2 21.8 %all-to-all-start.1 = ((bf16[32,16,512]{2,1,0:T(8,128)(2,1)}), bf16[32,16,512]{2,1,0:T(8,128)(2,1)S(1)}, u32[]{:S(2)}, u32[]{:S(2)}) async-start(bf16[32,16,512]{2,1,0:T(8,128)(2,1)} %bitcast.36), calls=%async_computation.1 | async-start | bytes 1048576 | tf_op jit(solution)/shard_map/all_to_all | solution.py:238
  62.0 0.8 copy-start.1
  72.3 6.1 %copy-start = (bf16[8,512,512]{2,1,0:T(8,128)(2,1)S(1)}, bf16[8,512,512]{2,1,0:T(8,128)(2,1)}, u32[]{:S(2)}) copy-start(bf16[8,512,512]{2,1,0:T(8,128)(2,1)} %project.1) | copy-start | bytes 12582916
  74.1 4.2 %collective-permute-start = (bf16[4,512,512]{2,1,0:T(8,128)(2,1)S(1)}, bf16[4,512,512]{2,1,0:T(8,128)(2,1)S(1)}, u32[]{:S(2)}, u32[]{:S(2)}) collective-permute-start(bf16[4,512,512]{2,1,0:T(8,128)(2,1)S(1)} %slice.69), channel_id=1, source_target_pairs={{0,1},{1,0},{2,3},{3,2},{4,5},{5,4},{6,7},{7,6},{8,9},{9,8},{10,11... | collective-permute-start | bytes 6291464 | tf_op jit(solution)/shard_map/ppermute | solution.py:246
  78.7 9.7 %collective-permute-start.2 = (bf16[256,512]{1,0:T(8,128)(2,1)S(1)}, bf16[256,512]{1,0:T(8,128)(2,1)S(1)}, u32[]{:S(2)}, u32[]{:S(2)}) collective-permute-start(bf16[256,512]{1,0:T(8,128)(2,1)S(1)} %get-tuple-element.16), channel_id=1, source_target_pairs={{0,2},{1,3},{2,4},{3,5},{4,6},{5,7},{6,0},{7,1},{8,10},{9,11},{10,... | collective-permute-start | bytes 786440 | tf_op jit(solution)/shard_map/ppermute | solution.py:246
  80.3 10.1 %collective-permute-start.1 = (bf16[256,512]{1,0:T(8,128)(2,1)S(1)}, bf16[256,512]{1,0:T(8,128)(2,1)S(1)}, u32[]{:S(2)}, u32[]{:S(2)}) collective-permute-start(bf16[256,512]{1,0:T(8,128)(2,1)S(1)} %get-tuple-element.13), channel_id=1, source_target_pairs={{0,6},{1,7},{2,0},{3,1},{4,2},{5,3},{6,4},{7,5},{8,14},{9,15},{10,... | collective-permute-start | bytes 786440 | tf_op jit(solution)/shard_map/ppermute | solution.py:246
  82.0 12.0 %collective-permute-start.5 = (bf16[256,512]{1,0:T(8,128)(2,1)S(1)}, bf16[256,512]{1,0:T(8,128)(2,1)S(1)}, u32[]{:S(2)}, u32[]{:S(2)}) collective-permute-start(bf16[256,512]{1,0:T(8,128)(2,1)S(1)} %get-tuple-element.14), channel_id=1, source_target_pairs={{0,6},{1,7},{2,0},{3,1},{4,2},{5,3},{6,4},{7,5},{8,14},{9,15},{10,... | collective-permute-start | bytes 786440 | tf_op jit(solution)/shard_map/ppermute | solution.py:246
  88.5 10.5 %collective-permute-start.3 = (bf16[256,512]{1,0:T(8,128)(2,1)S(1)}, bf16[256,512]{1,0:T(8,128)(2,1)S(1)}, u32[]{:S(2)}, u32[]{:S(2)}) collective-permute-start(bf16[256,512]{1,0:T(8,128)(2,1)S(1)} %fusion.3), channel_id=1, source_target_pairs={{0,2},{1,3},{2,4},{3,5},{4,6},{5,7},{6,0},{7,1},{8,10},{9,11},{10,... | collective-permute-start | bytes 786440 | tf_op jit(solution)/shard_map/ppermute | solution.py:246
  88.9 14.1 %collective-permute-start.4 = (bf16[256,512]{1,0:T(8,128)(2,1)S(1)}, bf16[256,512]{1,0:T(8,128)(2,1)S(1)}, u32[]{:S(2)}, u32[]{:S(2)}) collective-permute-start(bf16[256,512]{1,0:T(8,128)(2,1)S(1)} %get-tuple-element.15), channel_id=1, source_target_pairs={{0,2},{1,3},{2,4},{3,5},{4,6},{5,7},{6,0},{7,1},{8,10},{9,11},{10,... | collective-permute-start | bytes 786440 | tf_op jit(solution)/shard_map/ppermute | solution.py:246
  99.2 6.4 %collective-permute-start.6 = (bf16[256,512]{1,0:T(8,128)(2,1)S(1)}, bf16[256,512]{1,0:T(8,128)(2,1)S(1)}, u32[]{:S(2)}, u32[]{:S(2)}) collective-permute-start(bf16[256,512]{1,0:T(8,128)(2,1)S(1)} %get-tuple-element.12), channel_id=1, source_target_pairs={{0,6},{1,7},{2,0},{3,1},{4,2},{5,3},{6,4},{7,5},{8,14},{9,15},{10,... | collective-permute-start | bytes 786440 | tf_op jit(solution)/shard_map/ppermute | solution.py:246

commit v2 on v1

--- a/solution.py
+++ b/solution.py
@@ -11,6 +11,7 @@
 WIN = 8
 LANES = 128
 CORES = 2
+PARAMS = pltpu.CompilerParams(vmem_limit_bytes=20 << 20)
 
 
 def odd_tables(length):
@@ -173,51 +174,129 @@
         cost_estimate=pl.CostEstimate(
             flops=4 * count * length * tiles * pair, bytes_accessed=3 << 20, transcendentals=0
         ),
+        compiler_params=PARAMS,
         name="convolve",
     )(turned, spectrum, table)
 
 
-def project_kernel(place_ref, conv_ref, mixed_ref, query_ref, skip_ref, weight_ref, out_ref, gated):
-    @pl.when(pl.program_id(0) == 0)
-    def _():
-        conv = conv_ref[...].T.astype(jnp.float32)
-        combined = conv + skip_ref[...] * mixed_ref[...].astype(jnp.float32)
-        gated[...] = (query_ref[...].astype(jnp.float32) * combined).astype(jnp.bfloat16)
-
-    out_ref[0] = jnp.dot(gated[...], weight_ref[...], preferred_element_type=jnp.float32).astype(jnp.bfloat16)
-
-
-def project(blocks, conv_turned, mixed, query_gate, skip_gain, out_weight):
+def gate_kernel(conv_ref, mixed_ref, query_ref, skip_ref, gated_ref):
+    conv = conv_ref[...].T.astype(jnp.float32)
+    combined = conv + skip_ref[...] * mixed_ref[...].astype(jnp.float32)
+    gated_ref[...] = (query_ref[...].astype(jnp.float32) * combined).astype(jnp.bfloat16)
+
+
+def gate(conv_turned, mixed, query_gate, skip_gain):
     length, width = mixed.shape
-    number = blocks.shape[0]
-    return pl.pallas_call(
-        project_kernel,
+    return pl.pallas_call(
+        gate_kernel,
+        out_shape=jax.ShapeDtypeStruct((length, width), jnp.bfloat16),
+        compiler_params=PARAMS,
+        cost_estimate=pl.CostEstimate(flops=4 * length * width, bytes_accessed=8 * length * width, transcendentals=0),
+        name="gate",
+    )(conv_turned, mixed, query_gate, skip_gain.reshape(1, width))
+
+
+def weights_kernel(number, blocks_ref, weight_ref, own_ref, partner_ref, sems):
+    width = weight_ref.shape[0]
+    copies = []
+    for k in range(number):
+        for at, ref in enumerate((partner_ref, own_ref)):
+            start = pl.multiple_of(blocks_ref[number * at + k] * width, width)
+            copies.append(
+                pltpu.make_async_copy(weight_ref.at[:, pl.ds(start, width)], ref.at[k], sems.at[number * at + k])
+            )
+    for copy in copies:
+        copy.start()
+    for copy in copies:
+        copy.wait()
+
+
+def weight_blocks(blocks, out_weight):
+    width = out_weight.shape[0]
+    number = blocks.shape[0] // 2
+    shape = jax.ShapeDtypeStruct((number, width, width), jnp.bfloat16)
+    return pl.pallas_call(
+        functools.partial(weights_kernel, number),
         grid_spec=pltpu.PrefetchScalarGridSpec(
             num_scalar_prefetch=1,
-            grid=(number,),
-            in_specs=[
-                pl.BlockSpec((width, length), lambda i, blocks: (0, 0)),
-                pl.BlockSpec((length, width), lambda i, blocks: (0, 0)),
-                pl.BlockSpec((length, width), lambda i, blocks: (0, 0)),
-                pl.BlockSpec((1, width), lambda i, blocks: (0, 0)),
-                pl.BlockSpec((width, width), lambda i, blocks: (0, blocks[i])),
-            ],
-            out_specs=pl.BlockSpec((1, length, width), lambda i, blocks: (i, 0, 0)),
-            scratch_shapes=[pltpu.VMEM((length, width), jnp.bfloat16)],
-        ),
-        out_shape=jax.ShapeDtypeStruct((number, length, width), jnp.bfloat16),
+            in_specs=[pl.BlockSpec(memory_space=pl.ANY)],
+            out_specs=[pl.BlockSpec(memory_space=pltpu.VMEM)] * 2,
+            scratch_shapes=[pltpu.SemaphoreType.DMA((2 * number,))],
+        ),
+        out_shape=[shape] * 2,
+        compiler_params=pltpu.CompilerParams(vmem_limit_bytes=48 << 20),
+        cost_estimate=pl.CostEstimate(flops=0, bytes_accessed=8 << 20, transcendentals=0),
+        name="weight_blocks",
+    )(blocks, out_weight)
+
+
+def own_part_kernel(number, gated_ref, weight_ref, out_ref):
+    for k in range(number):
+        out_ref[k] = jnp.dot(gated_ref[...], weight_ref[k], preferred_element_type=jnp.float32)
+
+
+def own_part(gated, own_weight):
+    length, width = gated.shape
+    number = own_weight.shape[0]
+    return pl.pallas_call(
+        functools.partial(own_part_kernel, number),
+        in_specs=[pl.BlockSpec(memory_space=pltpu.VMEM)] * 2,
+        out_specs=pl.BlockSpec(memory_space=pltpu.VMEM),
+        out_shape=jax.ShapeDtypeStruct((number, length, width), jnp.float32),
+        compiler_params=PARAMS,
         cost_estimate=pl.CostEstimate(
-            flops=2 * length * width * width * number, bytes_accessed=10 << 20, transcendentals=0
+            flops=2 * length * width * width * number, bytes_accessed=2 << 20, transcendentals=0
+        ),
+        name="own_part",
+    )(gated, own_weight)
+
+
+def project_kernel(which, part_ref, other_ref, weight_ref, *outs):
+    half = other_ref.shape[0] // 2
+    for at, k in enumerate(which):
+        total = part_ref[k] + jnp.dot(other_ref[...], weight_ref[k], preferred_element_type=jnp.float32)
+        total = total.astype(jnp.bfloat16)
+        outs[2 * at][...] = total[:half]
+        outs[2 * at + 1][...] = total[half:]
+
+
+def project(which, part, other, other_weight):
+    _, length, width = part.shape
+    number = len(which)
+    return pl.pallas_call(
+        functools.partial(project_kernel, which),
+        in_specs=[pl.BlockSpec(memory_space=pltpu.VMEM)] * 3,
+        out_specs=[pl.BlockSpec(memory_space=pltpu.VMEM)] * (2 * number),
+        out_shape=[jax.ShapeDtypeStruct((length // 2, width), jnp.bfloat16)] * (2 * number),
+        compiler_params=PARAMS,
+        cost_estimate=pl.CostEstimate(
+            flops=2 * length * width * width * number, bytes_accessed=number << 20, transcendentals=0
         ),
         name="project",
-    )(blocks, conv_turned, mixed, query_gate, skip_gain.reshape(1, width), out_weight)
-
-
-def added(*terms):
-    total = terms[0].astype(jnp.float32)
-    for term in terms[1:]:
-        total = total + term.astype(jnp.float32)
-    return total.astype(jnp.bfloat16)
+    )(part, other, other_weight)
+
+
+def finish_kernel(*refs):
+    out_ref = refs[-1]
+    half = out_ref.shape[0] // 2
+    for at in range(2):
+        total = sum(ref[...].astype(jnp.float32) for ref in refs[3 * at : 3 * at + 3])
+        out_ref[at * half : (at + 1) * half, :] = total.astype(jnp.bfloat16)
+
+
+def finish(low, high):
+    half, width = low[0].shape
+    return pl.pallas_call(
+        finish_kernel,
+        out_shape=jax.ShapeDtypeStruct((2 * half, width), jnp.bfloat16),
+        compiler_params=PARAMS,
+        cost_estimate=pl.CostEstimate(flops=6 * half * width, bytes_accessed=16 * half * width, transcendentals=0),
+        name="finish",
+    )(*low, *high)
+
+
+def added(one, two):
+    return (one.astype(jnp.float32) + two.astype(jnp.float32)).astype(jnp.bfloat16)
 
 
 def body(query_gate, key_gate, value_in, filter_taps, skip_gain, out_weight):
@@ -230,34 +309,34 @@
     per_tile = LANES // few
     table = jnp.asarray(odd_tables(length))
 
+    def ch_shift(block, dy, dcore):
+        route = [(i, ((i // CORES + dy) % ring) * CORES + (i % CORES + dcore) % CORES) for i in range(groups)]
+        return lax.ppermute(block, "ch", route)
+
     mixed, turned = mix(key_gate, value_in)
     place = jnp.stack([here // per_tile, here % per_tile]).astype(jnp.int32)
     spectrum = taps_spectrum(place, filter_taps, table, few)
+    ahead = [(y + step) % ring for step in (2, 1, 3, 0)]
+    blocks = jnp.stack([k * CORES + at for at in (1 - core, core) for k in ahead]).astype(jnp.int32)
+    own_weight, partner_weight = weight_blocks(blocks, out_weight)
+    other_weight = ch_shift(partner_weight, 0, 1)
+
     long_rows = lax.all_to_all(turned.reshape(ctx, few, length), "ctx", 0, 0)
     conv_rows = convolve(long_rows.reshape(ctx * few, length), spectrum, table, few)
     conv_turned = lax.all_to_all(conv_rows.reshape(ctx, few, length), "ctx", 0, 0).reshape(width, length)
 
-    ahead = (y + jnp.array([2, 1, 3, 0], jnp.int32)) % ring
-    blocks = jnp.concatenate([ahead * CORES + (1 - core), ahead * CORES + core]).astype(jnp.int32)
-    parts = project(blocks, conv_turned, mixed, query_gate, skip_gain, out_weight)
-
-    def ch_shift(block, dy, dcore):
-        route = [(i, ((i // CORES + dy) % ring) * CORES + (i % CORES + dcore) % CORES) for i in range(groups)]
-        return lax.ppermute(block, "ch", route)
-
-    partner = ch_shift(parts[:ring], 0, 1)
-    half = length // 2
-    across_low = added(parts[ring, :half], partner[0, :half])
-    across_high = added(parts[ring, half:], partner[0, half:])
-    got_across_low = ch_shift(across_low, 1, 0)
-    got_across_high = ch_shift(across_high, -1, 0)
-    up_high = ch_shift(added(parts[ring + 1, half:], partner[1, half:]), 1, 0)
-    down_low = ch_shift(added(parts[ring + 2, :half], partner[2, :half]), -1, 0)
-    up_low = ch_shift(added(parts[ring + 1, :half], partner[1, :half], got_across_low), 1, 0)
-    down_high = ch_shift(added(parts[ring + 2, half:], partner[2, half:], got_across_high), -1, 0)
-    low = added(parts[ring + 3, :half], partner[3, :half], down_low, up_low)
-    high = added(parts[ring + 3, half:], partner[3, half:], up_high, down_high)
-    return jnp.concatenate([low, high], axis=0)
+    gated = gate(conv_turned, mixed, query_gate, skip_gain)
+    other = ch_shift(gated, 0, 1)
+    part = own_part(gated, own_weight)
+    across_low, across_high = project((0,), part, other, other_weight)
+    got_low = ch_shift(across_low, 1, 0)
+    got_high = ch_shift(across_high, -1, 0)
+    up_low, up_high, down_low, down_high, own_low, own_high = project((1, 2, 3), part, other, other_weight)
+    from_below_high = ch_shift(up_high, 1, 0)
+    from_above_low = ch_shift(down_low, -1, 0)
+    from_below_low = ch_shift(added(up_low, got_low), 1, 0)
+    from_above_high = ch_shift(added(down_high, got_high), -1, 0)
+    return finish((own_low, from_above_low, from_below_low), (own_high, from_below_high, from_above_high))
 
 
 def solution(mesh):

time: 107 us -> 88.9 us (0.83)
  waiting for transfers between devices: 51.6 us -> 19.3 us
  blocking collectives: 0 us -> 21.6 us
  Pallas kernels: 24.8 us -> 22.5 us
  starting transfers between devices: 23.8 us -> 21.6 us
  other arithmetic: 2.8 us -> 0.75 us
    all_to_all x0 -> x1, blocking collectives: none -> 21.6 us  [body(): lax.all_to_all(conv_rows.reshape(ctx, few, length), 'ctx', 0, 0)]
    all_to_all x1 -> x0, waiting for transfers between devices: 16.3 us -> none  [body(): lax.all_to_all(conv_rows.reshape(ctx, few, length), 'ctx', 0, 0)]
    ppermute x7 -> x8, waiting for transfers between devices: 23.1 us -> 12.8 us  [ch_shift(): return lax.ppermute(block, 'ch', route)]
    all_to_all x1, waiting for transfers between devices: 12.2 us -> 6.49 us  [body(): long_rows = lax.all_to_all(turned.reshape(ctx, few, length), 'ctx', 0, 0)]
    all_to_all x1 -> x0, starting transfers between devices: 4.86 us -> none  [body(): lax.all_to_all(conv_rows.reshape(ctx, few, length), 'ctx', 0, 0)]
    ppermute x7 -> x8, starting transfers between devices: 7.77 us -> 10.4 us  [ch_shift(): return lax.ppermute(block, 'ch', route)]
    slice x1 -> x0, local copies, waits for them, and re-layouts: 1.88 us -> none  [body(): partner = ch_shift(parts[:ring], 0, 1)]
    pallas_call x1 -> x6, Pallas kernels: 9.48 us -> 8.04 us  [the longest x1 4.13 us: weight_blocks(): pl.pallas_call(functools.partial(weights_kernel, number), grid_spec=pltpu...]
  transfers between devices with their start and end apart: 9 -> 9, of which waited for: 8 -> 7; matrix products, arithmetic and copies ran while one was open for 1% -> 1% of each run, Pallas kernels for 4% -> 20%
where the time goes in v2:
time: 88.9 us; the launch traced here: 88.5 us
  Pallas kernels  22.5 us (25%)
  starting transfers between devices  21.6 us (24%)
  blocking collectives  21.6 us (24%)
  waiting for transfers between devices  19.3 us (22%)
  local copies, waits for them, and re-layouts  2.59 us (3%)
    all_to_all x1, blocking collectives, body(): lax.all_to_all(conv_rows.reshape(ctx, few, length), 'ctx', 0, 0)  21.6 us
    ppermute x8, waiting for transfers between devices, ch_shift(): return lax.ppermute(block, 'ch', route)  12.8 us
    all_to_all x1, starting transfers between devices, body(): long_rows = lax.all_to_all(turned.reshape(ctx, few, length), 'ctx', 0, 0)  11.2 us
    ppermute x8, starting transfers between devices, ch_shift(): return lax.ppermute(block, 'ch', route)  10.4 us
    all_to_all x1, waiting for transfers between devices, body(): long_rows = lax.all_to_all(turned.reshape(ctx, few, length), 'ctx', 0, 0)  6.49 us
    pallas_call x1, Pallas kernels, convolve(): pl.pallas_call(functools.partial(conv_kernel, few), grid=(tiles,), in_spe...  6.05 us
    pallas_call x1, Pallas kernels, taps_spectrum(): pl.pallas_call(functools.partial(taps_kernel, few), grid_spec=pltpu.Prefe...  4.93 us
    pallas_call x1, Pallas kernels, weight_blocks(): pl.pallas_call(functools.partial(weights_kernel, number), grid_spec=pltpu...  4.13 us
  transfers between devices with their start and end apart: 9, of which 7 were waited for; matrix products, arithmetic and copies ran while one was open for 1% of the time, Pallas kernels for 20%

profile of v2, /device:TPU:32, one launch (start us, length us, event | category | flops | bytes accessed | tf_op | source)
XLA Modules:
  0.0 88.5 jit_solution(928192807526456666)
XLA Ops:
  0.0 3.5 %mix.1 = (bf16[512,512]{1,0:T(8,128)(2,1)}, bf16[512,512]{1,0:T(8,128)(2,1)}) custom-call(bf16[512,512]{1,0:T(8,128)(2,1)} %key_ref.1, bf16[512,512]{1,0:T(8,128)(2,1)} %value_ref.1), custom_call_target="tpu_custom_call" | custom-call | flops 262144 | bytes 2097152 | tf_op jit(solution)/shard_map/mix/pallas_call | solution.py:36
  3.5 11.2 %all-to-all-start = ((bf16[32,16,512]{2,1,0:T(8,128)(2,1)}), bf16[32,16,512]{2,1,0:T(8,128)(2,1)}, u32[]{:S(2)}, u32[]{:S(2)}) async-start(bf16[32,16,512]{2,1,0:T(8,128)(2,1)} %bitcast.18), calls=%async_computation | async-start | bytes 1048576 | tf_op jit(solution)/shard_map/all_to_all | solution.py:324
  14.9 4.1 %weight_blocks.1 = (bf16[4,512,512]{2,1,0:T(8,128)(2,1)S(1)}, bf16[4,512,512]{2,1,0:T(8,128)(2,1)}) custom-call(s32[8]{0:T(128)S(1)} %stack.47.blocks_ref, bf16[512,4096]{1,0:T(8,128)(2,1)} %weight_ref.1), custom_call_target="tpu_custom_call" | custom-call | bytes 8388608 | tf_op jit(solution)/shard_map/weight_blocks/pallas_call | solution.py:218
  19.0 1.3 %copy-done = bf16[4,512,512]{2,1,0:T(8,128)(2,1)} copy-done((bf16[4,512,512]{2,1,0:T(8,128)(2,1)}, bf16[4,512,512]{2,1,0:T(8,128)(2,1)S(1)}, u32[]{:S(2)}) %copy-start) | copy-done | bytes 2097176
  20.3 0.6 pad_add_fusion.place_ref
  21.0 4.9 %taps_spectrum.1.h_ref = f32[4,128,256]{2,1,0:T(8,128)} custom-call(s32[2]{0:T(128)} %pad_add_fusion.place_ref, f32[4096,512]{1,0:T(8,128)} %taps_ref.1, bf16[4,512,256]{2,1,0:T(8,128)(2,1)} %constant.77.clone.table_ref), custom_call_target="tpu_custom_call" | custom-call | flops 134217728 | bytes 3145728 | tf_op jit(solution)/shard_map/taps_spectrum/pallas_call | solution.py:76
  25.9 6.5 %all-to-all-done = bf16[32,16,512]{2,1,0:T(8,128)(2,1)} async-done(((bf16[32,16,512]{2,1,0:T(8,128)(2,1)}), bf16[32,16,512]{2,1,0:T(8,128)(2,1)}, u32[]{:S(2)}, u32[]{:S(2)}) %all-to-all-start) | async-done | bytes 524320 | tf_op jit(solution)/shard_map/all_to_all | solution.py:324
  32.4 1.2 %copy-done.5 = f32[4,128,256]{2,1,0:T(8,128)S(1)} copy-done((f32[4,128,256]{2,1,0:T(8,128)S(1)}, f32[4,128,256]{2,1,0:T(8,128)}, u32[]{:S(2)}) %copy-start.5) | copy-done | bytes 524312
  33.6 6.1 %convolve.1 = bf16[512,512]{1,0:T(8,128)(2,1)S(1)} custom-call(bf16[512,512]{1,0:T(8,128)(2,1)} %bitcast.1.x_ref, f32[4,128,256]{2,1,0:T(8,128)S(1)} %copy-done.5, bf16[4,512,256]{2,1,0:T(8,128)(2,1)S(1)} %copy-done.2), custom_call_target="tpu_custom_call" | custom-call | flops 1073741824 | bytes 3145728 | tf_op jit(solution)/shard_map/convolve/pallas_call | solution.py:158
  39.7 21.6 %all_to_all.10 = bf16[32,16,512]{2,1,0:T(8,128)(2,1)S(1)} all-to-all(bf16[32,16,512]{2,1,0:T(8,128)(2,1)S(1)} %bitcast.16), channel_id=1, replica_groups=mesh['ctx'=32,'ch'=8] {'ctx'}, dimensions={0} | all-to-all | bytes 1048576 | tf_op jit(solution)/shard_map/all_to_all | solution.py:326
  61.3 0.3 gate.1.gated_ref
  61.6 1.3 %own_part.1.part_ref = f32[4,512,512]{2,1,0:T(8,128)S(1)} custom-call(bf16[512,512]{1,0:T(8,128)(2,1)S(1)} %gate.1.gated_ref, bf16[4,512,512]{2,1,0:T(8,128)(2,1)S(1)} %copy-done.1), custom_call_target="tpu_custom_call" | custom-call | flops 1073741824 | bytes 2097152 | tf_op jit(solution)/shard_map/own_part/pallas_call | solution.py:241
  62.9 0.6 collective-permute-done.other_ref
  63.5 0.4 project.3
  64.0 3.1 %collective-permute-start.6 = (bf16[256,512]{1,0:T(8,128)(2,1)S(1)}, bf16[256,512]{1,0:T(8,128)(2,1)S(1)}, u32[]{:S(2)}, u32[]{:S(2)}) collective-permute-start(bf16[256,512]{1,0:T(8,128)(2,1)S(1)} %get-tuple-element.28), channel_id=1, source_target_pairs={{0,6},{1,7},{2,0},{3,1},{4,2},{5,3},{6,4},{7,5},{8,14},{9,15},{10,... | collective-permute-start | bytes 786440 | tf_op jit(solution)/shard_map/ppermute | solution.py:314
  67.1 1.0 %project.2 = (bf16[256,512]{1,0:T(8,128)(2,1)S(1)}, bf16[256,512]{1,0:T(8,128)(2,1)S(1)}, bf16[256,512]{1,0:T(8,128)(2,1)S(1)}, bf16[256,512]{1,0:T(8,128)(2,1)S...) custom-call(f32[4,512,512]{2,1,0:T(8,128)S(1)} %own_part.1.part_ref, ...), custom_call_target="tpu_custom_call" | custom-call | flops 805306368 | bytes 3145728 | tf_op jit(solution)/shard_map/project/pallas_call | solution.py:266
  68.0 3.3 %collective-permute-start.2 = (bf16[256,512]{1,0:T(8,128)(2,1)S(1)}, bf16[256,512]{1,0:T(8,128)(2,1)S(1)}, u32[]{:S(2)}, u32[]{:S(2)}) collective-permute-start(bf16[256,512]{1,0:T(8,128)(2,1)S(1)} %get-tuple-element.22), channel_id=1, source_target_pairs={{0,6},{1,7},{2,0},{3,1},{4,2},{5,3},{6,4},{7,5},{8,14},{9,15},{10,... | collective-permute-start | bytes 786440 | tf_op jit(solution)/shard_map/ppermute | solution.py:314
  71.4 2.4 %collective-permute-done.6 = bf16[256,512]{1,0:T(8,128)(2,1)S(1)} collective-permute-done((bf16[256,512]{1,0:T(8,128)(2,1)S(1)}, bf16[256,512]{1,0:T(8,128)(2,1)S(1)}, u32[]{:S(2)}, u32[]{:S(2)}) %collective-permute-start.6) | collective-permute-done | bytes 262176 | tf_op jit(solution)/shard_map/ppermute | solution.py:314
  73.8 3.8 %collective-permute-start.7 = (bf16[256,512]{1,0:T(8,128)(2,1)S(1)}, bf16[256,512]{1,0:T(8,128)(2,1)S(1)}, u32[]{:S(2)}, u32[]{:S(2)}) collective-permute-start(bf16[256,512]{1,0:T(8,128)(2,1)S(1)} %add_convert_fusion), channel_id=1, source_target_pairs={{0,6},{1,7},{2,0},{3,1},{4,2},{5,3},{6,4},{7,5},{8,14},{9,15},{10,... | collective-permute-start | bytes 786440 | tf_op jit(solution)/shard_map/ppermute | solution.py:314
  77.8 1.6 %collective-permute-done.2.refs_1_ = bf16[256,512]{1,0:T(8,128)(2,1)S(1)} collective-permute-done((bf16[256,512]{1,0:T(8,128)(2,1)S(1)}, bf16[256,512]{1,0:T(8,128)(2,1)S(1)}, u32[]{:S(2)}, u32[]{:S(2)}) %collective-permute-start.2) | collective-permute-done | bytes 262176 | tf_op jit(solution)/shard_map/ppermute | solution.py:314
  79.4 3.7 %collective-permute-done.5.refs_4_ = bf16[256,512]{1,0:T(8,128)(2,1)S(1)} collective-permute-done((bf16[256,512]{1,0:T(8,128)(2,1)S(1)}, bf16[256,512]{1,0:T(8,128)(2,1)S(1)}, u32[]{:S(2)}, u32[]{:S(2)}) %collective-permute-start.5) | collective-permute-done | bytes 262176 | tf_op jit(solution)/shard_map/ppermute | solution.py:314
  83.1 1.1 %collective-permute-done.7.refs_5_ = bf16[256,512]{1,0:T(8,128)(2,1)S(1)} collective-permute-done((bf16[256,512]{1,0:T(8,128)(2,1)S(1)}, bf16[256,512]{1,0:T(8,128)(2,1)S(1)}, u32[]{:S(2)}, u32[]{:S(2)}) %collective-permute-start.7) | collective-permute-done | bytes 262176 | tf_op jit(solution)/shard_map/ppermute | solution.py:314
  84.2 3.4 %collective-permute-done.4.refs_2_ = bf16[256,512]{1,0:T(8,128)(2,1)S(1)} collective-permute-done((bf16[256,512]{1,0:T(8,128)(2,1)S(1)}, bf16[256,512]{1,0:T(8,128)(2,1)S(1)}, u32[]{:S(2)}, u32[]{:S(2)}) %collective-permute-start.4) | collective-permute-done | bytes 262176 | tf_op jit(solution)/shard_map/ppermute | solution.py:314
  87.6 1.0 %finish.1 = bf16[512,512]{1,0:T(8,128)(2,1)} custom-call(bf16[256,512]{1,0:T(8,128)(2,1)S(1)} %get-tuple-element.21.refs_0_, bf16[256,512]{1,0:T(8,128)(2,1)S(1)} %collective-permute-done.2.refs_1_, bf16[256,512]{1,0:T(8,128)(2,1)S(1)} %collective-permute-done.4.refs_2_, bf16[256,512]{1,0:T(8,128)(2,1)S(1)} %get-tuple-element.25.refs_3_, ...), custom_call_target="tpu_custom_call" | custom-call | flops 786432 | bytes 2097152 | tf_op jit(solution)/shard_map/finish/pallas_call | solution.py:289
  (22 shorter events, 0.4 us)
Async XLA Ops:
  3.5 28.9 %all-to-all-start = ((bf16[32,16,512]{2,1,0:T(8,128)(2,1)}), bf16[32,16,512]{2,1,0:T(8,128)(2,1)}, u32[]{:S(2)}, u32[]{:S(2)}) async-start(bf16[32,16,512]{2,1,0:T(8,128)(2,1)} %bitcast.18), calls=%async_computation | async-start | bytes 1048576 | tf_op jit(solution)/shard_map/all_to_all | solution.py:324
  19.0 1.3 %copy-start = (bf16[4,512,512]{2,1,0:T(8,128)(2,1)}, bf16[4,512,512]{2,1,0:T(8,128)(2,1)S(1)}, u32[]{:S(2)}) copy-start(bf16[4,512,512]{2,1,0:T(8,128)(2,1)S(1)} %get-tuple-element.19.weight_ref) | copy-start | bytes 6291460
  20.3 42.5 %collective-permute-start.1 = (bf16[4,512,512]{2,1,0:T(8,128)(2,1)}, bf16[4,512,512]{2,1,0:T(8,128)(2,1)S(1)}, u32[]{:S(2)}, u32[]{:S(2)}) collective-permute-start(bf16[4,512,512]{2,1,0:T(8,128)(2,1)} %get-tuple-element.20), channel_id=1, source_target_pairs={{0,1},{1,0},{2,3},{3,2},{4,5},{5,4},{6,7},{7,6},{8,9},{9,8},{10,11... | collective-permute-start | bytes 6291464 | tf_op jit(solution)/shard_map/ppermute | solution.py:314
  21.0 11.4 %copy-start.2 = (bf16[4,512,256]{2,1,0:T(8,128)(2,1)S(1)}, bf16[4,512,256]{2,1,0:T(8,128)(2,1)}, u32[]{:S(2)}) copy-start(bf16[4,512,256]{2,1,0:T(8,128)(2,1)} %constant.77.clone.table_ref) | copy-start | bytes 3145732
  21.0 40.3 %copy-start.6 = (f32[512]{0:T(512)S(1)}, f32[512]{0:T(512)}, u32[]{:S(2)}) copy-start(f32[512]{0:T(512)} %param.11) | copy-start | bytes 6148
  32.4 28.9 %copy-start.3 = (bf16[512,512]{1,0:T(8,128)(2,1)S(1)}, bf16[512,512]{1,0:T(8,128)(2,1)}, u32[]{:S(2)}) copy-start(bf16[512,512]{1,0:T(8,128)(2,1)} %query_ref.1) | copy-start | bytes 1572868
  32.4 28.9 %copy-start.4 = (bf16[512,512]{1,0:T(8,128)(2,1)S(1)}, bf16[512,512]{1,0:T(8,128)(2,1)}, u32[]{:S(2)}) copy-start(bf16[512,512]{1,0:T(8,128)(2,1)} %get-tuple-element.18.mixed_ref) | copy-start | bytes 1572868
  32.4 29.2 %copy-start.1 = (bf16[4,512,512]{2,1,0:T(8,128)(2,1)S(1)}, bf16[4,512,512]{2,1,0:T(8,128)(2,1)}, u32[]{:S(2)}) copy-start(bf16[4,512,512]{2,1,0:T(8,128)(2,1)} %copy-done) | copy-start | bytes 6291460
  32.4 1.2 %copy-start.5 = (f32[4,128,256]{2,1,0:T(8,128)S(1)}, f32[4,128,256]{2,1,0:T(8,128)}, u32[]{:S(2)}) copy-start(f32[4,128,256]{2,1,0:T(8,128)} %taps_spectrum.1.h_ref) | copy-start | bytes 1572868
  61.5 2.0 %collective-permute-start = (bf16[512,512]{1,0:T(8,128)(2,1)S(1)}, bf16[512,512]{1,0:T(8,128)(2,1)S(1)}, u32[]{:S(2)}, u32[]{:S(2)}) collective-permute-start(bf16[512,512]{1,0:T(8,128)(2,1)S(1)} %gate.1.gated_ref), channel_id=1, source_target_pairs={{0,1},{1,0},{2,3},{3,2},{4,5},{5,4},{6,7},{7,6},{8,9},{9,8},{10,11... | collective-permute-start | bytes 1572872 | tf_op jit(solution)/shard_map/ppermute | solution.py:314
  64.0 9.8 %collective-permute-start.6 = (bf16[256,512]{1,0:T(8,128)(2,1)S(1)}, bf16[256,512]{1,0:T(8,128)(2,1)S(1)}, u32[]{:S(2)}, u32[]{:S(2)}) collective-permute-start(bf16[256,512]{1,0:T(8,128)(2,1)S(1)} %get-tuple-element.28), channel_id=1, source_target_pairs={{0,6},{1,7},{2,0},{3,1},{4,2},{5,3},{6,4},{7,5},{8,14},{9,15},{10,... | collective-permute-start | bytes 786440 | tf_op jit(solution)/shard_map/ppermute | solution.py:314
  67.1 10.5 %collective-permute-start.3 = (bf16[256,512]{1,0:T(8,128)(2,1)S(1)}, bf16[256,512]{1,0:T(8,128)(2,1)S(1)}, u32[]{:S(2)}, u32[]{:S(2)}) collective-permute-start(bf16[256,512]{1,0:T(8,128)(2,1)S(1)} %get-tuple-element.24), channel_id=1, source_target_pairs={{0,2},{1,3},{2,4},{3,5},{4,6},{5,7},{6,0},{7,1},{8,10},{9,11},{10,... | collective-permute-start | bytes 786440 | tf_op jit(solution)/shard_map/ppermute | solution.py:314
  68.0 11.3 %collective-permute-start.2 = (bf16[256,512]{1,0:T(8,128)(2,1)S(1)}, bf16[256,512]{1,0:T(8,128)(2,1)S(1)}, u32[]{:S(2)}, u32[]{:S(2)}) collective-permute-start(bf16[256,512]{1,0:T(8,128)(2,1)S(1)} %get-tuple-element.22), channel_id=1, source_target_pairs={{0,6},{1,7},{2,0},{3,1},{4,2},{5,3},{6,4},{7,5},{8,14},{9,15},{10,... | collective-permute-start | bytes 786440 | tf_op jit(solution)/shard_map/ppermute | solution.py:314
  71.4 11.7 %collective-permute-start.5 = (bf16[256,512]{1,0:T(8,128)(2,1)S(1)}, bf16[256,512]{1,0:T(8,128)(2,1)S(1)}, u32[]{:S(2)}, u32[]{:S(2)}) collective-permute-start(bf16[256,512]{1,0:T(8,128)(2,1)S(1)} %get-tuple-element.26), channel_id=1, source_target_pairs={{0,2},{1,3},{2,4},{3,5},{4,6},{5,7},{6,0},{7,1},{8,10},{9,11},{10,... | collective-permute-start | bytes 786440 | tf_op jit(solution)/shard_map/ppermute | solution.py:314
  73.8 10.3 %collective-permute-start.7 = (bf16[256,512]{1,0:T(8,128)(2,1)S(1)}, bf16[256,512]{1,0:T(8,128)(2,1)S(1)}, u32[]{:S(2)}, u32[]{:S(2)}) collective-permute-start(bf16[256,512]{1,0:T(8,128)(2,1)S(1)} %add_convert_fusion), channel_id=1, source_target_pairs={{0,6},{1,7},{2,0},{3,1},{4,2},{5,3},{6,4},{7,5},{8,14},{9,15},{10,... | collective-permute-start | bytes 786440 | tf_op jit(solution)/shard_map/ppermute | solution.py:314
  77.7 9.9 %collective-permute-start.4 = (bf16[256,512]{1,0:T(8,128)(2,1)S(1)}, bf16[256,512]{1,0:T(8,128)(2,1)S(1)}, u32[]{:S(2)}, u32[]{:S(2)}) collective-permute-start(bf16[256,512]{1,0:T(8,128)(2,1)S(1)} %add_convert_fusion.1), channel_id=1, source_target_pairs={{0,2},{1,3},{2,4},{3,5},{4,6},{5,7},{6,0},{7,1},{8,10},{9,11},{10,... | collective-permute-start | bytes 786440 | tf_op jit(solution)/shard_map/ppermute | solution.py:314

commit v3 on v2

--- a/solution.py
+++ b/solution.py
@@ -25,49 +25,70 @@
     return table.astype(jnp.bfloat16)
 
 
-def mix_kernel(key_ref, value_ref, mixed_ref, turned_ref):
-    product = (key_ref[...].astype(jnp.float32) * value_ref[...].astype(jnp.float32)).astype(jnp.bfloat16)
-    mixed_ref[...] = product
-    turned_ref[...] = product.T
+def mix_kernel(chunks, key_ref, value_ref, mixed_ref, turned_ref, keys, values, sems):
+    size = key_ref.shape[0] // chunks
+
+    def fetch(k):
+        rows = pl.ds(k * size, size)
+        return (
+            pltpu.make_async_copy(key_ref.at[rows], keys.at[rows], sems.at[0, k]),
+            pltpu.make_async_copy(value_ref.at[rows], values.at[rows], sems.at[1, k]),
+        )
+
+    for k in range(chunks):
+        for copy in fetch(k):
+            copy.start()
+    for k in range(chunks):
+        for copy in fetch(k):
+            copy.wait()
+        rows = slice(k * size, (k + 1) * size)
+        product = (keys[rows, :].astype(jnp.float32) * values[rows, :].astype(jnp.float32)).astype(jnp.bfloat16)
+        mixed_ref[rows, :] = product
+        turned_ref[:, rows] = product.T
 
 
 def mix(key_gate, value_in):
     length, width = key_gate.shape
-    return pl.pallas_call(
-        mix_kernel,
-        grid=(width // LANES,),
-        in_specs=[pl.BlockSpec((length, LANES), lambda i: (0, i))] * 2,
-        out_specs=[
-            pl.BlockSpec((length, LANES), lambda i: (0, i)),
-            pl.BlockSpec((LANES, length), lambda i: (i, 0)),
-        ],
+    chunks = length // LANES
+    return pl.pallas_call(
+        functools.partial(mix_kernel, chunks),
+        in_specs=[pl.BlockSpec(memory_space=pl.ANY)] * 2,
+        out_specs=[pl.BlockSpec(memory_space=pltpu.VMEM)] * 2,
         out_shape=[
             jax.ShapeDtypeStruct((length, width), jnp.bfloat16),
             jax.ShapeDtypeStruct((width, length), jnp.bfloat16),
         ],
+        scratch_shapes=[pltpu.VMEM((length, width), jnp.bfloat16)] * 2 + [pltpu.SemaphoreType.DMA((2, chunks))],
         cost_estimate=pl.CostEstimate(flops=length * width, bytes_accessed=8 * length * width, transcendentals=0),
         name="mix",
     )(key_gate, value_in)
 
 
-def taps_kernel(few, place_ref, taps_ref, table_ref, out_ref, turned):
-    step = pl.program_id(0)
-    length = table_ref.shape[1]
+def taps_kernel(few, place_ref, taps_ref, table_ref, out_ref, taps, turned, sems):
+    tiles, length, _ = table_ref.shape
+    column = pl.multiple_of(place_ref[0] * LANES, LANES)
+
+    def fetch(k):
+        rows = pl.ds(k * length, length)
+        return pltpu.make_async_copy(taps_ref.at[rows, pl.ds(column, LANES)], taps.at[rows], sems.at[k])
+
+    for k in range(WIN):
+        fetch(k).start()
     first = place_ref[1] * few
     rows = lax.broadcasted_iota(jnp.int32, (few, LANES), 0)
     lanes = lax.broadcasted_iota(jnp.int32, (few, LANES), 1)
     pick = (lanes == rows + first).astype(jnp.bfloat16)
-    picked = lax.dot_general(
-        pick, taps_ref[...].astype(jnp.bfloat16), (((1,), (1,)), ((), ())), preferred_element_type=jnp.float32
-    ).astype(jnp.bfloat16)
-    for half in range(2):
-        start = pl.multiple_of((2 * step + half) * few, few)
-        turned[pl.ds(start, few), :] = picked[:, half * length : (half + 1) * length]
-
-    @pl.when(step == pl.num_programs(0) - 1)
-    def _():
-        for tile in range(table_ref.shape[0]):
-            out_ref[tile] = jnp.dot(turned[...], table_ref[tile], preferred_element_type=jnp.float32)
+    for k in range(WIN):
+        fetch(k).wait()
+        picked = lax.dot_general(
+            pick,
+            taps[k * length : (k + 1) * length, :].astype(jnp.bfloat16),
+            (((1,), (1,)), ((), ())),
+            preferred_element_type=jnp.float32,
+        )
+        turned[k * few : (k + 1) * few, :] = picked.astype(jnp.bfloat16)
+    for tile in range(tiles):
+        out_ref[tile] = jnp.dot(turned[...], table_ref[tile], preferred_element_type=jnp.float32)
 
 
 def taps_spectrum(place, filter_taps, table, few):
@@ -77,13 +98,13 @@
         functools.partial(taps_kernel, few),
         grid_spec=pltpu.PrefetchScalarGridSpec(
             num_scalar_prefetch=1,
-            grid=(WIN // 2,),
-            in_specs=[
-                pl.BlockSpec((2 * length, LANES), lambda i, place: (i, place[0])),
-                pl.BlockSpec((tiles, length, pair), lambda i, place: (0, 0, 0)),
+            in_specs=[pl.BlockSpec(memory_space=pl.ANY), pl.BlockSpec(memory_space=pltpu.VMEM)],
+            out_specs=pl.BlockSpec(memory_space=pltpu.VMEM),
+            scratch_shapes=[
+                pltpu.VMEM((WIN * length, LANES), jnp.float32),
+                pltpu.VMEM((rows, length), jnp.bfloat16),
+                pltpu.SemaphoreType.DMA((WIN,)),
             ],
-            out_specs=pl.BlockSpec((tiles, rows, pair), lambda i, place: (0, 0, 0)),
-            scratch_shapes=[pltpu.VMEM((rows, length), jnp.bfloat16)],
         ),
         out_shape=jax.ShapeDtypeStruct((tiles, rows, pair), jnp.float32),
         cost_estimate=pl.CostEstimate(
@@ -93,88 +114,88 @@
     )(place, filter_taps, table)
 
 
-def conv_kernel(few, x_ref, h_ref, table_ref, out_ref, window, total, product, gathered):
-    tile = pl.program_id(0)
-    tiles = pl.num_programs(0)
-    count, length = x_ref.shape
+def conv_kernel(few, x_ref, h_ref, table_ref, out_ref, rows, taps, table, window, product, sems):
+    tiles, length, pair = table_ref.shape
+    count = x_ref.shape[0]
     spans = count // few
-    spectrum = jnp.dot(x_ref[...], table_ref[0], preferred_element_type=jnp.float32)
-    real, imag = spectrum[:, :LANES], spectrum[:, LANES:]
-    sign = jnp.where(tile < tiles // 2, 1.0, -1.0).astype(jnp.float32)
-    zero = jnp.zeros((few, LANES), jnp.float32)
-    before_real = jnp.concatenate([zero, real[:-few]], axis=0)
-    before_imag = jnp.concatenate([zero, imag[:-few]], axis=0)
-    window_real = before_real + sign * imag
-    window_imag = before_imag - sign * real
-    window[0] = window_real
-    window[1] = window_imag
-    window[2] = window_real + window_imag
-    for part in range(few // 8):
-        low = part * 8
+
+    def fetch(k):
+        if k == 0:
+            return pltpu.make_async_copy(x_ref, rows, sems.at[0])
+        tile = (k - 1) // 2
+        if k % 2:
+            return pltpu.make_async_copy(table_ref.at[tile], table.at[tile], sems.at[k])
+        return pltpu.make_async_copy(h_ref.at[tile], taps.at[tile], sems.at[k])
+
+    for k in range(1 + 2 * tiles):
+        fetch(k).start()
+    fetch(0).wait()
+    for tile in range(tiles):
+        fetch(1 + 2 * tile).wait()
+        spectrum = jnp.dot(rows[...], table[tile], preferred_element_type=jnp.float32)
+        fetch(2 + 2 * tile).wait()
+        sign = 1.0 if tile < tiles // 2 else -1.0
+        for span in range(spans):
+            now = slice(span * few, (span + 1) * few)
+            window_real = sign * spectrum[now, LANES:]
+            window_imag = -sign * spectrum[now, :LANES]
+            if span > 0:
+                before = slice((span - 1) * few, span * few)
+                window_real = spectrum[before, :LANES] + window_real
+                window_imag = spectrum[before, LANES:] + window_imag
+            window[tile, 0, now, :] = window_real
+            window[tile, 1, now, :] = window_imag
+            window[tile, 2, now, :] = window_real + window_imag
         first, plus, minus = [], [], []
         for lag in range(WIN):
-            h_real = h_ref[0, lag * few + low : lag * few + low + 8, :LANES]
-            h_imag = h_ref[0, lag * few + low : lag * few + low + 8, LANES:]
+            h_real = (-sign / length) * taps[tile, lag * few : (lag + 1) * few, :LANES]
+            h_imag = (-sign / length) * taps[tile, lag * few : (lag + 1) * few, LANES:]
             first.append(h_real)
             plus.append(h_real + h_imag)
             minus.append(h_imag - h_real)
-        for span in range(spans):
-            one = two = three = None
-            for lag in range(min(WIN, span + 1)):
-                at = (span - lag) * few + low
-                term_one = first[lag] * window[2, at : at + 8, :]
-                term_two = plus[lag] * window[1, at : at + 8, :]
-                term_three = minus[lag] * window[0, at : at + 8, :]
-                one = term_one if one is None else one + term_one
-                two = term_two if two is None else two + term_two
-                three = term_three if three is None else three + term_three
-            at = span * few + low
-            total[0, at : at + 8, :] = one + three
-            total[1, at : at + 8, :] = one - two
-    scale = sign * (1.0 / length)
-    product[:, :LANES] = (-scale * total[0]).astype(jnp.bfloat16)
-    product[:, LANES:] = (scale * total[1]).astype(jnp.bfloat16)
-    part_out = lax.dot_general(
-        product[...], table_ref[0], (((1,), (1,)), ((), ())), preferred_element_type=jnp.float32
-    )
-
-    @pl.when(tile == 0)
-    def _():
-        gathered[...] = part_out
-
-    @pl.when(tile > 0)
-    def _():
-        gathered[...] += part_out
-
-    @pl.when(tile == tiles - 1)
-    def _():
-        out_ref[...] = gathered[...].astype(jnp.bfloat16)
+        for low in range(0, few, 8):
+            part = slice(low, low + 8)
+            for span in range(spans):
+                one = two = three = None
+                for lag in range(min(WIN, span + 1)):
+                    at = (span - lag) * few + low
+                    term_one = first[lag][part] * window[tile, 2, at : at + 8, :]
+                    term_two = plus[lag][part] * window[tile, 1, at : at + 8, :]
+                    term_three = minus[lag][part] * window[tile, 0, at : at + 8, :]
+                    one = term_one if one is None else one + term_one
+                    two = term_two if two is None else two + term_two
+                    three = term_three if three is None else three + term_three
+                at = span * few + low
+                product[tile, at : at + 8, :LANES] = (one + three).astype(jnp.bfloat16)
+                product[tile, at : at + 8, LANES:] = (two - one).astype(jnp.bfloat16)
+    total = None
+    for tile in range(tiles):
+        term = lax.dot_general(
+            product[tile], table[tile], (((1,), (1,)), ((), ())), preferred_element_type=jnp.float32
+        )
+        total = term if total is None else total + term
+    out_ref[...] = total.astype(jnp.bfloat16)
 
 
 def convolve(turned, spectrum, table, few):
     count, length = turned.shape
     tiles, _, pair = table.shape
-    rows = WIN * few
     return pl.pallas_call(
         functools.partial(conv_kernel, few),
-        grid=(tiles,),
-        in_specs=[
-            pl.BlockSpec((count, length), lambda i: (0, 0)),
-            pl.BlockSpec((1, rows, pair), lambda i: (i, 0, 0)),
-            pl.BlockSpec((1, length, pair), lambda i: (i, 0, 0)),
-        ],
-        out_specs=pl.BlockSpec((count, length), lambda i: (0, 0)),
+        in_specs=[pl.BlockSpec(memory_space=pl.ANY)] * 3,
+        out_specs=pl.BlockSpec(memory_space=pltpu.VMEM),
         out_shape=jax.ShapeDtypeStruct((count, length), jnp.bfloat16),
         scratch_shapes=[
-            pltpu.VMEM((3, count, LANES), jnp.float32),
-            pltpu.VMEM((2, count, LANES), jnp.float32),
-            pltpu.VMEM((count, pair), jnp.bfloat16),
-            pltpu.VMEM((count, length), jnp.float32),
+            pltpu.VMEM((count, length), jnp.bfloat16),
+            pltpu.VMEM(spectrum.shape, jnp.float32),
+            pltpu.VMEM(table.shape, jnp.bfloat16),
+            pltpu.VMEM((tiles, 3, count, LANES), jnp.float32),
+            pltpu.VMEM((tiles, count, pair), jnp.bfloat16),
+            pltpu.SemaphoreType.DMA((1 + 2 * tiles,)),
         ],
         cost_estimate=pl.CostEstimate(
             flops=4 * count * length * tiles * pair, bytes_accessed=3 << 20, transcendentals=0
         ),
-        compiler_params=PARAMS,
         name="convolve",
     )(turned, spectrum, table)
 
@@ -224,7 +245,6 @@
             scratch_shapes=[pltpu.SemaphoreType.DMA((2 * number,))],
         ),
         out_shape=[shape] * 2,
-        compiler_params=pltpu.CompilerParams(vmem_limit_bytes=48 << 20),
         cost_estimate=pl.CostEstimate(flops=0, bytes_accessed=8 << 20, transcendentals=0),
         name="weight_blocks",
     )(blocks, out_weight)

time: 88.9 us -> 87.1 us (0.980)
  local copies, waits for them, and re-layouts: 2.59 us -> 0.64 us
    unnamed x14 -> x8, local copies, waits for them, and re-layouts: 2.51 us -> 0.02 us
    pallas_call x2, Pallas kernels: 9.53 us -> 8.33 us  [the longest x1 5.94 us: convolve(): pl.pallas_call(functools.partial(conv_kernel, few), in_specs=[pl.BlockSpe...]
  transfers between devices with their start and end apart: 9 -> 9, of which waited for: 7 -> 7; matrix products, arithmetic and copies ran while one was open for 1% -> 2% of each run, Pallas kernels for 20% -> 21%
where the time goes in v3:
time: 87.1 us; the launch traced here: 86.7 us
  Pallas kernels  22.3 us (26%)
  blocking collectives  22.2 us (25%)
  starting transfers between devices  21.7 us (25%)
  waiting for transfers between devices  19 us (22%)
    all_to_all x1, blocking collectives, body(): lax.all_to_all(conv_rows.reshape(ctx, few, length), 'ctx', 0, 0)  22.2 us
    ppermute x8, waiting for transfers between devices, ch_shift(): return lax.ppermute(block, 'ch', route)  12.8 us
    all_to_all x1, starting transfers between devices, body(): long_rows = lax.all_to_all(turned.reshape(ctx, few, length), 'ctx', 0, 0)  11.3 us
    ppermute x8, starting transfers between devices, ch_shift(): return lax.ppermute(block, 'ch', route)  10.4 us
    all_to_all x1, waiting for transfers between devices, body(): long_rows = lax.all_to_all(turned.reshape(ctx, few, length), 'ctx', 0, 0)  6.14 us
    pallas_call x1, Pallas kernels, convolve(): pl.pallas_call(functools.partial(conv_kernel, few), in_specs=[pl.BlockSpe...  5.94 us
    pallas_call x1, Pallas kernels, taps_spectrum(): pl.pallas_call(functools.partial(taps_kernel, few), grid_spec=pltpu.Prefe...  5.2 us
    pallas_call x1, Pallas kernels, weight_blocks(): pl.pallas_call(functools.partial(weights_kernel, number), grid_spec=pltpu...  4.87 us
  transfers between devices with their start and end apart: 9, of which 7 were waited for; matrix products, arithmetic and copies ran while one was open for 2% of the time, Pallas kernels for 21%

profile of v3, /device:TPU:32, one launch (start us, length us, event | category | flops | bytes accessed | tf_op | source)
XLA Modules:
  0.0 86.7 jit_solution(9398058397138172034)
XLA Ops:
  0.0 2.4 %mix.1 = (bf16[512,512]{1,0:T(8,128)(2,1)}, bf16[512,512]{1,0:T(8,128)(2,1)}) custom-call(bf16[512,512]{1,0:T(8,128)(2,1)} %key_ref.1, bf16[512,512]{1,0:T(8,128)(2,1)} %value_ref.1), custom_call_target="tpu_custom_call" | custom-call | flops 262144 | bytes 2097152 | tf_op jit(solution)/shard_map/mix/pallas_call | solution.py:53
  2.4 11.3 %all-to-all-start = ((bf16[32,16,512]{2,1,0:T(8,128)(2,1)}), bf16[32,16,512]{2,1,0:T(8,128)(2,1)}, u32[]{:S(2)}, u32[]{:S(2)}) async-start(bf16[32,16,512]{2,1,0:T(8,128)(2,1)} %bitcast.17), calls=%async_computation | async-start | bytes 1048576 | tf_op jit(solution)/shard_map/all_to_all | solution.py:344
  13.7 0.6 stack.47.blocks_ref
  14.4 4.9 %weight_blocks.1 = (bf16[4,512,512]{2,1,0:T(8,128)(2,1)}, bf16[4,512,512]{2,1,0:T(8,128)(2,1)}) custom-call(s32[8]{0:T(128)} %stack.47.blocks_ref, bf16[512,4096]{1,0:T(8,128)(2,1)} %weight_ref.1), custom_call_target="tpu_custom_call" | custom-call | bytes 8388608 | tf_op jit(solution)/shard_map/weight_blocks/pallas_call | solution.py:239
  19.4 0.6 pad_add_fusion.place_ref
  19.9 5.2 %taps_spectrum.1.h_ref = f32[4,128,256]{2,1,0:T(8,128)} custom-call(s32[2]{0:T(128)} %pad_add_fusion.place_ref, f32[4096,512]{1,0:T(8,128)} %taps_ref.1, bf16[4,512,256]{2,1,0:T(8,128)(2,1)} %constant.77.clone.table_ref), custom_call_target="tpu_custom_call" | custom-call | flops 134217728 | bytes 3145728 | tf_op jit(solution)/shard_map/taps_spectrum/pallas_call | solution.py:97
  25.2 6.1 %all-to-all-done = bf16[32,16,512]{2,1,0:T(8,128)(2,1)} async-done(((bf16[32,16,512]{2,1,0:T(8,128)(2,1)}), bf16[32,16,512]{2,1,0:T(8,128)(2,1)}, u32[]{:S(2)}, u32[]{:S(2)}) %all-to-all-start) | async-done | bytes 524320 | tf_op jit(solution)/shard_map/all_to_all | solution.py:344
  31.3 5.9 %convolve.1 = bf16[512,512]{1,0:T(8,128)(2,1)} custom-call(bf16[512,512]{1,0:T(8,128)(2,1)} %bitcast.1.x_ref, f32[4,128,256]{2,1,0:T(8,128)} %taps_spectrum.1.h_ref, bf16[4,512,256]{2,1,0:T(8,128)(2,1)} %constant.77.clone.table_ref), custom_call_target="tpu_custom_call" | custom-call | flops 1073741824 | bytes 3145728 | tf_op jit(solution)/shard_map/convolve/pallas_call | solution.py:183
  37.3 22.2 %all_to_all.10 = bf16[32,16,512]{2,1,0:T(8,128)(2,1)S(1)} all-to-all(bf16[32,16,512]{2,1,0:T(8,128)(2,1)} %bitcast.18), channel_id=1, replica_groups=mesh['ctx'=32,'ch'=8] {'ctx'}, dimensions={0} | all-to-all | bytes 1048576 | tf_op jit(solution)/shard_map/all_to_all | solution.py:346
  59.4 0.3 gate.1.gated_ref
  59.7 0.1 collective-permute-start
  59.8 1.3 %own_part.1.part_ref = f32[4,512,512]{2,1,0:T(8,128)S(1)} custom-call(bf16[512,512]{1,0:T(8,128)(2,1)S(1)} %gate.1.gated_ref, bf16[4,512,512]{2,1,0:T(8,128)(2,1)S(1)} %copy-done), custom_call_target="tpu_custom_call" | custom-call | flops 1073741824 | bytes 2097152 | tf_op jit(solution)/shard_map/own_part/pallas_call | solution.py:261
  61.1 0.6 collective-permute-done.other_ref
  61.7 0.4 project.3
  62.2 3.1 %collective-permute-start.6 = (bf16[256,512]{1,0:T(8,128)(2,1)S(1)}, bf16[256,512]{1,0:T(8,128)(2,1)S(1)}, u32[]{:S(2)}, u32[]{:S(2)}) collective-permute-start(bf16[256,512]{1,0:T(8,128)(2,1)S(1)} %get-tuple-element.28), channel_id=1, source_target_pairs={{0,6},{1,7},{2,0},{3,1},{4,2},{5,3},{6,4},{7,5},{8,14},{9,15},{10,... | collective-permute-start | bytes 786440 | tf_op jit(solution)/shard_map/ppermute | solution.py:334
  65.2 1.0 %project.2 = (bf16[256,512]{1,0:T(8,128)(2,1)S(1)}, bf16[256,512]{1,0:T(8,128)(2,1)S(1)}, bf16[256,512]{1,0:T(8,128)(2,1)S(1)}, bf16[256,512]{1,0:T(8,128)(2,1)S...) custom-call(f32[4,512,512]{2,1,0:T(8,128)S(1)} %own_part.1.part_ref, ...), custom_call_target="tpu_custom_call" | custom-call | flops 805306368 | bytes 3145728 | tf_op jit(solution)/shard_map/project/pallas_call | solution.py:286
  66.2 3.3 %collective-permute-start.2 = (bf16[256,512]{1,0:T(8,128)(2,1)S(1)}, bf16[256,512]{1,0:T(8,128)(2,1)S(1)}, u32[]{:S(2)}, u32[]{:S(2)}) collective-permute-start(bf16[256,512]{1,0:T(8,128)(2,1)S(1)} %get-tuple-element.22), channel_id=1, source_target_pairs={{0,6},{1,7},{2,0},{3,1},{4,2},{5,3},{6,4},{7,5},{8,14},{9,15},{10,... | collective-permute-start | bytes 786440 | tf_op jit(solution)/shard_map/ppermute | solution.py:334
  69.5 2.4 %collective-permute-done.6 = bf16[256,512]{1,0:T(8,128)(2,1)S(1)} collective-permute-done((bf16[256,512]{1,0:T(8,128)(2,1)S(1)}, bf16[256,512]{1,0:T(8,128)(2,1)S(1)}, u32[]{:S(2)}, u32[]{:S(2)}) %collective-permute-start.6) | collective-permute-done | bytes 262176 | tf_op jit(solution)/shard_map/ppermute | solution.py:334
  72.0 3.8 %collective-permute-start.7 = (bf16[256,512]{1,0:T(8,128)(2,1)S(1)}, bf16[256,512]{1,0:T(8,128)(2,1)S(1)}, u32[]{:S(2)}, u32[]{:S(2)}) collective-permute-start(bf16[256,512]{1,0:T(8,128)(2,1)S(1)} %add_convert_fusion), channel_id=1, source_target_pairs={{0,6},{1,7},{2,0},{3,1},{4,2},{5,3},{6,4},{7,5},{8,14},{9,15},{10,... | collective-permute-start | bytes 786440 | tf_op jit(solution)/shard_map/ppermute | solution.py:334
  75.9 1.6 %collective-permute-done.2.refs_1_ = bf16[256,512]{1,0:T(8,128)(2,1)S(1)} collective-permute-done((bf16[256,512]{1,0:T(8,128)(2,1)S(1)}, bf16[256,512]{1,0:T(8,128)(2,1)S(1)}, u32[]{:S(2)}, u32[]{:S(2)}) %collective-permute-start.2) | collective-permute-done | bytes 262176 | tf_op jit(solution)/shard_map/ppermute | solution.py:334
  77.6 3.7 %collective-permute-done.5.refs_4_ = bf16[256,512]{1,0:T(8,128)(2,1)S(1)} collective-permute-done((bf16[256,512]{1,0:T(8,128)(2,1)S(1)}, bf16[256,512]{1,0:T(8,128)(2,1)S(1)}, u32[]{:S(2)}, u32[]{:S(2)}) %collective-permute-start.5) | collective-permute-done | bytes 262176 | tf_op jit(solution)/shard_map/ppermute | solution.py:334
  81.3 1.1 %collective-permute-done.7.refs_5_ = bf16[256,512]{1,0:T(8,128)(2,1)S(1)} collective-permute-done((bf16[256,512]{1,0:T(8,128)(2,1)S(1)}, bf16[256,512]{1,0:T(8,128)(2,1)S(1)}, u32[]{:S(2)}, u32[]{:S(2)}) %collective-permute-start.7) | collective-permute-done | bytes 262176 | tf_op jit(solution)/shard_map/ppermute | solution.py:334
  82.3 3.4 %collective-permute-done.4.refs_2_ = bf16[256,512]{1,0:T(8,128)(2,1)S(1)} collective-permute-done((bf16[256,512]{1,0:T(8,128)(2,1)S(1)}, bf16[256,512]{1,0:T(8,128)(2,1)S(1)}, u32[]{:S(2)}, u32[]{:S(2)}) %collective-permute-start.4) | collective-permute-done | bytes 262176 | tf_op jit(solution)/shard_map/ppermute | solution.py:334
  85.8 1.0 %finish.1 = bf16[512,512]{1,0:T(8,128)(2,1)} custom-call(bf16[256,512]{1,0:T(8,128)(2,1)S(1)} %get-tuple-element.21.refs_0_, bf16[256,512]{1,0:T(8,128)(2,1)S(1)} %collective-permute-done.2.refs_1_, bf16[256,512]{1,0:T(8,128)(2,1)S(1)} %collective-permute-done.4.refs_2_, bf16[256,512]{1,0:T(8,128)(2,1)S(1)} %get-tuple-element.25.refs_3_, ...), custom_call_target="tpu_custom_call" | custom-call | flops 786432 | bytes 2097152 | tf_op jit(solution)/shard_map/finish/pallas_call | solution.py:309
  (16 shorter events, 0.3 us)
Async XLA Ops:
  2.4 28.9 %all-to-all-start = ((bf16[32,16,512]{2,1,0:T(8,128)(2,1)}), bf16[32,16,512]{2,1,0:T(8,128)(2,1)}, u32[]{:S(2)}, u32[]{:S(2)}) async-start(bf16[32,16,512]{2,1,0:T(8,128)(2,1)} %bitcast.17), calls=%async_computation | async-start | bytes 1048576 | tf_op jit(solution)/shard_map/all_to_all | solution.py:344
  19.2 41.8 %collective-permute-start.1 = (bf16[4,512,512]{2,1,0:T(8,128)(2,1)}, bf16[4,512,512]{2,1,0:T(8,128)(2,1)S(1)}, u32[]{:S(2)}, u32[]{:S(2)}) collective-permute-start(bf16[4,512,512]{2,1,0:T(8,128)(2,1)} %get-tuple-element.20), channel_id=1, source_target_pairs={{0,1},{1,0},{2,3},{3,2},{4,5},{5,4},{6,7},{7,6},{8,9},{9,8},{10,11... | collective-permute-start | bytes 6291464 | tf_op jit(solution)/shard_map/ppermute | solution.py:334
  25.1 34.3 %copy-start.1 = (bf16[512,512]{1,0:T(8,128)(2,1)S(1)}, bf16[512,512]{1,0:T(8,128)(2,1)}, u32[]{:S(2)}) copy-start(bf16[512,512]{1,0:T(8,128)(2,1)} %query_ref.1) | copy-start | bytes 1572868
  25.2 34.3 %copy-start.2 = (bf16[512,512]{1,0:T(8,128)(2,1)S(1)}, bf16[512,512]{1,0:T(8,128)(2,1)}, u32[]{:S(2)}) copy-start(bf16[512,512]{1,0:T(8,128)(2,1)} %get-tuple-element.18.mixed_ref) | copy-start | bytes 1572868
  25.2 34.3 %copy-start.3 = (f32[512]{0:T(512)S(1)}, f32[512]{0:T(512)}, u32[]{:S(2)}) copy-start(f32[512]{0:T(512)} %param.11) | copy-start | bytes 6148
  37.3 22.5 %copy-start = (bf16[4,512,512]{2,1,0:T(8,128)(2,1)S(1)}, bf16[4,512,512]{2,1,0:T(8,128)(2,1)}, u32[]{:S(2)}) copy-start(bf16[4,512,512]{2,1,0:T(8,128)(2,1)} %get-tuple-element.19.weight_ref) | copy-start | bytes 6291460
  59.7 2.0 %collective-permute-start = (bf16[512,512]{1,0:T(8,128)(2,1)S(1)}, bf16[512,512]{1,0:T(8,128)(2,1)S(1)}, u32[]{:S(2)}, u32[]{:S(2)}) collective-permute-start(bf16[512,512]{1,0:T(8,128)(2,1)S(1)} %gate.1.gated_ref), channel_id=1, source_target_pairs={{0,1},{1,0},{2,3},{3,2},{4,5},{5,4},{6,7},{7,6},{8,9},{9,8},{10,11... | collective-permute-start | bytes 1572872 | tf_op jit(solution)/shard_map/ppermute | solution.py:334
  62.2 9.8 %collective-permute-start.6 = (bf16[256,512]{1,0:T(8,128)(2,1)S(1)}, bf16[256,512]{1,0:T(8,128)(2,1)S(1)}, u32[]{:S(2)}, u32[]{:S(2)}) collective-permute-start(bf16[256,512]{1,0:T(8,128)(2,1)S(1)} %get-tuple-element.28), channel_id=1, source_target_pairs={{0,6},{1,7},{2,0},{3,1},{4,2},{5,3},{6,4},{7,5},{8,14},{9,15},{10,... | collective-permute-start | bytes 786440 | tf_op jit(solution)/shard_map/ppermute | solution.py:334
  65.2 10.5 %collective-permute-start.3 = (bf16[256,512]{1,0:T(8,128)(2,1)S(1)}, bf16[256,512]{1,0:T(8,128)(2,1)S(1)}, u32[]{:S(2)}, u32[]{:S(2)}) collective-permute-start(bf16[256,512]{1,0:T(8,128)(2,1)S(1)} %get-tuple-element.24), channel_id=1, source_target_pairs={{0,2},{1,3},{2,4},{3,5},{4,6},{5,7},{6,0},{7,1},{8,10},{9,11},{10,... | collective-permute-start | bytes 786440 | tf_op jit(solution)/shard_map/ppermute | solution.py:334
  66.2 11.3 %collective-permute-start.2 = (bf16[256,512]{1,0:T(8,128)(2,1)S(1)}, bf16[256,512]{1,0:T(8,128)(2,1)S(1)}, u32[]{:S(2)}, u32[]{:S(2)}) collective-permute-start(bf16[256,512]{1,0:T(8,128)(2,1)S(1)} %get-tuple-element.22), channel_id=1, source_target_pairs={{0,6},{1,7},{2,0},{3,1},{4,2},{5,3},{6,4},{7,5},{8,14},{9,15},{10,... | collective-permute-start | bytes 786440 | tf_op jit(solution)/shard_map/ppermute | solution.py:334
  69.5 11.7 %collective-permute-start.5 = (bf16[256,512]{1,0:T(8,128)(2,1)S(1)}, bf16[256,512]{1,0:T(8,128)(2,1)S(1)}, u32[]{:S(2)}, u32[]{:S(2)}) collective-permute-start(bf16[256,512]{1,0:T(8,128)(2,1)S(1)} %get-tuple-element.26), channel_id=1, source_target_pairs={{0,2},{1,3},{2,4},{3,5},{4,6},{5,7},{6,0},{7,1},{8,10},{9,11},{10,... | collective-permute-start | bytes 786440 | tf_op jit(solution)/shard_map/ppermute | solution.py:334
  72.0 10.3 %collective-permute-start.7 = (bf16[256,512]{1,0:T(8,128)(2,1)S(1)}, bf16[256,512]{1,0:T(8,128)(2,1)S(1)}, u32[]{:S(2)}, u32[]{:S(2)}) collective-permute-start(bf16[256,512]{1,0:T(8,128)(2,1)S(1)} %add_convert_fusion), channel_id=1, source_target_pairs={{0,6},{1,7},{2,0},{3,1},{4,2},{5,3},{6,4},{7,5},{8,14},{9,15},{10,... | collective-permute-start | bytes 786440 | tf_op jit(solution)/shard_map/ppermute | solution.py:334
  75.8 9.9 %collective-permute-start.4 = (bf16[256,512]{1,0:T(8,128)(2,1)S(1)}, bf16[256,512]{1,0:T(8,128)(2,1)S(1)}, u32[]{:S(2)}, u32[]{:S(2)}) collective-permute-start(bf16[256,512]{1,0:T(8,128)(2,1)S(1)} %add_convert_fusion.1), channel_id=1, source_target_pairs={{0,2},{1,3},{2,4},{3,5},{4,6},{5,7},{6,0},{7,1},{8,10},{9,11},{10,... | collective-permute-start | bytes 786440 | tf_op jit(solution)/shard_map/ppermute | solution.py:334

commit v4 on v3

--- a/solution.py
+++ b/solution.py
@@ -11,6 +11,7 @@
 WIN = 8
 LANES = 128
 CORES = 2
+CHUNKS = 2
 PARAMS = pltpu.CompilerParams(vmem_limit_bytes=20 << 20)
 
 
@@ -25,8 +26,13 @@
     return table.astype(jnp.bfloat16)
 
 
-def mix_kernel(chunks, key_ref, value_ref, mixed_ref, turned_ref, keys, values, sems):
+def mixed_of(key, value):
+    return (key.astype(jnp.float32) * value.astype(jnp.float32)).astype(jnp.bfloat16)
+
+
+def mix_kernel(chunks, key_ref, value_ref, turned_ref, keys, values, turned, sems):
     size = key_ref.shape[0] // chunks
+    share = turned_ref.shape[0] // chunks
 
     def fetch(k):
         rows = pl.ds(k * size, size)
@@ -34,6 +40,10 @@
             pltpu.make_async_copy(key_ref.at[rows], keys.at[rows], sems.at[0, k]),
             pltpu.make_async_copy(value_ref.at[rows], values.at[rows], sems.at[1, k]),
         )
+
+    def put(k):
+        rows = pl.ds(k * share, share)
+        return pltpu.make_async_copy(turned.at[rows], turned_ref.at[rows], sems.at[2, k])
 
     for k in range(chunks):
         for copy in fetch(k):
@@ -42,9 +52,14 @@
         for copy in fetch(k):
             copy.wait()
         rows = slice(k * size, (k + 1) * size)
-        product = (keys[rows, :].astype(jnp.float32) * values[rows, :].astype(jnp.float32)).astype(jnp.bfloat16)
-        mixed_ref[rows, :] = product
-        turned_ref[:, rows] = product.T
+        last = k == chunks - 1
+        for at in range(chunks):
+            columns = slice(at * share, (at + 1) * share)
+            turned[columns, rows] = mixed_of(keys[rows, columns], values[rows, columns]).T
+            if last:
+                put(at).start()
+    for k in range(chunks):
+        put(k).wait()
 
 
 def mix(key_gate, value_in):
@@ -53,13 +68,15 @@
     return pl.pallas_call(
         functools.partial(mix_kernel, chunks),
         in_specs=[pl.BlockSpec(memory_space=pl.ANY)] * 2,
-        out_specs=[pl.BlockSpec(memory_space=pltpu.VMEM)] * 2,
-        out_shape=[
-            jax.ShapeDtypeStruct((length, width), jnp.bfloat16),
-            jax.ShapeDtypeStruct((width, length), jnp.bfloat16),
+        out_specs=pl.BlockSpec(memory_space=pl.ANY),
+        out_shape=jax.ShapeDtypeStruct((width, length), jnp.bfloat16),
+        scratch_shapes=[
+            pltpu.VMEM((length, width), jnp.bfloat16),
+            pltpu.VMEM((length, width), jnp.bfloat16),
+            pltpu.VMEM((width, length), jnp.bfloat16),
+            pltpu.SemaphoreType.DMA((3, chunks)),
         ],
-        scratch_shapes=[pltpu.VMEM((length, width), jnp.bfloat16)] * 2 + [pltpu.SemaphoreType.DMA((2, chunks))],
-        cost_estimate=pl.CostEstimate(flops=length * width, bytes_accessed=8 * length * width, transcendentals=0),
+        cost_estimate=pl.CostEstimate(flops=length * width, bytes_accessed=6 * length * width, transcendentals=0),
         name="mix",
     )(key_gate, value_in)
 
@@ -114,26 +131,45 @@
     )(place, filter_taps, table)
 
 
-def conv_kernel(few, x_ref, h_ref, table_ref, out_ref, rows, taps, table, window, product, sems):
+def conv_kernel(few, x_ref, h_ref, table_ref, out_ref, rows, taps, table, window, product, out, sems):
     tiles, length, pair = table_ref.shape
     count = x_ref.shape[0]
     spans = count // few
 
+    size = count // CHUNKS
+
     def fetch(k):
-        if k == 0:
-            return pltpu.make_async_copy(x_ref, rows, sems.at[0])
-        tile = (k - 1) // 2
-        if k % 2:
-            return pltpu.make_async_copy(table_ref.at[tile], table.at[tile], sems.at[k])
-        return pltpu.make_async_copy(h_ref.at[tile], taps.at[tile], sems.at[k])
-
-    for k in range(1 + 2 * tiles):
+        part = pl.ds(k * size, size)
+        return pltpu.make_async_copy(x_ref.at[part], rows.at[part], sems.at[0, k])
+
+    def fetch_table(tile):
+        return pltpu.make_async_copy(table_ref.at[tile], table.at[tile], sems.at[1, tile])
+
+    def fetch_taps(tile):
+        return pltpu.make_async_copy(h_ref.at[tile], taps.at[tile], sems.at[2, tile])
+
+    def put(k):
+        part = pl.ds(k * size, size)
+        return pltpu.make_async_copy(out.at[part], out_ref.at[part], sems.at[3, k])
+
+    fetch_table(0).start()
+    for k in range(CHUNKS):
         fetch(k).start()
-    fetch(0).wait()
+    fetch_taps(0).start()
+    for tile in range(1, tiles):
+        fetch_table(tile).start()
+        fetch_taps(tile).start()
     for tile in range(tiles):
-        fetch(1 + 2 * tile).wait()
-        spectrum = jnp.dot(rows[...], table[tile], preferred_element_type=jnp.float32)
-        fetch(2 + 2 * tile).wait()
+        fetch_table(tile).wait()
+        spectra = []
+        for k in range(CHUNKS):
+            if tile == 0:
+                fetch(k).wait()
+            spectra.append(
+                jnp.dot(rows[k * size : (k + 1) * size, :], table[tile], preferred_element_type=jnp.float32)
+            )
+        spectrum = jnp.concatenate(spectra, axis=0)
+        fetch_taps(tile).wait()
         sign = 1.0 if tile < tiles // 2 else -1.0
         for span in range(spans):
             now = slice(span * few, (span + 1) * few)
@@ -168,13 +204,18 @@
                 at = span * few + low
                 product[tile, at : at + 8, :LANES] = (one + three).astype(jnp.bfloat16)
                 product[tile, at : at + 8, LANES:] = (two - one).astype(jnp.bfloat16)
-    total = None
-    for tile in range(tiles):
-        term = lax.dot_general(
-            product[tile], table[tile], (((1,), (1,)), ((), ())), preferred_element_type=jnp.float32
-        )
-        total = term if total is None else total + term
-    out_ref[...] = total.astype(jnp.bfloat16)
+    for k in range(CHUNKS):
+        part = slice(k * size, (k + 1) * size)
+        total = None
+        for tile in range(tiles):
+            term = lax.dot_general(
+                product[tile, part, :], table[tile], (((1,), (1,)), ((), ())), preferred_element_type=jnp.float32
+            )
+            total = term if total is None else total + term
+        out[part, :] = total.astype(jnp.bfloat16)
+        put(k).start()
+    for k in range(CHUNKS):
+        put(k).wait()
 
 
 def convolve(turned, spectrum, table, few):
@@ -183,7 +224,7 @@
     return pl.pallas_call(
         functools.partial(conv_kernel, few),
         in_specs=[pl.BlockSpec(memory_space=pl.ANY)] * 3,
-        out_specs=pl.BlockSpec(memory_space=pltpu.VMEM),
+        out_specs=pl.BlockSpec(memory_space=pl.ANY),
         out_shape=jax.ShapeDtypeStruct((count, length), jnp.bfloat16),
         scratch_shapes=[
             pltpu.VMEM((count, length), jnp.bfloat16),
@@ -191,7 +232,8 @@
             pltpu.VMEM(table.shape, jnp.bfloat16),
             pltpu.VMEM((tiles, 3, count, LANES), jnp.float32),
             pltpu.VMEM((tiles, count, pair), jnp.bfloat16),
-            pltpu.SemaphoreType.DMA((1 + 2 * tiles,)),
+            pltpu.VMEM((count, length), jnp.bfloat16),
+            pltpu.SemaphoreType.DMA((4, tiles)),
         ],
         cost_estimate=pl.CostEstimate(
             flops=4 * count * length * tiles * pair, bytes_accessed=3 << 20, transcendentals=0
@@ -207,7 +249,7 @@
 
 
 def gate(conv_turned, mixed, query_gate, skip_gain):
-    length, width = mixed.shape
+    length, width = query_gate.shape
     return pl.pallas_call(
         gate_kernel,
         out_shape=jax.ShapeDtypeStruct((length, width), jnp.bfloat16),
@@ -297,18 +339,31 @@
 
 
 def finish_kernel(*refs):
-    out_ref = refs[-1]
-    half = out_ref.shape[0] // 2
-    for at in range(2):
-        total = sum(ref[...].astype(jnp.float32) for ref in refs[3 * at : 3 * at + 3])
-        out_ref[at * half : (at + 1) * half, :] = total.astype(jnp.bfloat16)
+    out_ref, out, sems = refs[6:]
+    half = refs[0].shape[0]
+    size = half // 2
+
+    def put(k):
+        part = pl.ds(k * size, size)
+        return pltpu.make_async_copy(out.at[part], out_ref.at[part], sems.at[k])
+
+    for k in range(4):
+        rows = slice(k % 2 * size, (k % 2 + 1) * size)
+        total = sum(ref[rows, :].astype(jnp.float32) for ref in refs[3 * (k // 2) : 3 * (k // 2) + 3])
+        out[k * size : (k + 1) * size, :] = total.astype(jnp.bfloat16)
+        put(k).start()
+    for k in range(4):
+        put(k).wait()
 
 
 def finish(low, high):
     half, width = low[0].shape
     return pl.pallas_call(
         finish_kernel,
+        in_specs=[pl.BlockSpec(memory_space=pltpu.VMEM)] * 6,
+        out_specs=pl.BlockSpec(memory_space=pl.ANY),
         out_shape=jax.ShapeDtypeStruct((2 * half, width), jnp.bfloat16),
+        scratch_shapes=[pltpu.VMEM((2 * half, width), jnp.bfloat16), pltpu.SemaphoreType.DMA((4,))],
         compiler_params=PARAMS,
         cost_estimate=pl.CostEstimate(flops=6 * half * width, bytes_accessed=16 * half * width, transcendentals=0),
         name="finish",
@@ -333,7 +388,7 @@
         route = [(i, ((i // CORES + dy) % ring) * CORES + (i % CORES + dcore) % CORES) for i in range(groups)]
         return lax.ppermute(block, "ch", route)
 
-    mixed, turned = mix(key_gate, value_in)
+    turned = mix(key_gate, value_in)
     place = jnp.stack([here // per_tile, here % per_tile]).astype(jnp.int32)
     spectrum = taps_spectrum(place, filter_taps, table, few)
     ahead = [(y + step) % ring for step in (2, 1, 3, 0)]
@@ -345,7 +400,7 @@
     conv_rows = convolve(long_rows.reshape(ctx * few, length), spectrum, table, few)
     conv_turned = lax.all_to_all(conv_rows.reshape(ctx, few, length), "ctx", 0, 0).reshape(width, length)
 
-    gated = gate(conv_turned, mixed, query_gate, skip_gain)
+    gated = gate(conv_turned, mixed_of(key_gate, value_in), query_gate, skip_gain)
     other = ch_shift(gated, 0, 1)
     part = own_part(gated, own_weight)
     across_low, across_high = project((0,), part, other, other_weight)

time: 87.1 us -> 89.5 us (1.028)
  blocking collectives: 22.2 us -> 0 us
  waiting for transfers between devices: 19 us -> 34.5 us
  starting transfers between devices: 21.7 us -> 26.5 us
  local copies, waits for them, and re-layouts: 0.64 us -> 4.04 us
  other arithmetic: 0.71 us -> 2.04 us
    all_to_all x1 -> x0, blocking collectives: 22.2 us -> none  [body(): lax.all_to_all(conv_rows.reshape(ctx, few, length), 'ctx', 0, 0)]
    all_to_all x0 -> x1, waiting for transfers between devices: none -> 15.7 us  [body(): lax.all_to_all(conv_rows.reshape(ctx, few, length), 'ctx', 0, 0)]
    all_to_all x0 -> x1, starting transfers between devices: none -> 4.87 us  [body(): lax.all_to_all(conv_rows.reshape(ctx, few, length), 'ctx', 0, 0)]
    unnamed x8, local copies, waits for them, and re-layouts: 0.02 us -> 3.43 us
    convert_element_type x0 -> x1, other arithmetic: none -> 1.34 us  [mixed_of(): (key.astype(jnp.float32) * value.astype(jnp.float32)).astype(jnp.bfloat16)]
  transfers between devices with their start and end apart: 9 -> 10, of which waited for: 7 -> 7; matrix products, arithmetic and copies ran while one was open for 2% -> 3% of each run, Pallas kernels for 21% -> 20%
where the time goes in v4:
time: 89.5 us; the launch traced here: 89 us
  waiting for transfers between devices  34.5 us (39%)
  starting transfers between devices  26.5 us (30%)
  Pallas kernels  21.7 us (24%)
  local copies, waits for them, and re-layouts  4.04 us (5%)
  other arithmetic  2.04 us (2%)
    all_to_all x1, waiting for transfers between devices, body(): lax.all_to_all(conv_rows.reshape(ctx, few, length), 'ctx', 0, 0)  15.7 us
    ppermute x8, waiting for transfers between devices, ch_shift(): return lax.ppermute(block, 'ch', route)  12.6 us
    all_to_all x1, starting transfers between devices, body(): long_rows = lax.all_to_all(turned.reshape(ctx, few, length), 'ctx', 0, 0)  11.2 us
    ppermute x8, starting transfers between devices, ch_shift(): return lax.ppermute(block, 'ch', route)  10.4 us
    all_to_all x1, waiting for transfers between devices, body(): long_rows = lax.all_to_all(turned.reshape(ctx, few, length), 'ctx', 0, 0)  6.15 us
    pallas_call x1, Pallas kernels, convolve(): pl.pallas_call(functools.partial(conv_kernel, few), in_specs=[pl.BlockSpe...  5.62 us
    pallas_call x1, Pallas kernels, taps_spectrum(): pl.pallas_call(functools.partial(taps_kernel, few), grid_spec=pltpu.Prefe...  5.17 us
    all_to_all x1, starting transfers between devices, body(): lax.all_to_all(conv_rows.reshape(ctx, few, length), 'ctx', 0, 0)  4.87 us
  transfers between devices with their start and end apart: 10, of which 7 were waited for; matrix products, arithmetic and copies ran while one was open for 3% of the time, Pallas kernels for 20%

profile of v4, /device:TPU:32, one launch (start us, length us, event | category | flops | bytes accessed | tf_op | source)
XLA Modules:
  0.0 89.0 jit_solution(6623614939343627341)
XLA Ops:
  0.0 2.3 %mix.1 = bf16[512,512]{1,0:T(8,128)(2,1)} custom-call(bf16[512,512]{1,0:T(8,128)(2,1)} %key_ref.1, bf16[512,512]{1,0:T(8,128)(2,1)} %value_ref.1), custom_call_target="tpu_custom_call" | custom-call | flops 262144 | bytes 1572864 | tf_op jit(solution)/shard_map/mix/pallas_call | solution.py:68
  2.3 11.2 %all-to-all-start = ((bf16[32,16,512]{2,1,0:T(8,128)(2,1)}), bf16[32,16,512]{2,1,0:T(8,128)(2,1)S(1)}, u32[]{:S(2)}, u32[]{:S(2)}) async-start(bf16[32,16,512]{2,1,0:T(8,128)(2,1)} %bitcast.17), calls=%async_computation | async-start | bytes 1048576 | tf_op jit(solution)/shard_map/all_to_all | solution.py:399
  13.6 0.6 stack.47.blocks_ref
  14.2 4.9 %weight_blocks.1 = (bf16[4,512,512]{2,1,0:T(8,128)(2,1)}, bf16[4,512,512]{2,1,0:T(8,128)(2,1)}) custom-call(s32[8]{0:T(128)} %stack.47.blocks_ref, bf16[512,4096]{1,0:T(8,128)(2,1)} %weight_ref.1), custom_call_target="tpu_custom_call" | custom-call | bytes 8388608 | tf_op jit(solution)/shard_map/weight_blocks/pallas_call | solution.py:281
  19.7 5.2 %taps_spectrum.1.h_ref = f32[4,128,256]{2,1,0:T(8,128)} custom-call(s32[2]{0:T(128)} %pad_add_fusion.place_ref, f32[4096,512]{1,0:T(8,128)} %taps_ref.1, bf16[4,512,256]{2,1,0:T(8,128)(2,1)} %constant.77.clone.table_ref), custom_call_target="tpu_custom_call" | custom-call | flops 134217728 | bytes 3145728 | tf_op jit(solution)/shard_map/taps_spectrum/pallas_call | solution.py:114
  24.9 6.1 %all-to-all-done = bf16[32,16,512]{2,1,0:T(8,128)(2,1)S(1)} async-done(((bf16[32,16,512]{2,1,0:T(8,128)(2,1)}), bf16[32,16,512]{2,1,0:T(8,128)(2,1)S(1)}, u32[]{:S(2)}, u32[]{:S(2)}) %all-to-all-start) | async-done | bytes 524320 | tf_op jit(solution)/shard_map/all_to_all | solution.py:399
  31.1 0.8 copy-done.3
  31.9 5.6 %convolve.1 = bf16[512,512]{1,0:T(8,128)(2,1)} custom-call(bf16[512,512]{1,0:T(8,128)(2,1)} %bitcast.18, f32[4,128,256]{2,1,0:T(8,128)} %taps_spectrum.1.h_ref, bf16[4,512,256]{2,1,0:T(8,128)(2,1)} %constant.77.clone.table_ref), custom_call_target="tpu_custom_call" | custom-call | flops 1073741824 | bytes 3145728 | tf_op jit(solution)/shard_map/convolve/pallas_call | solution.py:224
  37.5 4.9 %all-to-all-start.1 = ((bf16[32,16,512]{2,1,0:T(8,128)(2,1)}), bf16[32,16,512]{2,1,0:T(8,128)(2,1)S(1)}, u32[]{:S(2)}, u32[]{:S(2)}) async-start(bf16[32,16,512]{2,1,0:T(8,128)(2,1)} %bitcast.19), calls=%async_computation.1 | async-start | bytes 1048576 | tf_op jit(solution)/shard_map/all_to_all | solution.py:401
  42.4 1.3 %multiply_convert_fusion.mixed_ref = bf16[512,512]{1,0:T(8,128)(2,1)S(1)} fusion(bf16[512,512]{1,0:T(8,128)(2,1)} %value_ref.1, bf16[512,512]{1,0:T(8,128)(2,1)} %key_ref.1), kind=kLoop, calls=%fused_computation | loop fusion | flops 1048576 | bytes 1572864 | tf_op jit(solution)/shard_map/convert_element_type | solution.py:30
  43.7 15.7 %all-to-all-done.1 = bf16[32,16,512]{2,1,0:T(8,128)(2,1)S(1)} async-done(((bf16[32,16,512]{2,1,0:T(8,128)(2,1)}), bf16[32,16,512]{2,1,0:T(8,128)(2,1)S(1)}, u32[]{:S(2)}, u32[]{:S(2)}) %all-to-all-start.1) | async-done | bytes 524320 | tf_op jit(solution)/shard_map/all_to_all | solution.py:401
  59.5 1.0 %copy-done.1 = bf16[512,512]{1,0:T(8,128)(2,1)S(1)} copy-done((bf16[512,512]{1,0:T(8,128)(2,1)S(1)}, bf16[512,512]{1,0:T(8,128)(2,1)}, u32[]{:S(2)}) %copy-start.1) | copy-done | bytes 524312
  60.9 1.6 %copy-done = bf16[4,512,512]{2,1,0:T(8,128)(2,1)S(1)} copy-done((bf16[4,512,512]{2,1,0:T(8,128)(2,1)S(1)}, bf16[4,512,512]{2,1,0:T(8,128)(2,1)}, u32[]{:S(2)}) %copy-start) | copy-done | bytes 2097176
  62.5 1.2 %own_part.1.part_ref = f32[4,512,512]{2,1,0:T(8,128)S(1)} custom-call(bf16[512,512]{1,0:T(8,128)(2,1)S(1)} %gate.1.gated_ref, bf16[4,512,512]{2,1,0:T(8,128)(2,1)S(1)} %copy-done), custom_call_target="tpu_custom_call" | custom-call | flops 1073741824 | bytes 2097152 | tf_op jit(solution)/shard_map/own_part/pallas_call | solution.py:303
  64.2 3.1 %collective-permute-start.6 = (bf16[256,512]{1,0:T(8,128)(2,1)S(1)}, bf16[256,512]{1,0:T(8,128)(2,1)S(1)}, u32[]{:S(2)}, u32[]{:S(2)}) collective-permute-start(bf16[256,512]{1,0:T(8,128)(2,1)S(1)} %get-tuple-element.24), channel_id=1, source_target_pairs={{0,6},{1,7},{2,0},{3,1},{4,2},{5,3},{6,4},{7,5},{8,14},{9,15},{10,... | collective-permute-start | bytes 786440 | tf_op jit(solution)/shard_map/ppermute | solution.py:389
  67.3 1.0 %project.2 = (bf16[256,512]{1,0:T(8,128)(2,1)S(1)}, bf16[256,512]{1,0:T(8,128)(2,1)S(1)}, bf16[256,512]{1,0:T(8,128)(2,1)S(1)}, bf16[256,512]{1,0:T(8,128)(2,1)S...) custom-call(f32[4,512,512]{2,1,0:T(8,128)S(1)} %own_part.1.part_ref, ...), custom_call_target="tpu_custom_call" | custom-call | flops 805306368 | bytes 3145728 | tf_op jit(solution)/shard_map/project/pallas_call | solution.py:328
  68.2 3.3 %collective-permute-start.2 = (bf16[256,512]{1,0:T(8,128)(2,1)S(1)}, bf16[256,512]{1,0:T(8,128)(2,1)S(1)}, u32[]{:S(2)}, u32[]{:S(2)}) collective-permute-start(bf16[256,512]{1,0:T(8,128)(2,1)S(1)} %get-tuple-element.18), channel_id=1, source_target_pairs={{0,6},{1,7},{2,0},{3,1},{4,2},{5,3},{6,4},{7,5},{8,14},{9,15},{10,... | collective-permute-start | bytes 786440 | tf_op jit(solution)/shard_map/ppermute | solution.py:389
  71.6 2.4 %collective-permute-done.6 = bf16[256,512]{1,0:T(8,128)(2,1)S(1)} collective-permute-done((bf16[256,512]{1,0:T(8,128)(2,1)S(1)}, bf16[256,512]{1,0:T(8,128)(2,1)S(1)}, u32[]{:S(2)}, u32[]{:S(2)}) %collective-permute-start.6) | collective-permute-done | bytes 262176 | tf_op jit(solution)/shard_map/ppermute | solution.py:389
  74.0 3.8 %collective-permute-start.7 = (bf16[256,512]{1,0:T(8,128)(2,1)S(1)}, bf16[256,512]{1,0:T(8,128)(2,1)S(1)}, u32[]{:S(2)}, u32[]{:S(2)}) collective-permute-start(bf16[256,512]{1,0:T(8,128)(2,1)S(1)} %add_convert_fusion), channel_id=1, source_target_pairs={{0,6},{1,7},{2,0},{3,1},{4,2},{5,3},{6,4},{7,5},{8,14},{9,15},{10,... | collective-permute-start | bytes 786440 | tf_op jit(solution)/shard_map/ppermute | solution.py:389
  78.0 1.6 %collective-permute-done.2.refs_1_ = bf16[256,512]{1,0:T(8,128)(2,1)S(1)} collective-permute-done((bf16[256,512]{1,0:T(8,128)(2,1)S(1)}, bf16[256,512]{1,0:T(8,128)(2,1)S(1)}, u32[]{:S(2)}, u32[]{:S(2)}) %collective-permute-start.2) | collective-permute-done | bytes 262176 | tf_op jit(solution)/shard_map/ppermute | solution.py:389
  79.6 3.7 %collective-permute-done.5.refs_4_ = bf16[256,512]{1,0:T(8,128)(2,1)S(1)} collective-permute-done((bf16[256,512]{1,0:T(8,128)(2,1)S(1)}, bf16[256,512]{1,0:T(8,128)(2,1)S(1)}, u32[]{:S(2)}, u32[]{:S(2)}) %collective-permute-start.5) | collective-permute-done | bytes 262176 | tf_op jit(solution)/shard_map/ppermute | solution.py:389
  83.3 1.5 %collective-permute-done.7.refs_5_ = bf16[256,512]{1,0:T(8,128)(2,1)S(1)} collective-permute-done((bf16[256,512]{1,0:T(8,128)(2,1)S(1)}, bf16[256,512]{1,0:T(8,128)(2,1)S(1)}, u32[]{:S(2)}, u32[]{:S(2)}) %collective-permute-start.7) | collective-permute-done | bytes 262176 | tf_op jit(solution)/shard_map/ppermute | solution.py:389
  84.7 3.4 %collective-permute-done.4.refs_2_ = bf16[256,512]{1,0:T(8,128)(2,1)S(1)} collective-permute-done((bf16[256,512]{1,0:T(8,128)(2,1)S(1)}, bf16[256,512]{1,0:T(8,128)(2,1)S(1)}, u32[]{:S(2)}, u32[]{:S(2)}) %collective-permute-start.4) | collective-permute-done | bytes 262176 | tf_op jit(solution)/shard_map/ppermute | solution.py:389
  88.1 0.9 finish.1
  (18 shorter events, 1.7 us)
Async XLA Ops:
  2.3 28.8 %all-to-all-start = ((bf16[32,16,512]{2,1,0:T(8,128)(2,1)}), bf16[32,16,512]{2,1,0:T(8,128)(2,1)S(1)}, u32[]{:S(2)}, u32[]{:S(2)}) async-start(bf16[32,16,512]{2,1,0:T(8,128)(2,1)} %bitcast.17), calls=%async_computation | async-start | bytes 1048576 | tf_op jit(solution)/shard_map/all_to_all | solution.py:399
  19.0 44.7 %collective-permute-start.1 = (bf16[4,512,512]{2,1,0:T(8,128)(2,1)}, bf16[4,512,512]{2,1,0:T(8,128)(2,1)S(1)}, u32[]{:S(2)}, u32[]{:S(2)}) collective-permute-start(bf16[4,512,512]{2,1,0:T(8,128)(2,1)} %get-tuple-element.16), channel_id=1, source_target_pairs={{0,1},{1,0},{2,3},{3,2},{4,5},{5,4},{6,7},{7,6},{8,9},{9,8},{10,11... | collective-permute-start | bytes 6291464 | tf_op jit(solution)/shard_map/ppermute | solution.py:389
  24.9 34.5 %copy-start.2 = (f32[512]{0:T(512)S(1)}, f32[512]{0:T(512)}, u32[]{:S(2)}) copy-start(f32[512]{0:T(512)} %param.11) | copy-start | bytes 6148
  31.1 0.8 copy-start.3
  37.5 21.9 %all-to-all-start.1 = ((bf16[32,16,512]{2,1,0:T(8,128)(2,1)}), bf16[32,16,512]{2,1,0:T(8,128)(2,1)S(1)}, u32[]{:S(2)}, u32[]{:S(2)}) async-start(bf16[32,16,512]{2,1,0:T(8,128)(2,1)} %bitcast.19), calls=%async_computation.1 | async-start | bytes 1048576 | tf_op jit(solution)/shard_map/all_to_all | solution.py:401
  59.5 1.0 %copy-start.1 = (bf16[512,512]{1,0:T(8,128)(2,1)S(1)}, bf16[512,512]{1,0:T(8,128)(2,1)}, u32[]{:S(2)}) copy-start(bf16[512,512]{1,0:T(8,128)(2,1)} %query_ref.1) | copy-start | bytes 1572868
  60.8 3.0 %collective-permute-start = (bf16[512,512]{1,0:T(8,128)(2,1)S(1)}, bf16[512,512]{1,0:T(8,128)(2,1)S(1)}, u32[]{:S(2)}, u32[]{:S(2)}) collective-permute-start(bf16[512,512]{1,0:T(8,128)(2,1)S(1)} %gate.1.gated_ref), channel_id=1, source_target_pairs={{0,1},{1,0},{2,3},{3,2},{4,5},{5,4},{6,7},{7,6},{8,9},{9,8},{10,11... | collective-permute-start | bytes 1572872 | tf_op jit(solution)/shard_map/ppermute | solution.py:389
  60.9 1.6 %copy-start = (bf16[4,512,512]{2,1,0:T(8,128)(2,1)S(1)}, bf16[4,512,512]{2,1,0:T(8,128)(2,1)}, u32[]{:S(2)}) copy-start(bf16[4,512,512]{2,1,0:T(8,128)(2,1)} %get-tuple-element.15.weight_ref) | copy-start | bytes 6291460
  64.2 9.8 %collective-permute-start.6 = (bf16[256,512]{1,0:T(8,128)(2,1)S(1)}, bf16[256,512]{1,0:T(8,128)(2,1)S(1)}, u32[]{:S(2)}, u32[]{:S(2)}) collective-permute-start(bf16[256,512]{1,0:T(8,128)(2,1)S(1)} %get-tuple-element.24), channel_id=1, source_target_pairs={{0,6},{1,7},{2,0},{3,1},{4,2},{5,3},{6,4},{7,5},{8,14},{9,15},{10,... | collective-permute-start | bytes 786440 | tf_op jit(solution)/shard_map/ppermute | solution.py:389
  67.3 10.5 %collective-permute-start.3 = (bf16[256,512]{1,0:T(8,128)(2,1)S(1)}, bf16[256,512]{1,0:T(8,128)(2,1)S(1)}, u32[]{:S(2)}, u32[]{:S(2)}) collective-permute-start(bf16[256,512]{1,0:T(8,128)(2,1)S(1)} %get-tuple-element.20), channel_id=1, source_target_pairs={{0,2},{1,3},{2,4},{3,5},{4,6},{5,7},{6,0},{7,1},{8,10},{9,11},{10,... | collective-permute-start | bytes 786440 | tf_op jit(solution)/shard_map/ppermute | solution.py:389
  68.2 11.3 %collective-permute-start.2 = (bf16[256,512]{1,0:T(8,128)(2,1)S(1)}, bf16[256,512]{1,0:T(8,128)(2,1)S(1)}, u32[]{:S(2)}, u32[]{:S(2)}) collective-permute-start(bf16[256,512]{1,0:T(8,128)(2,1)S(1)} %get-tuple-element.18), channel_id=1, source_target_pairs={{0,6},{1,7},{2,0},{3,1},{4,2},{5,3},{6,4},{7,5},{8,14},{9,15},{10,... | collective-permute-start | bytes 786440 | tf_op jit(solution)/shard_map/ppermute | solution.py:389
  71.6 11.7 %collective-permute-start.5 = (bf16[256,512]{1,0:T(8,128)(2,1)S(1)}, bf16[256,512]{1,0:T(8,128)(2,1)S(1)}, u32[]{:S(2)}, u32[]{:S(2)}) collective-permute-start(bf16[256,512]{1,0:T(8,128)(2,1)S(1)} %get-tuple-element.22), channel_id=1, source_target_pairs={{0,2},{1,3},{2,4},{3,5},{4,6},{5,7},{6,0},{7,1},{8,10},{9,11},{10,... | collective-permute-start | bytes 786440 | tf_op jit(solution)/shard_map/ppermute | solution.py:389
  74.0 10.7 %collective-permute-start.7 = (bf16[256,512]{1,0:T(8,128)(2,1)S(1)}, bf16[256,512]{1,0:T(8,128)(2,1)S(1)}, u32[]{:S(2)}, u32[]{:S(2)}) collective-permute-start(bf16[256,512]{1,0:T(8,128)(2,1)S(1)} %add_convert_fusion), channel_id=1, source_target_pairs={{0,6},{1,7},{2,0},{3,1},{4,2},{5,3},{6,4},{7,5},{8,14},{9,15},{10,... | collective-permute-start | bytes 786440 | tf_op jit(solution)/shard_map/ppermute | solution.py:389
  77.9 10.3 %collective-permute-start.4 = (bf16[256,512]{1,0:T(8,128)(2,1)S(1)}, bf16[256,512]{1,0:T(8,128)(2,1)S(1)}, u32[]{:S(2)}, u32[]{:S(2)}) collective-permute-start(bf16[256,512]{1,0:T(8,128)(2,1)S(1)} %add_convert_fusion.1), channel_id=1, source_target_pairs={{0,2},{1,3},{2,4},{3,5},{4,6},{5,7},{6,0},{7,1},{8,10},{9,11},{10,... | collective-permute-start | bytes 786440 | tf_op jit(solution)/shard_map/ppermute | solution.py:389

commit v5 on v3

--- a/solution.py
+++ b/solution.py
@@ -11,6 +11,7 @@
 WIN = 8
 LANES = 128
 CORES = 2
+CONV_BYTES = 53 << 20
 PARAMS = pltpu.CompilerParams(vmem_limit_bytes=20 << 20)
 
 
@@ -119,21 +120,26 @@
     count = x_ref.shape[0]
     spans = count // few
 
-    def fetch(k):
-        if k == 0:
-            return pltpu.make_async_copy(x_ref, rows, sems.at[0])
-        tile = (k - 1) // 2
-        if k % 2:
-            return pltpu.make_async_copy(table_ref.at[tile], table.at[tile], sems.at[k])
-        return pltpu.make_async_copy(h_ref.at[tile], taps.at[tile], sems.at[k])
-
-    for k in range(1 + 2 * tiles):
-        fetch(k).start()
-    fetch(0).wait()
+    def fetch_rows():
+        return pltpu.make_async_copy(x_ref, rows, sems.at[0, 0])
+
+    def fetch_table(tile):
+        return pltpu.make_async_copy(table_ref.at[tile], table.at[tile], sems.at[1, tile])
+
+    def fetch_taps(tile):
+        return pltpu.make_async_copy(h_ref.at[tile], taps.at[tile], sems.at[2, tile])
+
+    fetch_rows().start()
+    fetch_table(0).start()
+    fetch_taps(0).start()
+    fetch_rows().wait()
+    for tile in range(1, tiles):
+        fetch_table(tile).start()
+        fetch_taps(tile).start()
     for tile in range(tiles):
-        fetch(1 + 2 * tile).wait()
+        fetch_table(tile).wait()
         spectrum = jnp.dot(rows[...], table[tile], preferred_element_type=jnp.float32)
-        fetch(2 + 2 * tile).wait()
+        fetch_taps(tile).wait()
         sign = 1.0 if tile < tiles // 2 else -1.0
         for span in range(spans):
             now = slice(span * few, (span + 1) * few)
@@ -191,8 +197,9 @@
             pltpu.VMEM(table.shape, jnp.bfloat16),
             pltpu.VMEM((tiles, 3, count, LANES), jnp.float32),
             pltpu.VMEM((tiles, count, pair), jnp.bfloat16),
-            pltpu.SemaphoreType.DMA((1 + 2 * tiles,)),
+            pltpu.SemaphoreType.DMA((3, tiles)),
         ],
+        compiler_params=pltpu.CompilerParams(vmem_limit_bytes=CONV_BYTES),
         cost_estimate=pl.CostEstimate(
             flops=4 * count * length * tiles * pair, bytes_accessed=3 << 20, transcendentals=0
         ),
@@ -297,18 +304,31 @@
 
 
 def finish_kernel(*refs):
-    out_ref = refs[-1]
-    half = out_ref.shape[0] // 2
-    for at in range(2):
-        total = sum(ref[...].astype(jnp.float32) for ref in refs[3 * at : 3 * at + 3])
-        out_ref[at * half : (at + 1) * half, :] = total.astype(jnp.bfloat16)
+    out_ref, out, sems = refs[6:]
+    half = refs[0].shape[0]
+    size = half // 2
+
+    def put(k):
+        part = pl.ds(k * size, size)
+        return pltpu.make_async_copy(out.at[part], out_ref.at[part], sems.at[k])
+
+    for k in range(4):
+        rows = slice(k % 2 * size, (k % 2 + 1) * size)
+        total = sum(ref[rows, :].astype(jnp.float32) for ref in refs[3 * (k // 2) : 3 * (k // 2) + 3])
+        out[k * size : (k + 1) * size, :] = total.astype(jnp.bfloat16)
+        put(k).start()
+    for k in range(4):
+        put(k).wait()
 
 
 def finish(low, high):
     half, width = low[0].shape
     return pl.pallas_call(
         finish_kernel,
+        in_specs=[pl.BlockSpec(memory_space=pltpu.VMEM)] * 6,
+        out_specs=pl.BlockSpec(memory_space=pl.ANY),
         out_shape=jax.ShapeDtypeStruct((2 * half, width), jnp.bfloat16),
+        scratch_shapes=[pltpu.VMEM((2 * half, width), jnp.bfloat16), pltpu.SemaphoreType.DMA((4,))],
         compiler_params=PARAMS,
         cost_estimate=pl.CostEstimate(flops=6 * half * width, bytes_accessed=16 * half * width, transcendentals=0),
         name="finish",

time: 87.1 us -> 86 us (0.987)
  no operation moved by 1% of the time
where the time goes in v5:
time: 86 us; the launch traced here: 85.7 us
  Pallas kernels  21.7 us (25%)
  starting transfers between devices  21.7 us (25%)
  blocking collectives  21.7 us (25%)
  waiting for transfers between devices  19 us (22%)
    all_to_all x1, blocking collectives, body(): lax.all_to_all(conv_rows.reshape(ctx, few, length), 'ctx', 0, 0)  21.7 us
    ppermute x8, waiting for transfers between devices, ch_shift(): return lax.ppermute(block, 'ch', route)  12.8 us
    all_to_all x1, starting transfers between devices, body(): long_rows = lax.all_to_all(turned.reshape(ctx, few, length), 'ctx', 0, 0)  11.3 us
    ppermute x8, starting transfers between devices, ch_shift(): return lax.ppermute(block, 'ch', route)  10.4 us
    all_to_all x1, waiting for transfers between devices, body(): long_rows = lax.all_to_all(turned.reshape(ctx, few, length), 'ctx', 0, 0)  6.14 us
    pallas_call x1, Pallas kernels, convolve(): pl.pallas_call(functools.partial(conv_kernel, few), in_specs=[pl.BlockSpe...  5.39 us
    pallas_call x1, Pallas kernels, taps_spectrum(): pl.pallas_call(functools.partial(taps_kernel, few), grid_spec=pltpu.Prefe...  5.2 us
    pallas_call x1, Pallas kernels, weight_blocks(): pl.pallas_call(functools.partial(weights_kernel, number), grid_spec=pltpu...  4.87 us
  transfers between devices with their start and end apart: 9, of which 7 were waited for; matrix products, arithmetic and copies ran while one was open for 2% of the time, Pallas kernels for 21%

profile of v5, /device:TPU:32, one launch (start us, length us, event | category | flops | bytes accessed | tf_op | source)
XLA Modules:
  0.0 85.7 jit_solution(131602417703593037)
XLA Ops:
  0.0 2.4 %mix.1 = (bf16[512,512]{1,0:T(8,128)(2,1)}, bf16[512,512]{1,0:T(8,128)(2,1)}) custom-call(bf16[512,512]{1,0:T(8,128)(2,1)} %key_ref.1, bf16[512,512]{1,0:T(8,128)(2,1)} %value_ref.1), custom_call_target="tpu_custom_call" | custom-call | flops 262144 | bytes 2097152 | tf_op jit(solution)/shard_map/mix/pallas_call | solution.py:54
  2.4 11.3 %all-to-all-start = ((bf16[32,16,512]{2,1,0:T(8,128)(2,1)}), bf16[32,16,512]{2,1,0:T(8,128)(2,1)}, u32[]{:S(2)}, u32[]{:S(2)}) async-start(bf16[32,16,512]{2,1,0:T(8,128)(2,1)} %bitcast.18), calls=%async_computation | async-start | bytes 1048576 | tf_op jit(solution)/shard_map/all_to_all | solution.py:364
  13.7 0.6 stack.47.blocks_ref
  14.4 4.9 %weight_blocks.1 = (bf16[4,512,512]{2,1,0:T(8,128)(2,1)}, bf16[4,512,512]{2,1,0:T(8,128)(2,1)}) custom-call(s32[8]{0:T(128)} %stack.47.blocks_ref, bf16[512,4096]{1,0:T(8,128)(2,1)} %weight_ref.1), custom_call_target="tpu_custom_call" | custom-call | bytes 8388608 | tf_op jit(solution)/shard_map/weight_blocks/pallas_call | solution.py:246
  19.4 0.6 pad_add_fusion.place_ref
  19.9 5.2 %taps_spectrum.1.h_ref = f32[4,128,256]{2,1,0:T(8,128)} custom-call(s32[2]{0:T(128)} %pad_add_fusion.place_ref, f32[4096,512]{1,0:T(8,128)} %taps_ref.1, bf16[4,512,256]{2,1,0:T(8,128)(2,1)} %constant.77.clone.table_ref), custom_call_target="tpu_custom_call" | custom-call | flops 134217728 | bytes 3145728 | tf_op jit(solution)/shard_map/taps_spectrum/pallas_call | solution.py:98
  25.2 6.1 %all-to-all-done = bf16[32,16,512]{2,1,0:T(8,128)(2,1)} async-done(((bf16[32,16,512]{2,1,0:T(8,128)(2,1)}), bf16[32,16,512]{2,1,0:T(8,128)(2,1)}, u32[]{:S(2)}, u32[]{:S(2)}) %all-to-all-start) | async-done | bytes 524320 | tf_op jit(solution)/shard_map/all_to_all | solution.py:364
  31.3 5.4 %convolve.1 = bf16[512,512]{1,0:T(8,128)(2,1)S(1)} custom-call(bf16[512,512]{1,0:T(8,128)(2,1)} %bitcast.1.x_ref, f32[4,128,256]{2,1,0:T(8,128)} %taps_spectrum.1.h_ref, bf16[4,512,256]{2,1,0:T(8,128)(2,1)} %constant.77.clone.table_ref), custom_call_target="tpu_custom_call" | custom-call | flops 1073741824 | bytes 3145728 | tf_op jit(solution)/shard_map/convolve/pallas_call | solution.py:189
  36.7 21.7 %all_to_all.10 = bf16[32,16,512]{2,1,0:T(8,128)(2,1)S(1)} all-to-all(bf16[32,16,512]{2,1,0:T(8,128)(2,1)S(1)} %bitcast.16), channel_id=1, replica_groups=mesh['ctx'=32,'ch'=8] {'ctx'}, dimensions={0} | all-to-all | bytes 1048576 | tf_op jit(solution)/shard_map/all_to_all | solution.py:366
  58.5 0.3 gate.1.gated_ref
  58.7 0.1 collective-permute-start
  58.9 1.3 %own_part.1.part_ref = f32[4,512,512]{2,1,0:T(8,128)S(1)} custom-call(bf16[512,512]{1,0:T(8,128)(2,1)S(1)} %gate.1.gated_ref, bf16[4,512,512]{2,1,0:T(8,128)(2,1)S(1)} %copy-done), custom_call_target="tpu_custom_call" | custom-call | flops 1073741824 | bytes 2097152 | tf_op jit(solution)/shard_map/own_part/pallas_call | solution.py:268
  60.1 0.6 collective-permute-done.other_ref
  60.7 0.4 project.3
  61.2 3.1 %collective-permute-start.6 = (bf16[256,512]{1,0:T(8,128)(2,1)S(1)}, bf16[256,512]{1,0:T(8,128)(2,1)S(1)}, u32[]{:S(2)}, u32[]{:S(2)}) collective-permute-start(bf16[256,512]{1,0:T(8,128)(2,1)S(1)} %get-tuple-element.28), channel_id=1, source_target_pairs={{0,6},{1,7},{2,0},{3,1},{4,2},{5,3},{6,4},{7,5},{8,14},{9,15},{10,... | collective-permute-start | bytes 786440 | tf_op jit(solution)/shard_map/ppermute | solution.py:354
  64.3 1.0 %project.2 = (bf16[256,512]{1,0:T(8,128)(2,1)S(1)}, bf16[256,512]{1,0:T(8,128)(2,1)S(1)}, bf16[256,512]{1,0:T(8,128)(2,1)S(1)}, bf16[256,512]{1,0:T(8,128)(2,1)S...) custom-call(f32[4,512,512]{2,1,0:T(8,128)S(1)} %own_part.1.part_ref, ...), custom_call_target="tpu_custom_call" | custom-call | flops 805306368 | bytes 3145728 | tf_op jit(solution)/shard_map/project/pallas_call | solution.py:293
  65.3 3.3 %collective-permute-start.2 = (bf16[256,512]{1,0:T(8,128)(2,1)S(1)}, bf16[256,512]{1,0:T(8,128)(2,1)S(1)}, u32[]{:S(2)}, u32[]{:S(2)}) collective-permute-start(bf16[256,512]{1,0:T(8,128)(2,1)S(1)} %get-tuple-element.22), channel_id=1, source_target_pairs={{0,6},{1,7},{2,0},{3,1},{4,2},{5,3},{6,4},{7,5},{8,14},{9,15},{10,... | collective-permute-start | bytes 786440 | tf_op jit(solution)/shard_map/ppermute | solution.py:354
  68.6 2.4 %collective-permute-done.6 = bf16[256,512]{1,0:T(8,128)(2,1)S(1)} collective-permute-done((bf16[256,512]{1,0:T(8,128)(2,1)S(1)}, bf16[256,512]{1,0:T(8,128)(2,1)S(1)}, u32[]{:S(2)}, u32[]{:S(2)}) %collective-permute-start.6) | collective-permute-done | bytes 262176 | tf_op jit(solution)/shard_map/ppermute | solution.py:354
  71.0 3.8 %collective-permute-start.7 = (bf16[256,512]{1,0:T(8,128)(2,1)S(1)}, bf16[256,512]{1,0:T(8,128)(2,1)S(1)}, u32[]{:S(2)}, u32[]{:S(2)}) collective-permute-start(bf16[256,512]{1,0:T(8,128)(2,1)S(1)} %add_convert_fusion), channel_id=1, source_target_pairs={{0,6},{1,7},{2,0},{3,1},{4,2},{5,3},{6,4},{7,5},{8,14},{9,15},{10,... | collective-permute-start | bytes 786440 | tf_op jit(solution)/shard_map/ppermute | solution.py:354
  75.0 1.6 %collective-permute-done.2.refs_1_ = bf16[256,512]{1,0:T(8,128)(2,1)S(1)} collective-permute-done((bf16[256,512]{1,0:T(8,128)(2,1)S(1)}, bf16[256,512]{1,0:T(8,128)(2,1)S(1)}, u32[]{:S(2)}, u32[]{:S(2)}) %collective-permute-start.2) | collective-permute-done | bytes 262176 | tf_op jit(solution)/shard_map/ppermute | solution.py:354
  76.6 3.7 %collective-permute-done.5.refs_4_ = bf16[256,512]{1,0:T(8,128)(2,1)S(1)} collective-permute-done((bf16[256,512]{1,0:T(8,128)(2,1)S(1)}, bf16[256,512]{1,0:T(8,128)(2,1)S(1)}, u32[]{:S(2)}, u32[]{:S(2)}) %collective-permute-start.5) | collective-permute-done | bytes 262176 | tf_op jit(solution)/shard_map/ppermute | solution.py:354
  80.3 1.1 %collective-permute-done.7.refs_5_ = bf16[256,512]{1,0:T(8,128)(2,1)S(1)} collective-permute-done((bf16[256,512]{1,0:T(8,128)(2,1)S(1)}, bf16[256,512]{1,0:T(8,128)(2,1)S(1)}, u32[]{:S(2)}, u32[]{:S(2)}) %collective-permute-start.7) | collective-permute-done | bytes 262176 | tf_op jit(solution)/shard_map/ppermute | solution.py:354
  81.4 3.4 %collective-permute-done.4.refs_2_ = bf16[256,512]{1,0:T(8,128)(2,1)S(1)} collective-permute-done((bf16[256,512]{1,0:T(8,128)(2,1)S(1)}, bf16[256,512]{1,0:T(8,128)(2,1)S(1)}, u32[]{:S(2)}, u32[]{:S(2)}) %collective-permute-start.4) | collective-permute-done | bytes 262176 | tf_op jit(solution)/shard_map/ppermute | solution.py:354
  84.8 0.9 %finish.1 = bf16[512,512]{1,0:T(8,128)(2,1)} custom-call(bf16[256,512]{1,0:T(8,128)(2,1)S(1)} %get-tuple-element.21.refs_0_, bf16[256,512]{1,0:T(8,128)(2,1)S(1)} %collective-permute-done.2.refs_1_, bf16[256,512]{1,0:T(8,128)(2,1)S(1)} %collective-permute-done.4.refs_2_, bf16[256,512]{1,0:T(8,128)(2,1)S(1)} %get-tuple-element.25.refs_3_, ...), custom_call_target="tpu_custom_call" | custom-call | flops 786432 | bytes 2097152 | tf_op jit(solution)/shard_map/finish/pallas_call | solution.py:326
  (16 shorter events, 0.3 us)
Async XLA Ops:
  2.4 28.9 %all-to-all-start = ((bf16[32,16,512]{2,1,0:T(8,128)(2,1)}), bf16[32,16,512]{2,1,0:T(8,128)(2,1)}, u32[]{:S(2)}, u32[]{:S(2)}) async-start(bf16[32,16,512]{2,1,0:T(8,128)(2,1)} %bitcast.18), calls=%async_computation | async-start | bytes 1048576 | tf_op jit(solution)/shard_map/all_to_all | solution.py:364
  19.2 40.9 %collective-permute-start.1 = (bf16[4,512,512]{2,1,0:T(8,128)(2,1)}, bf16[4,512,512]{2,1,0:T(8,128)(2,1)S(1)}, u32[]{:S(2)}, u32[]{:S(2)}) collective-permute-start(bf16[4,512,512]{2,1,0:T(8,128)(2,1)} %get-tuple-element.20), channel_id=1, source_target_pairs={{0,1},{1,0},{2,3},{3,2},{4,5},{5,4},{6,7},{7,6},{8,9},{9,8},{10,11... | collective-permute-start | bytes 6291464 | tf_op jit(solution)/shard_map/ppermute | solution.py:354
  25.1 33.3 %copy-start.1 = (bf16[512,512]{1,0:T(8,128)(2,1)S(1)}, bf16[512,512]{1,0:T(8,128)(2,1)}, u32[]{:S(2)}) copy-start(bf16[512,512]{1,0:T(8,128)(2,1)} %query_ref.1) | copy-start | bytes 1572868
  25.2 33.3 %copy-start.2 = (bf16[512,512]{1,0:T(8,128)(2,1)S(1)}, bf16[512,512]{1,0:T(8,128)(2,1)}, u32[]{:S(2)}) copy-start(bf16[512,512]{1,0:T(8,128)(2,1)} %get-tuple-element.18.mixed_ref) | copy-start | bytes 1572868
  25.2 33.3 %copy-start.3 = (f32[512]{0:T(512)S(1)}, f32[512]{0:T(512)}, u32[]{:S(2)}) copy-start(f32[512]{0:T(512)} %param.11) | copy-start | bytes 6148
  31.3 27.5 %copy-start = (bf16[4,512,512]{2,1,0:T(8,128)(2,1)S(1)}, bf16[4,512,512]{2,1,0:T(8,128)(2,1)}, u32[]{:S(2)}) copy-start(bf16[4,512,512]{2,1,0:T(8,128)(2,1)} %get-tuple-element.19.weight_ref) | copy-start | bytes 6291460
  58.7 2.0 %collective-permute-start = (bf16[512,512]{1,0:T(8,128)(2,1)S(1)}, bf16[512,512]{1,0:T(8,128)(2,1)S(1)}, u32[]{:S(2)}, u32[]{:S(2)}) collective-permute-start(bf16[512,512]{1,0:T(8,128)(2,1)S(1)} %gate.1.gated_ref), channel_id=1, source_target_pairs={{0,1},{1,0},{2,3},{3,2},{4,5},{5,4},{6,7},{7,6},{8,9},{9,8},{10,11... | collective-permute-start | bytes 1572872 | tf_op jit(solution)/shard_map/ppermute | solution.py:354
  61.2 9.8 %collective-permute-start.6 = (bf16[256,512]{1,0:T(8,128)(2,1)S(1)}, bf16[256,512]{1,0:T(8,128)(2,1)S(1)}, u32[]{:S(2)}, u32[]{:S(2)}) collective-permute-start(bf16[256,512]{1,0:T(8,128)(2,1)S(1)} %get-tuple-element.28), channel_id=1, source_target_pairs={{0,6},{1,7},{2,0},{3,1},{4,2},{5,3},{6,4},{7,5},{8,14},{9,15},{10,... | collective-permute-start | bytes 786440 | tf_op jit(solution)/shard_map/ppermute | solution.py:354
  64.3 10.5 %collective-permute-start.3 = (bf16[256,512]{1,0:T(8,128)(2,1)S(1)}, bf16[256,512]{1,0:T(8,128)(2,1)S(1)}, u32[]{:S(2)}, u32[]{:S(2)}) collective-permute-start(bf16[256,512]{1,0:T(8,128)(2,1)S(1)} %get-tuple-element.24), channel_id=1, source_target_pairs={{0,2},{1,3},{2,4},{3,5},{4,6},{5,7},{6,0},{7,1},{8,10},{9,11},{10,... | collective-permute-start | bytes 786440 | tf_op jit(solution)/shard_map/ppermute | solution.py:354
  65.3 11.3 %collective-permute-start.2 = (bf16[256,512]{1,0:T(8,128)(2,1)S(1)}, bf16[256,512]{1,0:T(8,128)(2,1)S(1)}, u32[]{:S(2)}, u32[]{:S(2)}) collective-permute-start(bf16[256,512]{1,0:T(8,128)(2,1)S(1)} %get-tuple-element.22), channel_id=1, source_target_pairs={{0,6},{1,7},{2,0},{3,1},{4,2},{5,3},{6,4},{7,5},{8,14},{9,15},{10,... | collective-permute-start | bytes 786440 | tf_op jit(solution)/shard_map/ppermute | solution.py:354
  68.6 11.7 %collective-permute-start.5 = (bf16[256,512]{1,0:T(8,128)(2,1)S(1)}, bf16[256,512]{1,0:T(8,128)(2,1)S(1)}, u32[]{:S(2)}, u32[]{:S(2)}) collective-permute-start(bf16[256,512]{1,0:T(8,128)(2,1)S(1)} %get-tuple-element.26), channel_id=1, source_target_pairs={{0,2},{1,3},{2,4},{3,5},{4,6},{5,7},{6,0},{7,1},{8,10},{9,11},{10,... | collective-permute-start | bytes 786440 | tf_op jit(solution)/shard_map/ppermute | solution.py:354
  71.0 10.3 %collective-permute-start.7 = (bf16[256,512]{1,0:T(8,128)(2,1)S(1)}, bf16[256,512]{1,0:T(8,128)(2,1)S(1)}, u32[]{:S(2)}, u32[]{:S(2)}) collective-permute-start(bf16[256,512]{1,0:T(8,128)(2,1)S(1)} %add_convert_fusion), channel_id=1, source_target_pairs={{0,6},{1,7},{2,0},{3,1},{4,2},{5,3},{6,4},{7,5},{8,14},{9,15},{10,... | collective-permute-start | bytes 786440 | tf_op jit(solution)/shard_map/ppermute | solution.py:354
  74.9 9.9 %collective-permute-start.4 = (bf16[256,512]{1,0:T(8,128)(2,1)S(1)}, bf16[256,512]{1,0:T(8,128)(2,1)S(1)}, u32[]{:S(2)}, u32[]{:S(2)}) collective-permute-start(bf16[256,512]{1,0:T(8,128)(2,1)S(1)} %add_convert_fusion.1), channel_id=1, source_target_pairs={{0,2},{1,3},{2,4},{3,5},{4,6},{5,7},{6,0},{7,1},{8,10},{9,11},{10,... | collective-permute-start | bytes 786440 | tf_op jit(solution)/shard_map/ppermute | solution.py:354

commit v6 on v5

--- a/solution.py
+++ b/solution.py
@@ -65,8 +65,8 @@
     )(key_gate, value_in)
 
 
-def taps_kernel(few, place_ref, taps_ref, table_ref, out_ref, taps, turned, sems):
-    tiles, length, _ = table_ref.shape
+def taps_kernel(few, place_ref, taps_ref, out_ref, taps, sems):
+    length = out_ref.shape[1]
     column = pl.multiple_of(place_ref[0] * LANES, LANES)
 
     def fetch(k):
@@ -87,59 +87,35 @@
             (((1,), (1,)), ((), ())),
             preferred_element_type=jnp.float32,
         )
-        turned[k * few : (k + 1) * few, :] = picked.astype(jnp.bfloat16)
-    for tile in range(tiles):
-        out_ref[tile] = jnp.dot(turned[...], table_ref[tile], preferred_element_type=jnp.float32)
-
-
-def taps_spectrum(place, filter_taps, table, few):
-    tiles, length, pair = table.shape
-    rows = WIN * few
+        out_ref[k * few : (k + 1) * few, :] = picked.astype(jnp.bfloat16)
+
+
+def turned_taps(place, filter_taps, few):
+    length = filter_taps.shape[0] // WIN
     return pl.pallas_call(
         functools.partial(taps_kernel, few),
         grid_spec=pltpu.PrefetchScalarGridSpec(
             num_scalar_prefetch=1,
-            in_specs=[pl.BlockSpec(memory_space=pl.ANY), pl.BlockSpec(memory_space=pltpu.VMEM)],
+            in_specs=[pl.BlockSpec(memory_space=pl.ANY)],
             out_specs=pl.BlockSpec(memory_space=pltpu.VMEM),
-            scratch_shapes=[
-                pltpu.VMEM((WIN * length, LANES), jnp.float32),
-                pltpu.VMEM((rows, length), jnp.bfloat16),
-                pltpu.SemaphoreType.DMA((WIN,)),
-            ],
-        ),
-        out_shape=jax.ShapeDtypeStruct((tiles, rows, pair), jnp.float32),
+            scratch_shapes=[pltpu.VMEM((WIN * length, LANES), jnp.float32), pltpu.SemaphoreType.DMA((WIN,))],
+        ),
+        out_shape=jax.ShapeDtypeStruct((WIN * few, length), jnp.bfloat16),
         cost_estimate=pl.CostEstimate(
-            flops=2 * rows * length * tiles * pair, bytes_accessed=3 << 20, transcendentals=0
-        ),
-        name="taps_spectrum",
-    )(place, filter_taps, table)
-
-
-def conv_kernel(few, x_ref, h_ref, table_ref, out_ref, rows, taps, table, window, product, sems):
+            flops=2 * few * LANES * WIN * length, bytes_accessed=2 << 20, transcendentals=0
+        ),
+        name="turned_taps",
+    )(place, filter_taps)
+
+
+def conv_kernel(few, x_ref, taps_ref, table_ref, out_ref, window, product):
     tiles, length, pair = table_ref.shape
     count = x_ref.shape[0]
     spans = count // few
 
-    def fetch_rows():
-        return pltpu.make_async_copy(x_ref, rows, sems.at[0, 0])
-
-    def fetch_table(tile):
-        return pltpu.make_async_copy(table_ref.at[tile], table.at[tile], sems.at[1, tile])
-
-    def fetch_taps(tile):
-        return pltpu.make_async_copy(h_ref.at[tile], taps.at[tile], sems.at[2, tile])
-
-    fetch_rows().start()
-    fetch_table(0).start()
-    fetch_taps(0).start()
-    fetch_rows().wait()
-    for tile in range(1, tiles):
-        fetch_table(tile).start()
-        fetch_taps(tile).start()
     for tile in range(tiles):
-        fetch_table(tile).wait()
-        spectrum = jnp.dot(rows[...], table[tile], preferred_element_type=jnp.float32)
-        fetch_taps(tile).wait()
+        spectrum = jnp.dot(x_ref[...], table_ref[tile], preferred_element_type=jnp.float32)
+        taps = jnp.dot(taps_ref[...], table_ref[tile], preferred_element_type=jnp.float32)
         sign = 1.0 if tile < tiles // 2 else -1.0
         for span in range(spans):
             now = slice(span * few, (span + 1) * few)
@@ -154,8 +130,8 @@
             window[tile, 2, now, :] = window_real + window_imag
         first, plus, minus = [], [], []
         for lag in range(WIN):
-            h_real = (-sign / length) * taps[tile, lag * few : (lag + 1) * few, :LANES]
-            h_imag = (-sign / length) * taps[tile, lag * few : (lag + 1) * few, LANES:]
+            h_real = (-sign / length) * taps[lag * few : (lag + 1) * few, :LANES]
+            h_imag = (-sign / length) * taps[lag * few : (lag + 1) * few, LANES:]
             first.append(h_real)
             plus.append(h_real + h_imag)
             minus.append(h_imag - h_real)
@@ -177,34 +153,30 @@
     total = None
     for tile in range(tiles):
         term = lax.dot_general(
-            product[tile], table[tile], (((1,), (1,)), ((), ())), preferred_element_type=jnp.float32
+            product[tile], table_ref[tile], (((1,), (1,)), ((), ())), preferred_element_type=jnp.float32
         )
         total = term if total is None else total + term
     out_ref[...] = total.astype(jnp.bfloat16)
 
 
-def convolve(turned, spectrum, table, few):
+def convolve(turned, taps, table, few):
     count, length = turned.shape
     tiles, _, pair = table.shape
     return pl.pallas_call(
         functools.partial(conv_kernel, few),
-        in_specs=[pl.BlockSpec(memory_space=pl.ANY)] * 3,
+        in_specs=[pl.BlockSpec(memory_space=pltpu.VMEM)] * 3,
         out_specs=pl.BlockSpec(memory_space=pltpu.VMEM),
         out_shape=jax.ShapeDtypeStruct((count, length), jnp.bfloat16),
         scratch_shapes=[
-            pltpu.VMEM((count, length), jnp.bfloat16),
-            pltpu.VMEM(spectrum.shape, jnp.float32),
-            pltpu.VMEM(table.shape, jnp.bfloat16),
             pltpu.VMEM((tiles, 3, count, LANES), jnp.float32),
             pltpu.VMEM((tiles, count, pair), jnp.bfloat16),
-            pltpu.SemaphoreType.DMA((3, tiles)),
         ],
         compiler_params=pltpu.CompilerParams(vmem_limit_bytes=CONV_BYTES),
         cost_estimate=pl.CostEstimate(
             flops=4 * count * length * tiles * pair, bytes_accessed=3 << 20, transcendentals=0
         ),
         name="convolve",
-    )(turned, spectrum, table)
+    )(turned, taps, table)
 
 
 def gate_kernel(conv_ref, mixed_ref, query_ref, skip_ref, gated_ref):
@@ -355,14 +327,14 @@
 
     mixed, turned = mix(key_gate, value_in)
     place = jnp.stack([here // per_tile, here % per_tile]).astype(jnp.int32)
-    spectrum = taps_spectrum(place, filter_taps, table, few)
+    taps = turned_taps(place, filter_taps, few)
     ahead = [(y + step) % ring for step in (2, 1, 3, 0)]
     blocks = jnp.stack([k * CORES + at for at in (1 - core, core) for k in ahead]).astype(jnp.int32)
     own_weight, partner_weight = weight_blocks(blocks, out_weight)
     other_weight = ch_shift(partner_weight, 0, 1)
 
     long_rows = lax.all_to_all(turned.reshape(ctx, few, length), "ctx", 0, 0)
-    conv_rows = convolve(long_rows.reshape(ctx * few, length), spectrum, table, few)
+    conv_rows = convolve(long_rows.reshape(ctx * few, length), taps, table, few)
     conv_turned = lax.all_to_all(conv_rows.reshape(ctx, few, length), "ctx", 0, 0).reshape(width, length)
 
     gated = gate(conv_turned, mixed, query_gate, skip_gain)

time: 86 us -> 85.5 us (level)
  Pallas kernels: 21.7 us -> 18.8 us
  waiting for transfers between devices: 19 us -> 20.4 us
  local copies, waits for them, and re-layouts: 0.64 us -> 1.73 us
    pallas_call x1, Pallas kernels: 5.2 us -> 3.71 us  [turned_taps(): pl.pallas_call(functools.partial(taps_kernel, few), grid_spec=pltpu.Prefe...]
    all_to_all x1, waiting for transfers between devices: 6.14 us -> 7.58 us  [body(): long_rows = lax.all_to_all(turned.reshape(ctx, few, length), 'ctx', 0, 0)]
    pallas_call x1, Pallas kernels: 5.39 us -> 4 us  [convolve(): pl.pallas_call(functools.partial(conv_kernel, few), in_specs=[pl.BlockSpe...]
    unnamed x8 -> x10, local copies, waits for them, and re-layouts: 0.02 us -> 1.07 us
  transfers between devices with their start and end apart: 9 -> 9, of which waited for: 7 -> 7; matrix products, arithmetic and copies ran while one was open for 2% -> 2% of each run, Pallas kernels for 21% -> 18%
where the time goes in v6:
time: 85.5 us; the launch traced here: 85.2 us
  starting transfers between devices  21.7 us (25%)
  blocking collectives  21.6 us (25%)
  waiting for transfers between devices  20.4 us (24%)
  Pallas kernels  18.8 us (22%)
  local copies, waits for them, and re-layouts  1.73 us (2%)
    all_to_all x1, blocking collectives, body(): lax.all_to_all(conv_rows.reshape(ctx, few, length), 'ctx', 0, 0)  21.6 us
    ppermute x8, waiting for transfers between devices, ch_shift(): return lax.ppermute(block, 'ch', route)  12.8 us
    all_to_all x1, starting transfers between devices, body(): long_rows = lax.all_to_all(turned.reshape(ctx, few, length), 'ctx', 0, 0)  11.3 us
    ppermute x8, starting transfers between devices, ch_shift(): return lax.ppermute(block, 'ch', route)  10.4 us
    all_to_all x1, waiting for transfers between devices, body(): long_rows = lax.all_to_all(turned.reshape(ctx, few, length), 'ctx', 0, 0)  7.58 us
    pallas_call x1, Pallas kernels, weight_blocks(): pl.pallas_call(functools.partial(weights_kernel, number), grid_spec=pltpu...  4.87 us
    pallas_call x1, Pallas kernels, convolve(): pl.pallas_call(functools.partial(conv_kernel, few), in_specs=[pl.BlockSpe...  4 us
    pallas_call x1, Pallas kernels, turned_taps(): pl.pallas_call(functools.partial(taps_kernel, few), grid_spec=pltpu.Prefe...  3.71 us
  transfers between devices with their start and end apart: 9, of which 7 were waited for; matrix products, arithmetic and copies ran while one was open for 2% of the time, Pallas kernels for 18%

profile of v6, /device:TPU:32, one launch (start us, length us, event | category | flops | bytes accessed | tf_op | source)
XLA Modules:
  0.0 85.2 jit_solution(1783328528933574585)
XLA Ops:
  0.0 2.4 %mix.1 = (bf16[512,512]{1,0:T(8,128)(2,1)}, bf16[512,512]{1,0:T(8,128)(2,1)}) custom-call(bf16[512,512]{1,0:T(8,128)(2,1)} %key_ref.1, bf16[512,512]{1,0:T(8,128)(2,1)} %value_ref.1), custom_call_target="tpu_custom_call" | custom-call | flops 262144 | bytes 2097152 | tf_op jit(solution)/shard_map/mix/pallas_call | solution.py:54
  2.4 11.3 %all-to-all-start = ((bf16[32,16,512]{2,1,0:T(8,128)(2,1)}), bf16[32,16,512]{2,1,0:T(8,128)(2,1)}, u32[]{:S(2)}, u32[]{:S(2)}) async-start(bf16[32,16,512]{2,1,0:T(8,128)(2,1)} %bitcast.18), calls=%async_computation | async-start | bytes 1048576 | tf_op jit(solution)/shard_map/all_to_all | solution.py:336
  13.7 0.7 stack.47.blocks_ref
  14.4 4.9 %weight_blocks.1 = (bf16[4,512,512]{2,1,0:T(8,128)(2,1)}, bf16[4,512,512]{2,1,0:T(8,128)(2,1)}) custom-call(s32[8]{0:T(128)} %stack.47.blocks_ref, bf16[512,4096]{1,0:T(8,128)(2,1)} %weight_ref.1), custom_call_target="tpu_custom_call" | custom-call | bytes 8388608 | tf_op jit(solution)/shard_map/weight_blocks/pallas_call | solution.py:218
  19.4 0.6 pad_add_fusion.place_ref
  20.0 3.7 %turned_taps.1.taps_ref = bf16[128,512]{1,0:T(8,128)(2,1)} custom-call(s32[2]{0:T(128)} %pad_add_fusion.place_ref, f32[4096,512]{1,0:T(8,128)} %taps_ref.1), custom_call_target="tpu_custom_call" | custom-call | flops 16777216 | bytes 2097152 | tf_op jit(solution)/shard_map/turned_taps/pallas_call | solution.py:95
  23.7 7.6 %all-to-all-done = bf16[32,16,512]{2,1,0:T(8,128)(2,1)} async-done(((bf16[32,16,512]{2,1,0:T(8,128)(2,1)}), bf16[32,16,512]{2,1,0:T(8,128)(2,1)}, u32[]{:S(2)}, u32[]{:S(2)}) %all-to-all-start) | async-done | bytes 524320 | tf_op jit(solution)/shard_map/all_to_all | solution.py:336
  31.3 1.1 %copy-done.3 = bf16[128,512]{1,0:T(8,128)(2,1)S(1)} copy-done((bf16[128,512]{1,0:T(8,128)(2,1)S(1)}, bf16[128,512]{1,0:T(8,128)(2,1)}, u32[]{:S(2)}) %copy-start.3) | copy-done | bytes 131096
  32.4 4.0 %convolve.1 = bf16[512,512]{1,0:T(8,128)(2,1)S(1)} custom-call(bf16[512,512]{1,0:T(8,128)(2,1)} %bitcast.1.x_ref, bf16[128,512]{1,0:T(8,128)(2,1)S(1)} %copy-done.3, bf16[4,512,256]{2,1,0:T(8,128)(2,1)} %constant.77.clone.table_ref), custom_call_target="tpu_custom_call" | custom-call | flops 1073741824 | bytes 3145728 | tf_op jit(solution)/shard_map/convolve/pallas_call | solution.py:165
  36.4 21.6 %all_to_all.10 = bf16[32,16,512]{2,1,0:T(8,128)(2,1)S(1)} all-to-all(bf16[32,16,512]{2,1,0:T(8,128)(2,1)S(1)} %bitcast.16), channel_id=1, replica_groups=mesh['ctx'=32,'ch'=8] {'ctx'}, dimensions={0} | all-to-all | bytes 1048576 | tf_op jit(solution)/shard_map/all_to_all | solution.py:338
  58.0 0.3 gate.1.gated_ref
  58.4 1.3 %own_part.1.part_ref = f32[4,512,512]{2,1,0:T(8,128)S(1)} custom-call(bf16[512,512]{1,0:T(8,128)(2,1)S(1)} %gate.1.gated_ref, bf16[4,512,512]{2,1,0:T(8,128)(2,1)S(1)} %copy-done), custom_call_target="tpu_custom_call" | custom-call | flops 1073741824 | bytes 2097152 | tf_op jit(solution)/shard_map/own_part/pallas_call | solution.py:240
  59.6 0.6 collective-permute-done.other_ref
  60.3 0.4 project.3
  60.7 3.1 %collective-permute-start.6 = (bf16[256,512]{1,0:T(8,128)(2,1)S(1)}, bf16[256,512]{1,0:T(8,128)(2,1)S(1)}, u32[]{:S(2)}, u32[]{:S(2)}) collective-permute-start(bf16[256,512]{1,0:T(8,128)(2,1)S(1)} %get-tuple-element.28), channel_id=1, source_target_pairs={{0,6},{1,7},{2,0},{3,1},{4,2},{5,3},{6,4},{7,5},{8,14},{9,15},{10,... | collective-permute-start | bytes 786440 | tf_op jit(solution)/shard_map/ppermute | solution.py:326
  63.8 1.0 %project.2 = (bf16[256,512]{1,0:T(8,128)(2,1)S(1)}, bf16[256,512]{1,0:T(8,128)(2,1)S(1)}, bf16[256,512]{1,0:T(8,128)(2,1)S(1)}, bf16[256,512]{1,0:T(8,128)(2,1)S...) custom-call(f32[4,512,512]{2,1,0:T(8,128)S(1)} %own_part.1.part_ref, ...), custom_call_target="tpu_custom_call" | custom-call | flops 805306368 | bytes 3145728 | tf_op jit(solution)/shard_map/project/pallas_call | solution.py:265
  64.8 3.3 %collective-permute-start.2 = (bf16[256,512]{1,0:T(8,128)(2,1)S(1)}, bf16[256,512]{1,0:T(8,128)(2,1)S(1)}, u32[]{:S(2)}, u32[]{:S(2)}) collective-permute-start(bf16[256,512]{1,0:T(8,128)(2,1)S(1)} %get-tuple-element.22), channel_id=1, source_target_pairs={{0,6},{1,7},{2,0},{3,1},{4,2},{5,3},{6,4},{7,5},{8,14},{9,15},{10,... | collective-permute-start | bytes 786440 | tf_op jit(solution)/shard_map/ppermute | solution.py:326
  68.1 2.4 %collective-permute-done.6 = bf16[256,512]{1,0:T(8,128)(2,1)S(1)} collective-permute-done((bf16[256,512]{1,0:T(8,128)(2,1)S(1)}, bf16[256,512]{1,0:T(8,128)(2,1)S(1)}, u32[]{:S(2)}, u32[]{:S(2)}) %collective-permute-start.6) | collective-permute-done | bytes 262176 | tf_op jit(solution)/shard_map/ppermute | solution.py:326
  70.5 3.8 %collective-permute-start.7 = (bf16[256,512]{1,0:T(8,128)(2,1)S(1)}, bf16[256,512]{1,0:T(8,128)(2,1)S(1)}, u32[]{:S(2)}, u32[]{:S(2)}) collective-permute-start(bf16[256,512]{1,0:T(8,128)(2,1)S(1)} %add_convert_fusion), channel_id=1, source_target_pairs={{0,6},{1,7},{2,0},{3,1},{4,2},{5,3},{6,4},{7,5},{8,14},{9,15},{10,... | collective-permute-start | bytes 786440 | tf_op jit(solution)/shard_map/ppermute | solution.py:326
  74.5 1.6 %collective-permute-done.2.refs_1_ = bf16[256,512]{1,0:T(8,128)(2,1)S(1)} collective-permute-done((bf16[256,512]{1,0:T(8,128)(2,1)S(1)}, bf16[256,512]{1,0:T(8,128)(2,1)S(1)}, u32[]{:S(2)}, u32[]{:S(2)}) %collective-permute-start.2) | collective-permute-done | bytes 262176 | tf_op jit(solution)/shard_map/ppermute | solution.py:326
  76.1 3.7 %collective-permute-done.5.refs_4_ = bf16[256,512]{1,0:T(8,128)(2,1)S(1)} collective-permute-done((bf16[256,512]{1,0:T(8,128)(2,1)S(1)}, bf16[256,512]{1,0:T(8,128)(2,1)S(1)}, u32[]{:S(2)}, u32[]{:S(2)}) %collective-permute-start.5) | collective-permute-done | bytes 262176 | tf_op jit(solution)/shard_map/ppermute | solution.py:326
  79.8 1.1 %collective-permute-done.7.refs_5_ = bf16[256,512]{1,0:T(8,128)(2,1)S(1)} collective-permute-done((bf16[256,512]{1,0:T(8,128)(2,1)S(1)}, bf16[256,512]{1,0:T(8,128)(2,1)S(1)}, u32[]{:S(2)}, u32[]{:S(2)}) %collective-permute-start.7) | collective-permute-done | bytes 262176 | tf_op jit(solution)/shard_map/ppermute | solution.py:326
  80.9 3.4 %collective-permute-done.4.refs_2_ = bf16[256,512]{1,0:T(8,128)(2,1)S(1)} collective-permute-done((bf16[256,512]{1,0:T(8,128)(2,1)S(1)}, bf16[256,512]{1,0:T(8,128)(2,1)S(1)}, u32[]{:S(2)}, u32[]{:S(2)}) %collective-permute-start.4) | collective-permute-done | bytes 262176 | tf_op jit(solution)/shard_map/ppermute | solution.py:326
  84.3 0.9 %finish.1 = bf16[512,512]{1,0:T(8,128)(2,1)} custom-call(bf16[256,512]{1,0:T(8,128)(2,1)S(1)} %get-tuple-element.21.refs_0_, bf16[256,512]{1,0:T(8,128)(2,1)S(1)} %collective-permute-done.2.refs_1_, bf16[256,512]{1,0:T(8,128)(2,1)S(1)} %collective-permute-done.4.refs_2_, bf16[256,512]{1,0:T(8,128)(2,1)S(1)} %get-tuple-element.25.refs_3_, ...), custom_call_target="tpu_custom_call" | custom-call | flops 786432 | bytes 2097152 | tf_op jit(solution)/shard_map/finish/pallas_call | solution.py:298
  (18 shorter events, 0.4 us)
Async XLA Ops:
  2.4 28.9 %all-to-all-start = ((bf16[32,16,512]{2,1,0:T(8,128)(2,1)}), bf16[32,16,512]{2,1,0:T(8,128)(2,1)}, u32[]{:S(2)}, u32[]{:S(2)}) async-start(bf16[32,16,512]{2,1,0:T(8,128)(2,1)} %bitcast.18), calls=%async_computation | async-start | bytes 1048576 | tf_op jit(solution)/shard_map/all_to_all | solution.py:336
  19.3 40.4 %collective-permute-start.1 = (bf16[4,512,512]{2,1,0:T(8,128)(2,1)}, bf16[4,512,512]{2,1,0:T(8,128)(2,1)S(1)}, u32[]{:S(2)}, u32[]{:S(2)}) collective-permute-start(bf16[4,512,512]{2,1,0:T(8,128)(2,1)} %get-tuple-element.20), channel_id=1, source_target_pairs={{0,1},{1,0},{2,3},{3,2},{4,5},{5,4},{6,7},{7,6},{8,9},{9,8},{10,11... | collective-permute-start | bytes 6291464 | tf_op jit(solution)/shard_map/ppermute | solution.py:326
  20.0 38.0 %copy-start.4 = (f32[512]{0:T(512)S(1)}, f32[512]{0:T(512)}, u32[]{:S(2)}) copy-start(f32[512]{0:T(512)} %param.11) | copy-start | bytes 6148
  23.7 34.3 %copy-start.1 = (bf16[512,512]{1,0:T(8,128)(2,1)S(1)}, bf16[512,512]{1,0:T(8,128)(2,1)}, u32[]{:S(2)}) copy-start(bf16[512,512]{1,0:T(8,128)(2,1)} %query_ref.1) | copy-start | bytes 1572868
  23.7 34.3 %copy-start.2 = (bf16[512,512]{1,0:T(8,128)(2,1)S(1)}, bf16[512,512]{1,0:T(8,128)(2,1)}, u32[]{:S(2)}) copy-start(bf16[512,512]{1,0:T(8,128)(2,1)} %get-tuple-element.18.mixed_ref) | copy-start | bytes 1572868
  31.3 27.0 %copy-start = (bf16[4,512,512]{2,1,0:T(8,128)(2,1)S(1)}, bf16[4,512,512]{2,1,0:T(8,128)(2,1)}, u32[]{:S(2)}) copy-start(bf16[4,512,512]{2,1,0:T(8,128)(2,1)} %get-tuple-element.19.weight_ref) | copy-start | bytes 6291460
  31.3 1.1 %copy-start.3 = (bf16[128,512]{1,0:T(8,128)(2,1)S(1)}, bf16[128,512]{1,0:T(8,128)(2,1)}, u32[]{:S(2)}) copy-start(bf16[128,512]{1,0:T(8,128)(2,1)} %turned_taps.1.taps_ref) | copy-start | bytes 393220
  58.3 2.0 %collective-permute-start = (bf16[512,512]{1,0:T(8,128)(2,1)S(1)}, bf16[512,512]{1,0:T(8,128)(2,1)S(1)}, u32[]{:S(2)}, u32[]{:S(2)}) collective-permute-start(bf16[512,512]{1,0:T(8,128)(2,1)S(1)} %gate.1.gated_ref), channel_id=1, source_target_pairs={{0,1},{1,0},{2,3},{3,2},{4,5},{5,4},{6,7},{7,6},{8,9},{9,8},{10,11... | collective-permute-start | bytes 1572872 | tf_op jit(solution)/shard_map/ppermute | solution.py:326
  60.7 9.8 %collective-permute-start.6 = (bf16[256,512]{1,0:T(8,128)(2,1)S(1)}, bf16[256,512]{1,0:T(8,128)(2,1)S(1)}, u32[]{:S(2)}, u32[]{:S(2)}) collective-permute-start(bf16[256,512]{1,0:T(8,128)(2,1)S(1)} %get-tuple-element.28), channel_id=1, source_target_pairs={{0,6},{1,7},{2,0},{3,1},{4,2},{5,3},{6,4},{7,5},{8,14},{9,15},{10,... | collective-permute-start | bytes 786440 | tf_op jit(solution)/shard_map/ppermute | solution.py:326
  63.8 10.5 %collective-permute-start.3 = (bf16[256,512]{1,0:T(8,128)(2,1)S(1)}, bf16[256,512]{1,0:T(8,128)(2,1)S(1)}, u32[]{:S(2)}, u32[]{:S(2)}) collective-permute-start(bf16[256,512]{1,0:T(8,128)(2,1)S(1)} %get-tuple-element.24), channel_id=1, source_target_pairs={{0,2},{1,3},{2,4},{3,5},{4,6},{5,7},{6,0},{7,1},{8,10},{9,11},{10,... | collective-permute-start | bytes 786440 | tf_op jit(solution)/shard_map/ppermute | solution.py:326
  64.8 11.3 %collective-permute-start.2 = (bf16[256,512]{1,0:T(8,128)(2,1)S(1)}, bf16[256,512]{1,0:T(8,128)(2,1)S(1)}, u32[]{:S(2)}, u32[]{:S(2)}) collective-permute-start(bf16[256,512]{1,0:T(8,128)(2,1)S(1)} %get-tuple-element.22), channel_id=1, source_target_pairs={{0,6},{1,7},{2,0},{3,1},{4,2},{5,3},{6,4},{7,5},{8,14},{9,15},{10,... | collective-permute-start | bytes 786440 | tf_op jit(solution)/shard_map/ppermute | solution.py:326
  68.1 11.7 %collective-permute-start.5 = (bf16[256,512]{1,0:T(8,128)(2,1)S(1)}, bf16[256,512]{1,0:T(8,128)(2,1)S(1)}, u32[]{:S(2)}, u32[]{:S(2)}) collective-permute-start(bf16[256,512]{1,0:T(8,128)(2,1)S(1)} %get-tuple-element.26), channel_id=1, source_target_pairs={{0,2},{1,3},{2,4},{3,5},{4,6},{5,7},{6,0},{7,1},{8,10},{9,11},{10,... | collective-permute-start | bytes 786440 | tf_op jit(solution)/shard_map/ppermute | solution.py:326
  70.5 10.3 %collective-permute-start.7 = (bf16[256,512]{1,0:T(8,128)(2,1)S(1)}, bf16[256,512]{1,0:T(8,128)(2,1)S(1)}, u32[]{:S(2)}, u32[]{:S(2)}) collective-permute-start(bf16[256,512]{1,0:T(8,128)(2,1)S(1)} %add_convert_fusion), channel_id=1, source_target_pairs={{0,6},{1,7},{2,0},{3,1},{4,2},{5,3},{6,4},{7,5},{8,14},{9,15},{10,... | collective-permute-start | bytes 786440 | tf_op jit(solution)/shard_map/ppermute | solution.py:326
  74.4 9.9 %collective-permute-start.4 = (bf16[256,512]{1,0:T(8,128)(2,1)S(1)}, bf16[256,512]{1,0:T(8,128)(2,1)S(1)}, u32[]{:S(2)}, u32[]{:S(2)}) collective-permute-start(bf16[256,512]{1,0:T(8,128)(2,1)S(1)} %add_convert_fusion.1), channel_id=1, source_target_pairs={{0,2},{1,3},{2,4},{3,5},{4,6},{5,7},{6,0},{7,1},{8,10},{9,11},{10,... | collective-permute-start | bytes 786440 | tf_op jit(solution)/shard_map/ppermute | solution.py:326

commit v7 on v6

--- a/solution.py
+++ b/solution.py
@@ -11,7 +11,7 @@
 WIN = 8
 LANES = 128
 CORES = 2
-CONV_BYTES = 53 << 20
+CONV_BYTES = 54400 << 10
 PARAMS = pltpu.CompilerParams(vmem_limit_bytes=20 << 20)
 
 
@@ -65,7 +65,7 @@
     )(key_gate, value_in)
 
 
-def taps_kernel(few, place_ref, taps_ref, out_ref, taps, sems):
+def taps_kernel(few, place_ref, taps_ref, out_ref, taps, out, sems):
     length = out_ref.shape[1]
     column = pl.multiple_of(place_ref[0] * LANES, LANES)
 
@@ -87,7 +87,10 @@
             (((1,), (1,)), ((), ())),
             preferred_element_type=jnp.float32,
         )
-        out_ref[k * few : (k + 1) * few, :] = picked.astype(jnp.bfloat16)
+        out[k * few : (k + 1) * few, :] = picked.astype(jnp.bfloat16)
+    put = pltpu.make_async_copy(out, out_ref.at[pl.ds(0, WIN * few)], sems.at[WIN])
+    put.start()
+    put.wait()
 
 
 def turned_taps(place, filter_taps, few):
@@ -97,10 +100,14 @@
         grid_spec=pltpu.PrefetchScalarGridSpec(
             num_scalar_prefetch=1,
             in_specs=[pl.BlockSpec(memory_space=pl.ANY)],
-            out_specs=pl.BlockSpec(memory_space=pltpu.VMEM),
-            scratch_shapes=[pltpu.VMEM((WIN * length, LANES), jnp.float32), pltpu.SemaphoreType.DMA((WIN,))],
-        ),
-        out_shape=jax.ShapeDtypeStruct((WIN * few, length), jnp.bfloat16),
+            out_specs=pl.BlockSpec(memory_space=pl.ANY),
+            scratch_shapes=[
+                pltpu.VMEM((WIN * length, LANES), jnp.float32),
+                pltpu.VMEM((WIN * few, length), jnp.bfloat16),
+                pltpu.SemaphoreType.DMA((WIN + 1,)),
+            ],
+        ),
+        out_shape=jax.ShapeDtypeStruct((length, length), jnp.bfloat16),
         cost_estimate=pl.CostEstimate(
             flops=2 * few * LANES * WIN * length, bytes_accessed=2 << 20, transcendentals=0
         ),
@@ -108,14 +115,23 @@
     )(place, filter_taps)
 
 
-def conv_kernel(few, x_ref, taps_ref, table_ref, out_ref, window, product):
+def conv_kernel(few, x_ref, taps_ref, table_ref, out_ref, rows, tap_rows, table, window, product, sems):
     tiles, length, pair = table_ref.shape
     count = x_ref.shape[0]
     spans = count // few
 
+    copies = [
+        pltpu.make_async_copy(x_ref, rows, sems.at[0]),
+        pltpu.make_async_copy(taps_ref.at[pl.ds(0, WIN * few)], tap_rows, sems.at[1]),
+        pltpu.make_async_copy(table_ref, table, sems.at[2]),
+    ]
+    for copy in copies:
+        copy.start()
+    for copy in copies:
+        copy.wait()
     for tile in range(tiles):
-        spectrum = jnp.dot(x_ref[...], table_ref[tile], preferred_element_type=jnp.float32)
-        taps = jnp.dot(taps_ref[...], table_ref[tile], preferred_element_type=jnp.float32)
+        spectrum = jnp.dot(rows[...], table[tile], preferred_element_type=jnp.float32)
+        taps = jnp.dot(tap_rows[...], table[tile], preferred_element_type=jnp.float32)
         sign = 1.0 if tile < tiles // 2 else -1.0
         for span in range(spans):
             now = slice(span * few, (span + 1) * few)
@@ -153,7 +169,7 @@
     total = None
     for tile in range(tiles):
         term = lax.dot_general(
-            product[tile], table_ref[tile], (((1,), (1,)), ((), ())), preferred_element_type=jnp.float32
+            product[tile], table[tile], (((1,), (1,)), ((), ())), preferred_element_type=jnp.float32
         )
         total = term if total is None else total + term
     out_ref[...] = total.astype(jnp.bfloat16)
@@ -164,12 +180,16 @@
     tiles, _, pair = table.shape
     return pl.pallas_call(
         functools.partial(conv_kernel, few),
-        in_specs=[pl.BlockSpec(memory_space=pltpu.VMEM)] * 3,
+        in_specs=[pl.BlockSpec(memory_space=pl.ANY)] * 3,
         out_specs=pl.BlockSpec(memory_space=pltpu.VMEM),
         out_shape=jax.ShapeDtypeStruct((count, length), jnp.bfloat16),
         scratch_shapes=[
+            pltpu.VMEM((count, length), jnp.bfloat16),
+            pltpu.VMEM((WIN * few, length), jnp.bfloat16),
+            pltpu.VMEM(table.shape, jnp.bfloat16),
             pltpu.VMEM((tiles, 3, count, LANES), jnp.float32),
             pltpu.VMEM((tiles, count, pair), jnp.bfloat16),
+            pltpu.SemaphoreType.DMA((3,)),
         ],
         compiler_params=pltpu.CompilerParams(vmem_limit_bytes=CONV_BYTES),
         cost_estimate=pl.CostEstimate(
@@ -340,10 +360,11 @@
     gated = gate(conv_turned, mixed, query_gate, skip_gain)
     other = ch_shift(gated, 0, 1)
     part = own_part(gated, own_weight)
-    across_low, across_high = project((0,), part, other, other_weight)
+    across_low, across_high, up_low, up_high, down_low, down_high, own_low, own_high = project(
+        (0, 1, 2, 3), part, other, other_weight
+    )
     got_low = ch_shift(across_low, 1, 0)
     got_high = ch_shift(across_high, -1, 0)
-    up_low, up_high, down_low, down_high, own_low, own_high = project((1, 2, 3), part, other, other_weight)
     from_below_high = ch_shift(up_high, 1, 0)
     from_above_low = ch_shift(down_low, -1, 0)
     from_below_low = ch_shift(added(up_low, got_low), 1, 0)

time: 85.5 us -> 85.4 us (level)
  waiting for transfers between devices: 20.4 us -> 21.5 us
  local copies, waits for them, and re-layouts: 1.73 us -> 0.69 us
    ppermute x8, waiting for transfers between devices: 12.8 us -> 13.9 us  [ch_shift(): return lax.ppermute(block, 'ch', route)]
    unnamed x10 -> x8, local copies, waits for them, and re-layouts: 1.07 us -> 0.02 us
  transfers between devices with their start and end apart: 9 -> 9, of which waited for: 7 -> 7; matrix products, arithmetic and copies ran while one was open for 2% -> 2% of each run, Pallas kernels for 18% -> 17%
where the time goes in v7:
time: 85.4 us; the launch traced here: 85.1 us
  starting transfers between devices  21.6 us (25%)
  blocking collectives  21.6 us (25%)
  waiting for transfers between devices  21.5 us (25%)
  Pallas kernels  18.7 us (22%)
    all_to_all x1, blocking collectives, body(): lax.all_to_all(conv_rows.reshape(ctx, few, length), 'ctx', 0, 0)  21.6 us
    ppermute x8, waiting for transfers between devices, ch_shift(): return lax.ppermute(block, 'ch', route)  13.9 us
    all_to_all x1, starting transfers between devices, body(): long_rows = lax.all_to_all(turned.reshape(ctx, few, length), 'ctx', 0, 0)  11.3 us
    ppermute x8, starting transfers between devices, ch_shift(): return lax.ppermute(block, 'ch', route)  10.4 us
    all_to_all x1, waiting for transfers between devices, body(): long_rows = lax.all_to_all(turned.reshape(ctx, few, length), 'ctx', 0, 0)  7.64 us
    pallas_call x1, Pallas kernels, weight_blocks(): pl.pallas_call(functools.partial(weights_kernel, number), grid_spec=pltpu...  4.88 us
    pallas_call x1, Pallas kernels, convolve(): pl.pallas_call(functools.partial(conv_kernel, few), in_specs=[pl.BlockSpe...  4.2 us
    pallas_call x1, Pallas kernels, turned_taps(): pl.pallas_call(functools.partial(taps_kernel, few), grid_spec=pltpu.Prefe...  3.61 us
  transfers between devices with their start and end apart: 9, of which 7 were waited for; matrix products, arithmetic and copies ran while one was open for 2% of the time, Pallas kernels for 17%

profile of v7, /device:TPU:32, one launch (start us, length us, event | category | flops | bytes accessed | tf_op | source)
XLA Modules:
  0.0 85.1 jit_solution(8541527423179773492)
XLA Ops:
  0.0 2.4 %mix.1 = (bf16[512,512]{1,0:T(8,128)(2,1)}, bf16[512,512]{1,0:T(8,128)(2,1)}) custom-call(bf16[512,512]{1,0:T(8,128)(2,1)} %key_ref.1, bf16[512,512]{1,0:T(8,128)(2,1)} %value_ref.1), custom_call_target="tpu_custom_call" | custom-call | flops 262144 | bytes 2097152 | tf_op jit(solution)/shard_map/mix/pallas_call | solution.py:54
  2.4 11.3 %all-to-all-start = ((bf16[32,16,512]{2,1,0:T(8,128)(2,1)}), bf16[32,16,512]{2,1,0:T(8,128)(2,1)}, u32[]{:S(2)}, u32[]{:S(2)}) async-start(bf16[32,16,512]{2,1,0:T(8,128)(2,1)} %bitcast.18), calls=%async_computation | async-start | bytes 1048576 | tf_op jit(solution)/shard_map/all_to_all | solution.py:356
  13.7 0.7 stack.47.blocks_ref
  14.4 4.9 %weight_blocks.1 = (bf16[4,512,512]{2,1,0:T(8,128)(2,1)}, bf16[4,512,512]{2,1,0:T(8,128)(2,1)}) custom-call(s32[8]{0:T(128)} %stack.47.blocks_ref, bf16[512,4096]{1,0:T(8,128)(2,1)} %weight_ref.1), custom_call_target="tpu_custom_call" | custom-call | bytes 8388608 | tf_op jit(solution)/shard_map/weight_blocks/pallas_call | solution.py:238
  19.3 0.1 collective-permute-start.1
  19.4 0.6 pad_add_fusion.place_ref
  20.0 3.6 %turned_taps.1.taps_ref = bf16[512,512]{1,0:T(8,128)(2,1)} custom-call(s32[2]{0:T(128)} %pad_add_fusion.place_ref, f32[4096,512]{1,0:T(8,128)} %taps_ref.1), custom_call_target="tpu_custom_call" | custom-call | flops 16777216 | bytes 2097152 | tf_op jit(solution)/shard_map/turned_taps/pallas_call | solution.py:98
  23.7 7.6 %all-to-all-done = bf16[32,16,512]{2,1,0:T(8,128)(2,1)} async-done(((bf16[32,16,512]{2,1,0:T(8,128)(2,1)}), bf16[32,16,512]{2,1,0:T(8,128)(2,1)}, u32[]{:S(2)}, u32[]{:S(2)}) %all-to-all-start) | async-done | bytes 524320 | tf_op jit(solution)/shard_map/all_to_all | solution.py:356
  31.3 4.2 %convolve.1 = bf16[512,512]{1,0:T(8,128)(2,1)S(1)} custom-call(bf16[512,512]{1,0:T(8,128)(2,1)} %bitcast.1.x_ref, bf16[512,512]{1,0:T(8,128)(2,1)} %turned_taps.1.taps_ref, bf16[4,512,256]{2,1,0:T(8,128)(2,1)} %constant.77.clone.table_ref), custom_call_target="tpu_custom_call" | custom-call | flops 1073741824 | bytes 3145728 | tf_op jit(solution)/shard_map/convolve/pallas_call | solution.py:181
  35.5 21.6 %all_to_all.10 = bf16[32,16,512]{2,1,0:T(8,128)(2,1)S(1)} all-to-all(bf16[32,16,512]{2,1,0:T(8,128)(2,1)S(1)} %bitcast.16), channel_id=1, replica_groups=mesh['ctx'=32,'ch'=8] {'ctx'}, dimensions={0} | all-to-all | bytes 1048576 | tf_op jit(solution)/shard_map/all_to_all | solution.py:358
  57.1 0.3 gate.1.gated_ref
  57.4 0.1 collective-permute-start
  57.5 1.3 %own_part.1.part_ref = f32[4,512,512]{2,1,0:T(8,128)S(1)} custom-call(bf16[512,512]{1,0:T(8,128)(2,1)S(1)} %gate.1.gated_ref, bf16[4,512,512]{2,1,0:T(8,128)(2,1)S(1)} %copy-done), custom_call_target="tpu_custom_call" | custom-call | flops 1073741824 | bytes 2097152 | tf_op jit(solution)/shard_map/own_part/pallas_call | solution.py:260
  58.8 0.6 collective-permute-done.other_ref
  59.4 1.3 %project.1 = (bf16[256,512]{1,0:T(8,128)(2,1)S(1)}, bf16[256,512]{1,0:T(8,128)(2,1)S(1)}, bf16[256,512]{1,0:T(8,128)(2,1)S(1)}, bf16[256,512]{1,0:T(8,128)(2,1)S...) custom-call(f32[4,512,512]{2,1,0:T(8,128)S(1)} %own_part.1.part_ref,, ...), custom_call_target="tpu_custom_call" | custom-call | flops 1073741824 | bytes 4194304 | tf_op jit(solution)/shard_map/project/pallas_call | solution.py:285
  60.6 3.1 %collective-permute-start.6 = (bf16[256,512]{1,0:T(8,128)(2,1)S(1)}, bf16[256,512]{1,0:T(8,128)(2,1)S(1)}, u32[]{:S(2)}, u32[]{:S(2)}) collective-permute-start(bf16[256,512]{1,0:T(8,128)(2,1)S(1)} %get-tuple-element.28), channel_id=1, source_target_pairs={{0,6},{1,7},{2,0},{3,1},{4,2},{5,3},{6,4},{7,5},{8,14},{9,15},{10,... | collective-permute-start | bytes 786440 | tf_op jit(solution)/shard_map/ppermute | solution.py:346
  63.7 3.2 %collective-permute-start.2 = (bf16[256,512]{1,0:T(8,128)(2,1)S(1)}, bf16[256,512]{1,0:T(8,128)(2,1)S(1)}, u32[]{:S(2)}, u32[]{:S(2)}) collective-permute-start(bf16[256,512]{1,0:T(8,128)(2,1)S(1)} %get-tuple-element.22), channel_id=1, source_target_pairs={{0,6},{1,7},{2,0},{3,1},{4,2},{5,3},{6,4},{7,5},{8,14},{9,15},{10,... | collective-permute-start | bytes 786440 | tf_op jit(solution)/shard_map/ppermute | solution.py:346
  67.0 3.5 %collective-permute-done.6 = bf16[256,512]{1,0:T(8,128)(2,1)S(1)} collective-permute-done((bf16[256,512]{1,0:T(8,128)(2,1)S(1)}, bf16[256,512]{1,0:T(8,128)(2,1)S(1)}, u32[]{:S(2)}, u32[]{:S(2)}) %collective-permute-start.6) | collective-permute-done | bytes 262176 | tf_op jit(solution)/shard_map/ppermute | solution.py:346
  70.5 3.8 %collective-permute-start.7 = (bf16[256,512]{1,0:T(8,128)(2,1)S(1)}, bf16[256,512]{1,0:T(8,128)(2,1)S(1)}, u32[]{:S(2)}, u32[]{:S(2)}) collective-permute-start(bf16[256,512]{1,0:T(8,128)(2,1)S(1)} %add_convert_fusion), channel_id=1, source_target_pairs={{0,6},{1,7},{2,0},{3,1},{4,2},{5,3},{6,4},{7,5},{8,14},{9,15},{10,... | collective-permute-start | bytes 786440 | tf_op jit(solution)/shard_map/ppermute | solution.py:346
  74.4 1.6 %collective-permute-done.2.refs_1_ = bf16[256,512]{1,0:T(8,128)(2,1)S(1)} collective-permute-done((bf16[256,512]{1,0:T(8,128)(2,1)S(1)}, bf16[256,512]{1,0:T(8,128)(2,1)S(1)}, u32[]{:S(2)}, u32[]{:S(2)}) %collective-permute-start.2) | collective-permute-done | bytes 262176 | tf_op jit(solution)/shard_map/ppermute | solution.py:346
  76.0 3.7 %collective-permute-done.5.refs_4_ = bf16[256,512]{1,0:T(8,128)(2,1)S(1)} collective-permute-done((bf16[256,512]{1,0:T(8,128)(2,1)S(1)}, bf16[256,512]{1,0:T(8,128)(2,1)S(1)}, u32[]{:S(2)}, u32[]{:S(2)}) %collective-permute-start.5) | collective-permute-done | bytes 262176 | tf_op jit(solution)/shard_map/ppermute | solution.py:346
  79.7 1.1 %collective-permute-done.7.refs_5_ = bf16[256,512]{1,0:T(8,128)(2,1)S(1)} collective-permute-done((bf16[256,512]{1,0:T(8,128)(2,1)S(1)}, bf16[256,512]{1,0:T(8,128)(2,1)S(1)}, u32[]{:S(2)}, u32[]{:S(2)}) %collective-permute-start.7) | collective-permute-done | bytes 262176 | tf_op jit(solution)/shard_map/ppermute | solution.py:346
  80.8 3.4 %collective-permute-done.4.refs_2_ = bf16[256,512]{1,0:T(8,128)(2,1)S(1)} collective-permute-done((bf16[256,512]{1,0:T(8,128)(2,1)S(1)}, bf16[256,512]{1,0:T(8,128)(2,1)S(1)}, u32[]{:S(2)}, u32[]{:S(2)}) %collective-permute-start.4) | collective-permute-done | bytes 262176 | tf_op jit(solution)/shard_map/ppermute | solution.py:346
  84.2 0.9 %finish.1 = bf16[512,512]{1,0:T(8,128)(2,1)} custom-call(bf16[256,512]{1,0:T(8,128)(2,1)S(1)} %get-tuple-element.21.refs_0_, bf16[256,512]{1,0:T(8,128)(2,1)S(1)} %collective-permute-done.2.refs_1_, bf16[256,512]{1,0:T(8,128)(2,1)S(1)} %collective-permute-done.4.refs_2_, bf16[256,512]{1,0:T(8,128)(2,1)S(1)} %get-tuple-element.25.refs_3_, ...), custom_call_target="tpu_custom_call" | custom-call | flops 786432 | bytes 2097152 | tf_op jit(solution)/shard_map/finish/pallas_call | solution.py:318
  (15 shorter events, 0.2 us)
Async XLA Ops:
  2.4 28.9 %all-to-all-start = ((bf16[32,16,512]{2,1,0:T(8,128)(2,1)}), bf16[32,16,512]{2,1,0:T(8,128)(2,1)}, u32[]{:S(2)}, u32[]{:S(2)}) async-start(bf16[32,16,512]{2,1,0:T(8,128)(2,1)} %bitcast.18), calls=%async_computation | async-start | bytes 1048576 | tf_op jit(solution)/shard_map/all_to_all | solution.py:356
  19.3 39.5 %collective-permute-start.1 = (bf16[4,512,512]{2,1,0:T(8,128)(2,1)}, bf16[4,512,512]{2,1,0:T(8,128)(2,1)S(1)}, u32[]{:S(2)}, u32[]{:S(2)}) collective-permute-start(bf16[4,512,512]{2,1,0:T(8,128)(2,1)} %get-tuple-element.20), channel_id=1, source_target_pairs={{0,1},{1,0},{2,3},{3,2},{4,5},{5,4},{6,7},{7,6},{8,9},{9,8},{10,11... | collective-permute-start | bytes 6291464 | tf_op jit(solution)/shard_map/ppermute | solution.py:346
  23.6 33.5 %copy-start.1 = (bf16[512,512]{1,0:T(8,128)(2,1)S(1)}, bf16[512,512]{1,0:T(8,128)(2,1)}, u32[]{:S(2)}) copy-start(bf16[512,512]{1,0:T(8,128)(2,1)} %query_ref.1) | copy-start | bytes 1572868
  23.6 33.5 %copy-start.2 = (bf16[512,512]{1,0:T(8,128)(2,1)S(1)}, bf16[512,512]{1,0:T(8,128)(2,1)}, u32[]{:S(2)}) copy-start(bf16[512,512]{1,0:T(8,128)(2,1)} %get-tuple-element.18.mixed_ref) | copy-start | bytes 1572868
  23.7 33.5 %copy-start.3 = (f32[512]{0:T(512)S(1)}, f32[512]{0:T(512)}, u32[]{:S(2)}) copy-start(f32[512]{0:T(512)} %param.11) | copy-start | bytes 6148
  31.3 26.2 %copy-start = (bf16[4,512,512]{2,1,0:T(8,128)(2,1)S(1)}, bf16[4,512,512]{2,1,0:T(8,128)(2,1)}, u32[]{:S(2)}) copy-start(bf16[4,512,512]{2,1,0:T(8,128)(2,1)} %get-tuple-element.19.weight_ref) | copy-start | bytes 6291460
  57.4 2.0 %collective-permute-start = (bf16[512,512]{1,0:T(8,128)(2,1)S(1)}, bf16[512,512]{1,0:T(8,128)(2,1)S(1)}, u32[]{:S(2)}, u32[]{:S(2)}) collective-permute-start(bf16[512,512]{1,0:T(8,128)(2,1)S(1)} %gate.1.gated_ref), channel_id=1, source_target_pairs={{0,1},{1,0},{2,3},{3,2},{4,5},{5,4},{6,7},{7,6},{8,9},{9,8},{10,11... | collective-permute-start | bytes 1572872 | tf_op jit(solution)/shard_map/ppermute | solution.py:346
  60.6 9.8 %collective-permute-start.6 = (bf16[256,512]{1,0:T(8,128)(2,1)S(1)}, bf16[256,512]{1,0:T(8,128)(2,1)S(1)}, u32[]{:S(2)}, u32[]{:S(2)}) collective-permute-start(bf16[256,512]{1,0:T(8,128)(2,1)S(1)} %get-tuple-element.28), channel_id=1, source_target_pairs={{0,6},{1,7},{2,0},{3,1},{4,2},{5,3},{6,4},{7,5},{8,14},{9,15},{10,... | collective-permute-start | bytes 786440 | tf_op jit(solution)/shard_map/ppermute | solution.py:346
  63.7 10.5 %collective-permute-start.3 = (bf16[256,512]{1,0:T(8,128)(2,1)S(1)}, bf16[256,512]{1,0:T(8,128)(2,1)S(1)}, u32[]{:S(2)}, u32[]{:S(2)}) collective-permute-start(bf16[256,512]{1,0:T(8,128)(2,1)S(1)} %get-tuple-element.24), channel_id=1, source_target_pairs={{0,2},{1,3},{2,4},{3,5},{4,6},{5,7},{6,0},{7,1},{8,10},{9,11},{10,... | collective-permute-start | bytes 786440 | tf_op jit(solution)/shard_map/ppermute | solution.py:346
  63.7 12.3 %collective-permute-start.2 = (bf16[256,512]{1,0:T(8,128)(2,1)S(1)}, bf16[256,512]{1,0:T(8,128)(2,1)S(1)}, u32[]{:S(2)}, u32[]{:S(2)}) collective-permute-start(bf16[256,512]{1,0:T(8,128)(2,1)S(1)} %get-tuple-element.22), channel_id=1, source_target_pairs={{0,6},{1,7},{2,0},{3,1},{4,2},{5,3},{6,4},{7,5},{8,14},{9,15},{10,... | collective-permute-start | bytes 786440 | tf_op jit(solution)/shard_map/ppermute | solution.py:346
  67.0 12.8 %collective-permute-start.5 = (bf16[256,512]{1,0:T(8,128)(2,1)S(1)}, bf16[256,512]{1,0:T(8,128)(2,1)S(1)}, u32[]{:S(2)}, u32[]{:S(2)}) collective-permute-start(bf16[256,512]{1,0:T(8,128)(2,1)S(1)} %get-tuple-element.26), channel_id=1, source_target_pairs={{0,2},{1,3},{2,4},{3,5},{4,6},{5,7},{6,0},{7,1},{8,10},{9,11},{10,... | collective-permute-start | bytes 786440 | tf_op jit(solution)/shard_map/ppermute | solution.py:346
  70.5 10.3 %collective-permute-start.7 = (bf16[256,512]{1,0:T(8,128)(2,1)S(1)}, bf16[256,512]{1,0:T(8,128)(2,1)S(1)}, u32[]{:S(2)}, u32[]{:S(2)}) collective-permute-start(bf16[256,512]{1,0:T(8,128)(2,1)S(1)} %add_convert_fusion), channel_id=1, source_target_pairs={{0,6},{1,7},{2,0},{3,1},{4,2},{5,3},{6,4},{7,5},{8,14},{9,15},{10,... | collective-permute-start | bytes 786440 | tf_op jit(solution)/shard_map/ppermute | solution.py:346
  74.3 9.9 %collective-permute-start.4 = (bf16[256,512]{1,0:T(8,128)(2,1)S(1)}, bf16[256,512]{1,0:T(8,128)(2,1)S(1)}, u32[]{:S(2)}, u32[]{:S(2)}) collective-permute-start(bf16[256,512]{1,0:T(8,128)(2,1)S(1)} %add_convert_fusion.1), channel_id=1, source_target_pairs={{0,2},{1,3},{2,4},{3,5},{4,6},{5,7},{6,0},{7,1},{8,10},{9,11},{10,... | collective-permute-start | bytes 786440 | tf_op jit(solution)/shard_map/ppermute | solution.py:346

commit v8 on v7

--- a/solution.py
+++ b/solution.py
@@ -295,36 +295,39 @@
     )(part, other, other_weight)
 
 
-def finish_kernel(*refs):
-    out_ref, out, sems = refs[6:]
-    half = refs[0].shape[0]
+def finish_kernel(first, one_ref, two_ref, three_ref, *refs):
+    out_ref, out, sems = refs[-3:]
+    half = one_ref.shape[0]
     size = half // 2
+    base = 0 if first else half
 
     def put(k):
         part = pl.ds(k * size, size)
-        return pltpu.make_async_copy(out.at[part], out_ref.at[part], sems.at[k])
-
-    for k in range(4):
-        rows = slice(k % 2 * size, (k % 2 + 1) * size)
-        total = sum(ref[rows, :].astype(jnp.float32) for ref in refs[3 * (k // 2) : 3 * (k // 2) + 3])
-        out[k * size : (k + 1) * size, :] = total.astype(jnp.bfloat16)
+        return pltpu.make_async_copy(out.at[part], out_ref.at[pl.ds(base + k * size, size)], sems.at[k])
+
+    for k in range(2):
+        rows = slice(k * size, (k + 1) * size)
+        total = sum(ref[rows, :].astype(jnp.float32) for ref in (one_ref, two_ref, three_ref))
+        out[rows, :] = total.astype(jnp.bfloat16)
         put(k).start()
-    for k in range(4):
+    for k in range(2):
         put(k).wait()
 
 
-def finish(low, high):
-    half, width = low[0].shape
-    return pl.pallas_call(
-        finish_kernel,
-        in_specs=[pl.BlockSpec(memory_space=pltpu.VMEM)] * 6,
+def finish(terms, into=None):
+    half, width = terms[0].shape
+    first = into is None
+    return pl.pallas_call(
+        functools.partial(finish_kernel, first),
+        in_specs=[pl.BlockSpec(memory_space=pltpu.VMEM)] * 3 + [pl.BlockSpec(memory_space=pl.ANY)] * (not first),
         out_specs=pl.BlockSpec(memory_space=pl.ANY),
         out_shape=jax.ShapeDtypeStruct((2 * half, width), jnp.bfloat16),
-        scratch_shapes=[pltpu.VMEM((2 * half, width), jnp.bfloat16), pltpu.SemaphoreType.DMA((4,))],
+        scratch_shapes=[pltpu.VMEM((half, width), jnp.bfloat16), pltpu.SemaphoreType.DMA((2,))],
+        input_output_aliases={} if first else {3: 0},
         compiler_params=PARAMS,
-        cost_estimate=pl.CostEstimate(flops=6 * half * width, bytes_accessed=16 * half * width, transcendentals=0),
+        cost_estimate=pl.CostEstimate(flops=3 * half * width, bytes_accessed=8 * half * width, transcendentals=0),
         name="finish",
-    )(*low, *high)
+    )(*terms, *([] if first else [into]))
 
 
 def added(one, two):
@@ -360,16 +363,17 @@
     gated = gate(conv_turned, mixed, query_gate, skip_gain)
     other = ch_shift(gated, 0, 1)
     part = own_part(gated, own_weight)
-    across_low, across_high, up_low, up_high, down_low, down_high, own_low, own_high = project(
-        (0, 1, 2, 3), part, other, other_weight
-    )
+    across_low, across_high = project((0,), part, other, other_weight)
     got_low = ch_shift(across_low, 1, 0)
+    up_low, up_high, down_low, down_high, own_low, own_high = project((1, 2, 3), part, other, other_weight)
+    across_high, up_high = lax.optimization_barrier((across_high, up_high))
     got_high = ch_shift(across_high, -1, 0)
     from_below_high = ch_shift(up_high, 1, 0)
     from_above_low = ch_shift(down_low, -1, 0)
     from_below_low = ch_shift(added(up_low, got_low), 1, 0)
     from_above_high = ch_shift(added(down_high, got_high), -1, 0)
-    return finish((own_low, from_above_low, from_below_low), (own_high, from_below_high, from_above_high))
+    lower = finish((own_low, from_above_low, from_below_low))
+    return finish((own_high, from_below_high, from_above_high), lower)
 
 
 def solution(mesh):

time: 85.4 us -> 82.9 us (0.971)
  waiting for transfers between devices: 21.5 us -> 19.3 us
  starting transfers between devices: 21.6 us -> 20.6 us
    ppermute x8, waiting for transfers between devices: 13.9 us -> 11.6 us  [ch_shift(): return lax.ppermute(block, 'ch', route)]
    ppermute x8, starting transfers between devices: 10.4 us -> 9.35 us  [ch_shift(): return lax.ppermute(block, 'ch', route)]
  transfers between devices with their start and end apart: 9 -> 9, of which waited for: 7 -> 7; matrix products, arithmetic and copies ran while one was open for 2% -> 2% of each run, Pallas kernels for 17% -> 19%
where the time goes in v8:
time: 82.9 us; the launch traced here: 82.6 us
  blocking collectives  21.6 us (26%)
  starting transfers between devices  20.6 us (25%)
  Pallas kernels  19.5 us (24%)
  waiting for transfers between devices  19.3 us (23%)
    all_to_all x1, blocking collectives, body(): lax.all_to_all(conv_rows.reshape(ctx, few, length), 'ctx', 0, 0)  21.6 us
    ppermute x8, waiting for transfers between devices, ch_shift(): return lax.ppermute(block, 'ch', route)  11.6 us
    all_to_all x1, starting transfers between devices, body(): long_rows = lax.all_to_all(turned.reshape(ctx, few, length), 'ctx', 0, 0)  11.3 us
    ppermute x8, starting transfers between devices, ch_shift(): return lax.ppermute(block, 'ch', route)  9.35 us
    all_to_all x1, waiting for transfers between devices, body(): long_rows = lax.all_to_all(turned.reshape(ctx, few, length), 'ctx', 0, 0)  7.75 us
    pallas_call x1, Pallas kernels, weight_blocks(): pl.pallas_call(functools.partial(weights_kernel, number), grid_spec=pltpu...  4.87 us
    pallas_call x1, Pallas kernels, convolve(): pl.pallas_call(functools.partial(conv_kernel, few), in_specs=[pl.BlockSpe...  4.2 us
    pallas_call x1, Pallas kernels, turned_taps(): pl.pallas_call(functools.partial(taps_kernel, few), grid_spec=pltpu.Prefe...  3.6 us
  transfers between devices with their start and end apart: 9, of which 7 were waited for; matrix products, arithmetic and copies ran while one was open for 2% of the time, Pallas kernels for 19%

profile of v8, /device:TPU:32, one launch (start us, length us, event | category | flops | bytes accessed | tf_op | source)
XLA Modules:
  0.0 82.6 jit_solution(13981999755194531011)
XLA Ops:
  0.0 2.4 %mix.1 = (bf16[512,512]{1,0:T(8,128)(2,1)}, bf16[512,512]{1,0:T(8,128)(2,1)}) custom-call(bf16[512,512]{1,0:T(8,128)(2,1)} %key_ref.1, bf16[512,512]{1,0:T(8,128)(2,1)} %value_ref.1), custom_call_target="tpu_custom_call" | custom-call | flops 262144 | bytes 2097152 | tf_op jit(solution)/shard_map/mix/pallas_call | solution.py:54
  2.4 11.3 %all-to-all-start = ((bf16[32,16,512]{2,1,0:T(8,128)(2,1)}), bf16[32,16,512]{2,1,0:T(8,128)(2,1)}, u32[]{:S(2)}, u32[]{:S(2)}) async-start(bf16[32,16,512]{2,1,0:T(8,128)(2,1)} %bitcast.18), calls=%async_computation | async-start | bytes 1048576 | tf_op jit(solution)/shard_map/all_to_all | solution.py:359
  13.7 0.6 stack.47.blocks_ref
  14.4 4.9 %weight_blocks.1 = (bf16[4,512,512]{2,1,0:T(8,128)(2,1)}, bf16[4,512,512]{2,1,0:T(8,128)(2,1)}) custom-call(s32[8]{0:T(128)} %stack.47.blocks_ref, bf16[512,4096]{1,0:T(8,128)(2,1)} %weight_ref.1), custom_call_target="tpu_custom_call" | custom-call | bytes 8388608 | tf_op jit(solution)/shard_map/weight_blocks/pallas_call | solution.py:238
  19.4 0.6 pad_add_fusion.place_ref
  19.9 3.6 %turned_taps.1.taps_ref = bf16[512,512]{1,0:T(8,128)(2,1)} custom-call(s32[2]{0:T(128)} %pad_add_fusion.place_ref, f32[4096,512]{1,0:T(8,128)} %taps_ref.1), custom_call_target="tpu_custom_call" | custom-call | flops 16777216 | bytes 2097152 | tf_op jit(solution)/shard_map/turned_taps/pallas_call | solution.py:98
  23.6 7.7 %all-to-all-done = bf16[32,16,512]{2,1,0:T(8,128)(2,1)} async-done(((bf16[32,16,512]{2,1,0:T(8,128)(2,1)}), bf16[32,16,512]{2,1,0:T(8,128)(2,1)}, u32[]{:S(2)}, u32[]{:S(2)}) %all-to-all-start) | async-done | bytes 524320 | tf_op jit(solution)/shard_map/all_to_all | solution.py:359
  31.3 4.2 %convolve.1 = bf16[512,512]{1,0:T(8,128)(2,1)S(1)} custom-call(bf16[512,512]{1,0:T(8,128)(2,1)} %bitcast.1.x_ref, bf16[512,512]{1,0:T(8,128)(2,1)} %turned_taps.1.taps_ref, bf16[4,512,256]{2,1,0:T(8,128)(2,1)} %constant.77.clone.table_ref), custom_call_target="tpu_custom_call" | custom-call | flops 1073741824 | bytes 3145728 | tf_op jit(solution)/shard_map/convolve/pallas_call | solution.py:181
  35.5 21.6 %all_to_all.10 = bf16[32,16,512]{2,1,0:T(8,128)(2,1)S(1)} all-to-all(bf16[32,16,512]{2,1,0:T(8,128)(2,1)S(1)} %bitcast.16), channel_id=1, replica_groups=mesh['ctx'=32,'ch'=8] {'ctx'}, dimensions={0} | all-to-all | bytes 1048576 | tf_op jit(solution)/shard_map/all_to_all | solution.py:361
  57.5 1.3 %own_part.1.part_ref = f32[4,512,512]{2,1,0:T(8,128)S(1)} custom-call(bf16[512,512]{1,0:T(8,128)(2,1)S(1)} %gate.1.gated_ref, bf16[4,512,512]{2,1,0:T(8,128)(2,1)S(1)} %copy-done), custom_call_target="tpu_custom_call" | custom-call | flops 1073741824 | bytes 2097152 | tf_op jit(solution)/shard_map/own_part/pallas_call | solution.py:260
  58.8 0.6 collective-permute-done.other_ref
  59.4 0.4 project.3
  59.8 1.6 %collective-permute-start.6 = (bf16[256,512]{1,0:T(8,128)(2,1)S(1)}, bf16[256,512]{1,0:T(8,128)(2,1)S(1)}, u32[]{:S(2)}, u32[]{:S(2)}) collective-permute-start(bf16[256,512]{1,0:T(8,128)(2,1)S(1)} %get-tuple-element.32), channel_id=1, source_target_pairs={{0,2},{1,3},{2,4},{3,5},{4,6},{5,7},{6,0},{7,1},{8,10},{9,11},{10,... | collective-permute-start | bytes 786440 | tf_op jit(solution)/shard_map/ppermute | solution.py:349
  61.5 1.0 %project.2 = (bf16[256,512]{1,0:T(8,128)(2,1)S(1)}, bf16[256,512]{1,0:T(8,128)(2,1)S(1)}, bf16[256,512]{1,0:T(8,128)(2,1)S(1)}, bf16[256,512]{1,0:T(8,128)(2,1)S...) custom-call(f32[4,512,512]{2,1,0:T(8,128)S(1)} %own_part.1.part_ref, ...), custom_call_target="tpu_custom_call" | custom-call | flops 805306368 | bytes 3145728 | tf_op jit(solution)/shard_map/project/pallas_call | solution.py:285
  62.5 1.7 %collective-permute-start.3 = (bf16[256,512]{1,0:T(8,128)(2,1)S(1)}, bf16[256,512]{1,0:T(8,128)(2,1)S(1)}, u32[]{:S(2)}, u32[]{:S(2)}) collective-permute-start(bf16[256,512]{1,0:T(8,128)(2,1)S(1)} %get-tuple-element.28), channel_id=1, source_target_pairs={{0,6},{1,7},{2,0},{3,1},{4,2},{5,3},{6,4},{7,5},{8,14},{9,15},{10,... | collective-permute-start | bytes 786440 | tf_op jit(solution)/shard_map/ppermute | solution.py:349
  64.2 1.8 %collective-permute-start.5 = (bf16[256,512]{1,0:T(8,128)(2,1)S(1)}, bf16[256,512]{1,0:T(8,128)(2,1)S(1)}, u32[]{:S(2)}, u32[]{:S(2)}) collective-permute-start(bf16[256,512]{1,0:T(8,128)(2,1)S(1)} %get-tuple-element.30), channel_id=1, source_target_pairs={{0,6},{1,7},{2,0},{3,1},{4,2},{5,3},{6,4},{7,5},{8,14},{9,15},{10,... | collective-permute-start | bytes 786440 | tf_op jit(solution)/shard_map/ppermute | solution.py:349
  66.2 3.7 %collective-permute-done.6 = bf16[256,512]{1,0:T(8,128)(2,1)S(1)} collective-permute-done((bf16[256,512]{1,0:T(8,128)(2,1)S(1)}, bf16[256,512]{1,0:T(8,128)(2,1)S(1)}, u32[]{:S(2)}, u32[]{:S(2)}) %collective-permute-start.6) | collective-permute-done | bytes 262176 | tf_op jit(solution)/shard_map/ppermute | solution.py:349
  70.0 0.8 collective-permute-start.7
  70.8 0.9 %collective-permute-done.3 = bf16[256,512]{1,0:T(8,128)(2,1)S(1)} collective-permute-done((bf16[256,512]{1,0:T(8,128)(2,1)S(1)}, bf16[256,512]{1,0:T(8,128)(2,1)S(1)}, u32[]{:S(2)}, u32[]{:S(2)}) %collective-permute-start.3) | collective-permute-done | bytes 262176 | tf_op jit(solution)/shard_map/ppermute | solution.py:349
  71.8 3.0 %collective-permute-start.4 = (bf16[256,512]{1,0:T(8,128)(2,1)S(1)}, bf16[256,512]{1,0:T(8,128)(2,1)S(1)}, u32[]{:S(2)}, u32[]{:S(2)}) collective-permute-start(bf16[256,512]{1,0:T(8,128)(2,1)S(1)} %add_convert_fusion.1), channel_id=1, source_target_pairs={{0,6},{1,7},{2,0},{3,1},{4,2},{5,3},{6,4},{7,5},{8,14},{9,15},{10,... | collective-permute-start | bytes 786440 | tf_op jit(solution)/shard_map/ppermute | solution.py:349
  74.8 2.6 %collective-permute-done.5.two_ref = bf16[256,512]{1,0:T(8,128)(2,1)S(1)} collective-permute-done((bf16[256,512]{1,0:T(8,128)(2,1)S(1)}, bf16[256,512]{1,0:T(8,128)(2,1)S(1)}, u32[]{:S(2)}, u32[]{:S(2)}) %collective-permute-start.5) | collective-permute-done | bytes 262176 | tf_op jit(solution)/shard_map/ppermute | solution.py:349
  77.3 3.4 %collective-permute-done.7.three_ref = bf16[256,512]{1,0:T(8,128)(2,1)S(1)} collective-permute-done((bf16[256,512]{1,0:T(8,128)(2,1)S(1)}, bf16[256,512]{1,0:T(8,128)(2,1)S(1)}, u32[]{:S(2)}, u32[]{:S(2)}) %collective-permute-start.7) | collective-permute-done | bytes 262176 | tf_op jit(solution)/shard_map/ppermute | solution.py:349
  80.8 0.8 finish.2.refs_0_
  81.9 0.8 finish.3
  (17 shorter events, 1.1 us)
Async XLA Ops:
  2.4 28.9 %all-to-all-start = ((bf16[32,16,512]{2,1,0:T(8,128)(2,1)}), bf16[32,16,512]{2,1,0:T(8,128)(2,1)}, u32[]{:S(2)}, u32[]{:S(2)}) async-start(bf16[32,16,512]{2,1,0:T(8,128)(2,1)} %bitcast.18), calls=%async_computation | async-start | bytes 1048576 | tf_op jit(solution)/shard_map/all_to_all | solution.py:359
  19.2 39.5 %collective-permute-start.1 = (bf16[4,512,512]{2,1,0:T(8,128)(2,1)}, bf16[4,512,512]{2,1,0:T(8,128)(2,1)S(1)}, u32[]{:S(2)}, u32[]{:S(2)}) collective-permute-start(bf16[4,512,512]{2,1,0:T(8,128)(2,1)} %get-tuple-element.22), channel_id=1, source_target_pairs={{0,1},{1,0},{2,3},{3,2},{4,5},{5,4},{6,7},{7,6},{8,9},{9,8},{10,11... | collective-permute-start | bytes 6291464 | tf_op jit(solution)/shard_map/ppermute | solution.py:349
  23.5 33.6 %copy-start.1 = (bf16[512,512]{1,0:T(8,128)(2,1)S(1)}, bf16[512,512]{1,0:T(8,128)(2,1)}, u32[]{:S(2)}) copy-start(bf16[512,512]{1,0:T(8,128)(2,1)} %query_ref.1) | copy-start | bytes 1572868
  23.5 33.6 %copy-start.2 = (bf16[512,512]{1,0:T(8,128)(2,1)S(1)}, bf16[512,512]{1,0:T(8,128)(2,1)}, u32[]{:S(2)}) copy-start(bf16[512,512]{1,0:T(8,128)(2,1)} %get-tuple-element.20.mixed_ref) | copy-start | bytes 1572868
  23.6 33.6 %copy-start.3 = (f32[512]{0:T(512)S(1)}, f32[512]{0:T(512)}, u32[]{:S(2)}) copy-start(f32[512]{0:T(512)} %param.11) | copy-start | bytes 6148
  31.3 26.2 %copy-start = (bf16[4,512,512]{2,1,0:T(8,128)(2,1)S(1)}, bf16[4,512,512]{2,1,0:T(8,128)(2,1)}, u32[]{:S(2)}) copy-start(bf16[4,512,512]{2,1,0:T(8,128)(2,1)} %get-tuple-element.21.weight_ref) | copy-start | bytes 6291460
  57.4 2.0 %collective-permute-start = (bf16[512,512]{1,0:T(8,128)(2,1)S(1)}, bf16[512,512]{1,0:T(8,128)(2,1)S(1)}, u32[]{:S(2)}, u32[]{:S(2)}) collective-permute-start(bf16[512,512]{1,0:T(8,128)(2,1)S(1)} %gate.1.gated_ref), channel_id=1, source_target_pairs={{0,1},{1,0},{2,3},{3,2},{4,5},{5,4},{6,7},{7,6},{8,9},{9,8},{10,11... | collective-permute-start | bytes 1572872 | tf_op jit(solution)/shard_map/ppermute | solution.py:349
  59.8 10.1 %collective-permute-start.6 = (bf16[256,512]{1,0:T(8,128)(2,1)S(1)}, bf16[256,512]{1,0:T(8,128)(2,1)S(1)}, u32[]{:S(2)}, u32[]{:S(2)}) collective-permute-start(bf16[256,512]{1,0:T(8,128)(2,1)S(1)} %get-tuple-element.32), channel_id=1, source_target_pairs={{0,2},{1,3},{2,4},{3,5},{4,6},{5,7},{6,0},{7,1},{8,10},{9,11},{10,... | collective-permute-start | bytes 786440 | tf_op jit(solution)/shard_map/ppermute | solution.py:349
  62.5 9.3 %collective-permute-start.3 = (bf16[256,512]{1,0:T(8,128)(2,1)S(1)}, bf16[256,512]{1,0:T(8,128)(2,1)S(1)}, u32[]{:S(2)}, u32[]{:S(2)}) collective-permute-start(bf16[256,512]{1,0:T(8,128)(2,1)S(1)} %get-tuple-element.28), channel_id=1, source_target_pairs={{0,6},{1,7},{2,0},{3,1},{4,2},{5,3},{6,4},{7,5},{8,14},{9,15},{10,... | collective-permute-start | bytes 786440 | tf_op jit(solution)/shard_map/ppermute | solution.py:349
  64.2 13.1 %collective-permute-start.5 = (bf16[256,512]{1,0:T(8,128)(2,1)S(1)}, bf16[256,512]{1,0:T(8,128)(2,1)S(1)}, u32[]{:S(2)}, u32[]{:S(2)}) collective-permute-start(bf16[256,512]{1,0:T(8,128)(2,1)S(1)} %get-tuple-element.30), channel_id=1, source_target_pairs={{0,6},{1,7},{2,0},{3,1},{4,2},{5,3},{6,4},{7,5},{8,14},{9,15},{10,... | collective-permute-start | bytes 786440 | tf_op jit(solution)/shard_map/ppermute | solution.py:349
  66.0 15.5 %collective-permute-start.2 = (bf16[256,512]{1,0:T(8,128)(2,1)S(1)}, bf16[256,512]{1,0:T(8,128)(2,1)S(1)}, u32[]{:S(2)}, u32[]{:S(2)}) collective-permute-start(bf16[256,512]{1,0:T(8,128)(2,1)S(1)} %get-tuple-element.26), channel_id=1, source_target_pairs={{0,2},{1,3},{2,4},{3,5},{4,6},{5,7},{6,0},{7,1},{8,10},{9,11},{10,... | collective-permute-start | bytes 786440 | tf_op jit(solution)/shard_map/ppermute | solution.py:349
  70.0 10.7 %collective-permute-start.7 = (bf16[256,512]{1,0:T(8,128)(2,1)S(1)}, bf16[256,512]{1,0:T(8,128)(2,1)S(1)}, u32[]{:S(2)}, u32[]{:S(2)}) collective-permute-start(bf16[256,512]{1,0:T(8,128)(2,1)S(1)} %add_convert_fusion), channel_id=1, source_target_pairs={{0,2},{1,3},{2,4},{3,5},{4,6},{5,7},{6,0},{7,1},{8,10},{9,11},{10,... | collective-permute-start | bytes 786440 | tf_op jit(solution)/shard_map/ppermute | solution.py:349
  71.8 10.1 %collective-permute-start.4 = (bf16[256,512]{1,0:T(8,128)(2,1)S(1)}, bf16[256,512]{1,0:T(8,128)(2,1)S(1)}, u32[]{:S(2)}, u32[]{:S(2)}) collective-permute-start(bf16[256,512]{1,0:T(8,128)(2,1)S(1)} %add_convert_fusion.1), channel_id=1, source_target_pairs={{0,6},{1,7},{2,0},{3,1},{4,2},{5,3},{6,4},{7,5},{8,14},{9,15},{10,... | collective-permute-start | bytes 786440 | tf_op jit(solution)/shard_map/ppermute | solution.py:349

commit v9 on v8

--- a/solution.py
+++ b/solution.py
@@ -26,7 +26,7 @@
     return table.astype(jnp.bfloat16)
 
 
-def mix_kernel(chunks, key_ref, value_ref, mixed_ref, turned_ref, keys, values, sems):
+def mix_kernel(chunks, key_ref, value_ref, mixed_ref, turned_ref, keys, values, mixed, turned, sems):
     size = key_ref.shape[0] // chunks
 
     def fetch(k):
@@ -34,6 +34,13 @@
         return (
             pltpu.make_async_copy(key_ref.at[rows], keys.at[rows], sems.at[0, k]),
             pltpu.make_async_copy(value_ref.at[rows], values.at[rows], sems.at[1, k]),
+        )
+
+    def put(k):
+        rows = pl.ds(k * size, size)
+        return (
+            pltpu.make_async_copy(turned.at[:, rows], turned_ref.at[:, rows], sems.at[2, k]),
+            pltpu.make_async_copy(mixed.at[rows], mixed_ref.at[rows], sems.at[3, k]),
         )
 
     for k in range(chunks):
@@ -44,8 +51,13 @@
             copy.wait()
         rows = slice(k * size, (k + 1) * size)
         product = (keys[rows, :].astype(jnp.float32) * values[rows, :].astype(jnp.float32)).astype(jnp.bfloat16)
-        mixed_ref[rows, :] = product
-        turned_ref[:, rows] = product.T
+        mixed[rows, :] = product
+        turned[:, rows] = product.T
+        for copy in put(k):
+            copy.start()
+    for k in range(chunks):
+        for copy in put(k):
+            copy.wait()
 
 
 def mix(key_gate, value_in):
@@ -54,12 +66,13 @@
     return pl.pallas_call(
         functools.partial(mix_kernel, chunks),
         in_specs=[pl.BlockSpec(memory_space=pl.ANY)] * 2,
-        out_specs=[pl.BlockSpec(memory_space=pltpu.VMEM)] * 2,
+        out_specs=[pl.BlockSpec(memory_space=pl.ANY)] * 2,
         out_shape=[
             jax.ShapeDtypeStruct((length, width), jnp.bfloat16),
             jax.ShapeDtypeStruct((width, length), jnp.bfloat16),
         ],
-        scratch_shapes=[pltpu.VMEM((length, width), jnp.bfloat16)] * 2 + [pltpu.SemaphoreType.DMA((2, chunks))],
+        scratch_shapes=[pltpu.VMEM((length, width), jnp.bfloat16)] * 3
+        + [pltpu.VMEM((width, length), jnp.bfloat16), pltpu.SemaphoreType.DMA((4, chunks))],
         cost_estimate=pl.CostEstimate(flops=length * width, bytes_accessed=8 * length * width, transcendentals=0),
         name="mix",
     )(key_gate, value_in)

time: 82.9 us -> 82.7 us (level)
  no operation moved by 1% of the time
where the time goes in v9:
time: 82.7 us; the launch traced here: 82.5 us
  blocking collectives  21.6 us (26%)
  starting transfers between devices  20.6 us (25%)
  Pallas kernels  19.4 us (23%)
  waiting for transfers between devices  19.3 us (23%)
    all_to_all x1, blocking collectives, body(): lax.all_to_all(conv_rows.reshape(ctx, few, length), 'ctx', 0, 0)  21.6 us
    ppermute x8, waiting for transfers between devices, ch_shift(): return lax.ppermute(block, 'ch', route)  11.6 us
    all_to_all x1, starting transfers between devices, body(): long_rows = lax.all_to_all(turned.reshape(ctx, few, length), 'ctx', 0, 0)  11.3 us
    ppermute x8, starting transfers between devices, ch_shift(): return lax.ppermute(block, 'ch', route)  9.35 us
    all_to_all x1, waiting for transfers between devices, body(): long_rows = lax.all_to_all(turned.reshape(ctx, few, length), 'ctx', 0, 0)  7.75 us
    pallas_call x1, Pallas kernels, weight_blocks(): pl.pallas_call(functools.partial(weights_kernel, number), grid_spec=pltpu...  4.87 us
    pallas_call x1, Pallas kernels, convolve(): pl.pallas_call(functools.partial(conv_kernel, few), in_specs=[pl.BlockSpe...  4.2 us
    pallas_call x1, Pallas kernels, turned_taps(): pl.pallas_call(functools.partial(taps_kernel, few), grid_spec=pltpu.Prefe...  3.6 us
  transfers between devices with their start and end apart: 9, of which 7 were waited for; matrix products, arithmetic and copies ran while one was open for 2% of the time, Pallas kernels for 19%

profile of v9, /device:TPU:32, one launch (start us, length us, event | category | flops | bytes accessed | tf_op | source)
XLA Modules:
  0.0 82.5 jit_solution(7390470312147192071)
XLA Ops:
  0.0 2.2 %mix.1 = (bf16[512,512]{1,0:T(8,128)(2,1)}, bf16[512,512]{1,0:T(8,128)(2,1)}) custom-call(bf16[512,512]{1,0:T(8,128)(2,1)} %key_ref.1, bf16[512,512]{1,0:T(8,128)(2,1)} %value_ref.1), custom_call_target="tpu_custom_call" | custom-call | flops 262144 | bytes 2097152 | tf_op jit(solution)/shard_map/mix/pallas_call | solution.py:66
  2.2 11.3 %all-to-all-start = ((bf16[32,16,512]{2,1,0:T(8,128)(2,1)}), bf16[32,16,512]{2,1,0:T(8,128)(2,1)}, u32[]{:S(2)}, u32[]{:S(2)}) async-start(bf16[32,16,512]{2,1,0:T(8,128)(2,1)} %bitcast.18), calls=%async_computation | async-start | bytes 1048576 | tf_op jit(solution)/shard_map/all_to_all | solution.py:372
  13.6 0.6 stack.47.blocks_ref
  14.2 4.9 %weight_blocks.1 = (bf16[4,512,512]{2,1,0:T(8,128)(2,1)}, bf16[4,512,512]{2,1,0:T(8,128)(2,1)}) custom-call(s32[8]{0:T(128)} %stack.47.blocks_ref, bf16[512,4096]{1,0:T(8,128)(2,1)} %weight_ref.1), custom_call_target="tpu_custom_call" | custom-call | bytes 8388608 | tf_op jit(solution)/shard_map/weight_blocks/pallas_call | solution.py:251
  19.2 0.6 pad_add_fusion.place_ref
  19.8 3.6 %turned_taps.1.taps_ref = bf16[512,512]{1,0:T(8,128)(2,1)} custom-call(s32[2]{0:T(128)} %pad_add_fusion.place_ref, f32[4096,512]{1,0:T(8,128)} %taps_ref.1), custom_call_target="tpu_custom_call" | custom-call | flops 16777216 | bytes 2097152 | tf_op jit(solution)/shard_map/turned_taps/pallas_call | solution.py:111
  23.4 7.7 %all-to-all-done = bf16[32,16,512]{2,1,0:T(8,128)(2,1)} async-done(((bf16[32,16,512]{2,1,0:T(8,128)(2,1)}), bf16[32,16,512]{2,1,0:T(8,128)(2,1)}, u32[]{:S(2)}, u32[]{:S(2)}) %all-to-all-start) | async-done | bytes 524320 | tf_op jit(solution)/shard_map/all_to_all | solution.py:372
  31.2 4.2 %convolve.1 = bf16[512,512]{1,0:T(8,128)(2,1)S(1)} custom-call(bf16[512,512]{1,0:T(8,128)(2,1)} %bitcast.1.x_ref, bf16[512,512]{1,0:T(8,128)(2,1)} %turned_taps.1.taps_ref, bf16[4,512,256]{2,1,0:T(8,128)(2,1)} %constant.77.clone.table_ref), custom_call_target="tpu_custom_call" | custom-call | flops 1073741824 | bytes 3145728 | tf_op jit(solution)/shard_map/convolve/pallas_call | solution.py:194
  35.4 21.6 %all_to_all.10 = bf16[32,16,512]{2,1,0:T(8,128)(2,1)S(1)} all-to-all(bf16[32,16,512]{2,1,0:T(8,128)(2,1)S(1)} %bitcast.16), channel_id=1, replica_groups=mesh['ctx'=32,'ch'=8] {'ctx'}, dimensions={0} | all-to-all | bytes 1048576 | tf_op jit(solution)/shard_map/all_to_all | solution.py:374
  57.3 1.3 %own_part.1.part_ref = f32[4,512,512]{2,1,0:T(8,128)S(1)} custom-call(bf16[512,512]{1,0:T(8,128)(2,1)S(1)} %gate.1.gated_ref, bf16[4,512,512]{2,1,0:T(8,128)(2,1)S(1)} %copy-done), custom_call_target="tpu_custom_call" | custom-call | flops 1073741824 | bytes 2097152 | tf_op jit(solution)/shard_map/own_part/pallas_call | solution.py:273
  58.6 0.6 collective-permute-done.other_ref
  59.2 0.4 project.3
  59.7 1.6 %collective-permute-start.6 = (bf16[256,512]{1,0:T(8,128)(2,1)S(1)}, bf16[256,512]{1,0:T(8,128)(2,1)S(1)}, u32[]{:S(2)}, u32[]{:S(2)}) collective-permute-start(bf16[256,512]{1,0:T(8,128)(2,1)S(1)} %get-tuple-element.32), channel_id=1, source_target_pairs={{0,2},{1,3},{2,4},{3,5},{4,6},{5,7},{6,0},{7,1},{8,10},{9,11},{10,... | collective-permute-start | bytes 786440 | tf_op jit(solution)/shard_map/ppermute | solution.py:362
  61.3 1.0 %project.2 = (bf16[256,512]{1,0:T(8,128)(2,1)S(1)}, bf16[256,512]{1,0:T(8,128)(2,1)S(1)}, bf16[256,512]{1,0:T(8,128)(2,1)S(1)}, bf16[256,512]{1,0:T(8,128)(2,1)S...) custom-call(f32[4,512,512]{2,1,0:T(8,128)S(1)} %own_part.1.part_ref, ...), custom_call_target="tpu_custom_call" | custom-call | flops 805306368 | bytes 3145728 | tf_op jit(solution)/shard_map/project/pallas_call | solution.py:298
  62.3 1.7 %collective-permute-start.3 = (bf16[256,512]{1,0:T(8,128)(2,1)S(1)}, bf16[256,512]{1,0:T(8,128)(2,1)S(1)}, u32[]{:S(2)}, u32[]{:S(2)}) collective-permute-start(bf16[256,512]{1,0:T(8,128)(2,1)S(1)} %get-tuple-element.28), channel_id=1, source_target_pairs={{0,6},{1,7},{2,0},{3,1},{4,2},{5,3},{6,4},{7,5},{8,14},{9,15},{10,... | collective-permute-start | bytes 786440 | tf_op jit(solution)/shard_map/ppermute | solution.py:362
  64.1 1.8 %collective-permute-start.5 = (bf16[256,512]{1,0:T(8,128)(2,1)S(1)}, bf16[256,512]{1,0:T(8,128)(2,1)S(1)}, u32[]{:S(2)}, u32[]{:S(2)}) collective-permute-start(bf16[256,512]{1,0:T(8,128)(2,1)S(1)} %get-tuple-element.30), channel_id=1, source_target_pairs={{0,6},{1,7},{2,0},{3,1},{4,2},{5,3},{6,4},{7,5},{8,14},{9,15},{10,... | collective-permute-start | bytes 786440 | tf_op jit(solution)/shard_map/ppermute | solution.py:362
  66.1 3.7 %collective-permute-done.6 = bf16[256,512]{1,0:T(8,128)(2,1)S(1)} collective-permute-done((bf16[256,512]{1,0:T(8,128)(2,1)S(1)}, bf16[256,512]{1,0:T(8,128)(2,1)S(1)}, u32[]{:S(2)}, u32[]{:S(2)}) %collective-permute-start.6) | collective-permute-done | bytes 262176 | tf_op jit(solution)/shard_map/ppermute | solution.py:362
  69.9 0.8 collective-permute-start.7
  70.6 0.9 %collective-permute-done.3 = bf16[256,512]{1,0:T(8,128)(2,1)S(1)} collective-permute-done((bf16[256,512]{1,0:T(8,128)(2,1)S(1)}, bf16[256,512]{1,0:T(8,128)(2,1)S(1)}, u32[]{:S(2)}, u32[]{:S(2)}) %collective-permute-start.3) | collective-permute-done | bytes 262176 | tf_op jit(solution)/shard_map/ppermute | solution.py:362
  71.6 3.0 %collective-permute-start.4 = (bf16[256,512]{1,0:T(8,128)(2,1)S(1)}, bf16[256,512]{1,0:T(8,128)(2,1)S(1)}, u32[]{:S(2)}, u32[]{:S(2)}) collective-permute-start(bf16[256,512]{1,0:T(8,128)(2,1)S(1)} %add_convert_fusion.1), channel_id=1, source_target_pairs={{0,6},{1,7},{2,0},{3,1},{4,2},{5,3},{6,4},{7,5},{8,14},{9,15},{10,... | collective-permute-start | bytes 786440 | tf_op jit(solution)/shard_map/ppermute | solution.py:362
  74.6 2.6 %collective-permute-done.5.two_ref = bf16[256,512]{1,0:T(8,128)(2,1)S(1)} collective-permute-done((bf16[256,512]{1,0:T(8,128)(2,1)S(1)}, bf16[256,512]{1,0:T(8,128)(2,1)S(1)}, u32[]{:S(2)}, u32[]{:S(2)}) %collective-permute-start.5) | collective-permute-done | bytes 262176 | tf_op jit(solution)/shard_map/ppermute | solution.py:362
  77.2 3.4 %collective-permute-done.7.three_ref = bf16[256,512]{1,0:T(8,128)(2,1)S(1)} collective-permute-done((bf16[256,512]{1,0:T(8,128)(2,1)S(1)}, bf16[256,512]{1,0:T(8,128)(2,1)S(1)}, u32[]{:S(2)}, u32[]{:S(2)}) %collective-permute-start.7) | collective-permute-done | bytes 262176 | tf_op jit(solution)/shard_map/ppermute | solution.py:362
  80.6 0.8 finish.2.refs_0_
  81.7 0.8 finish.3
  (17 shorter events, 1.1 us)
Async XLA Ops:
  2.2 28.9 %all-to-all-start = ((bf16[32,16,512]{2,1,0:T(8,128)(2,1)}), bf16[32,16,512]{2,1,0:T(8,128)(2,1)}, u32[]{:S(2)}, u32[]{:S(2)}) async-start(bf16[32,16,512]{2,1,0:T(8,128)(2,1)} %bitcast.18), calls=%async_computation | async-start | bytes 1048576 | tf_op jit(solution)/shard_map/all_to_all | solution.py:372
  19.1 39.5 %collective-permute-start.1 = (bf16[4,512,512]{2,1,0:T(8,128)(2,1)}, bf16[4,512,512]{2,1,0:T(8,128)(2,1)S(1)}, u32[]{:S(2)}, u32[]{:S(2)}) collective-permute-start(bf16[4,512,512]{2,1,0:T(8,128)(2,1)} %get-tuple-element.22), channel_id=1, source_target_pairs={{0,1},{1,0},{2,3},{3,2},{4,5},{5,4},{6,7},{7,6},{8,9},{9,8},{10,11... | collective-permute-start | bytes 6291464 | tf_op jit(solution)/shard_map/ppermute | solution.py:362
  23.4 33.6 %copy-start.1 = (bf16[512,512]{1,0:T(8,128)(2,1)S(1)}, bf16[512,512]{1,0:T(8,128)(2,1)}, u32[]{:S(2)}) copy-start(bf16[512,512]{1,0:T(8,128)(2,1)} %query_ref.1) | copy-start | bytes 1572868
  23.4 33.6 %copy-start.2 = (bf16[512,512]{1,0:T(8,128)(2,1)S(1)}, bf16[512,512]{1,0:T(8,128)(2,1)}, u32[]{:S(2)}) copy-start(bf16[512,512]{1,0:T(8,128)(2,1)} %get-tuple-element.20.mixed_ref) | copy-start | bytes 1572868
  23.4 33.6 %copy-start.3 = (f32[512]{0:T(512)S(1)}, f32[512]{0:T(512)}, u32[]{:S(2)}) copy-start(f32[512]{0:T(512)} %param.11) | copy-start | bytes 6148
  31.2 26.2 %copy-start = (bf16[4,512,512]{2,1,0:T(8,128)(2,1)S(1)}, bf16[4,512,512]{2,1,0:T(8,128)(2,1)}, u32[]{:S(2)}) copy-start(bf16[4,512,512]{2,1,0:T(8,128)(2,1)} %get-tuple-element.21.weight_ref) | copy-start | bytes 6291460
  57.2 2.0 %collective-permute-start = (bf16[512,512]{1,0:T(8,128)(2,1)S(1)}, bf16[512,512]{1,0:T(8,128)(2,1)S(1)}, u32[]{:S(2)}, u32[]{:S(2)}) collective-permute-start(bf16[512,512]{1,0:T(8,128)(2,1)S(1)} %gate.1.gated_ref), channel_id=1, source_target_pairs={{0,1},{1,0},{2,3},{3,2},{4,5},{5,4},{6,7},{7,6},{8,9},{9,8},{10,11... | collective-permute-start | bytes 1572872 | tf_op jit(solution)/shard_map/ppermute | solution.py:362
  59.7 10.1 %collective-permute-start.6 = (bf16[256,512]{1,0:T(8,128)(2,1)S(1)}, bf16[256,512]{1,0:T(8,128)(2,1)S(1)}, u32[]{:S(2)}, u32[]{:S(2)}) collective-permute-start(bf16[256,512]{1,0:T(8,128)(2,1)S(1)} %get-tuple-element.32), channel_id=1, source_target_pairs={{0,2},{1,3},{2,4},{3,5},{4,6},{5,7},{6,0},{7,1},{8,10},{9,11},{10,... | collective-permute-start | bytes 786440 | tf_op jit(solution)/shard_map/ppermute | solution.py:362
  62.3 9.3 %collective-permute-start.3 = (bf16[256,512]{1,0:T(8,128)(2,1)S(1)}, bf16[256,512]{1,0:T(8,128)(2,1)S(1)}, u32[]{:S(2)}, u32[]{:S(2)}) collective-permute-start(bf16[256,512]{1,0:T(8,128)(2,1)S(1)} %get-tuple-element.28), channel_id=1, source_target_pairs={{0,6},{1,7},{2,0},{3,1},{4,2},{5,3},{6,4},{7,5},{8,14},{9,15},{10,... | collective-permute-start | bytes 786440 | tf_op jit(solution)/shard_map/ppermute | solution.py:362
  64.1 13.1 %collective-permute-start.5 = (bf16[256,512]{1,0:T(8,128)(2,1)S(1)}, bf16[256,512]{1,0:T(8,128)(2,1)S(1)}, u32[]{:S(2)}, u32[]{:S(2)}) collective-permute-start(bf16[256,512]{1,0:T(8,128)(2,1)S(1)} %get-tuple-element.30), channel_id=1, source_target_pairs={{0,6},{1,7},{2,0},{3,1},{4,2},{5,3},{6,4},{7,5},{8,14},{9,15},{10,... | collective-permute-start | bytes 786440 | tf_op jit(solution)/shard_map/ppermute | solution.py:362
  65.9 15.5 %collective-permute-start.2 = (bf16[256,512]{1,0:T(8,128)(2,1)S(1)}, bf16[256,512]{1,0:T(8,128)(2,1)S(1)}, u32[]{:S(2)}, u32[]{:S(2)}) collective-permute-start(bf16[256,512]{1,0:T(8,128)(2,1)S(1)} %get-tuple-element.26), channel_id=1, source_target_pairs={{0,2},{1,3},{2,4},{3,5},{4,6},{5,7},{6,0},{7,1},{8,10},{9,11},{10,... | collective-permute-start | bytes 786440 | tf_op jit(solution)/shard_map/ppermute | solution.py:362
  69.9 10.7 %collective-permute-start.7 = (bf16[256,512]{1,0:T(8,128)(2,1)S(1)}, bf16[256,512]{1,0:T(8,128)(2,1)S(1)}, u32[]{:S(2)}, u32[]{:S(2)}) collective-permute-start(bf16[256,512]{1,0:T(8,128)(2,1)S(1)} %add_convert_fusion), channel_id=1, source_target_pairs={{0,2},{1,3},{2,4},{3,5},{4,6},{5,7},{6,0},{7,1},{8,10},{9,11},{10,... | collective-permute-start | bytes 786440 | tf_op jit(solution)/shard_map/ppermute | solution.py:362
  71.6 10.1 %collective-permute-start.4 = (bf16[256,512]{1,0:T(8,128)(2,1)S(1)}, bf16[256,512]{1,0:T(8,128)(2,1)S(1)}, u32[]{:S(2)}, u32[]{:S(2)}) collective-permute-start(bf16[256,512]{1,0:T(8,128)(2,1)S(1)} %add_convert_fusion.1), channel_id=1, source_target_pairs={{0,6},{1,7},{2,0},{3,1},{4,2},{5,3},{6,4},{7,5},{8,14},{9,15},{10,... | collective-permute-start | bytes 786440 | tf_op jit(solution)/shard_map/ppermute | solution.py:362

commit v10 on v9

--- a/solution.py
+++ b/solution.py
@@ -136,13 +136,18 @@
     copies = [
         pltpu.make_async_copy(x_ref, rows, sems.at[0]),
         pltpu.make_async_copy(taps_ref.at[pl.ds(0, WIN * few)], tap_rows, sems.at[1]),
-        pltpu.make_async_copy(table_ref, table, sems.at[2]),
+        pltpu.make_async_copy(table_ref.at[pl.ds(0, tiles // 2)], table.at[pl.ds(0, tiles // 2)], sems.at[2]),
+        pltpu.make_async_copy(
+            table_ref.at[pl.ds(tiles // 2, tiles // 2)], table.at[pl.ds(tiles // 2, tiles // 2)], sems.at[3]
+        ),
     ]
     for copy in copies:
         copy.start()
-    for copy in copies:
+    for copy in copies[:3]:
         copy.wait()
     for tile in range(tiles):
+        if tile == tiles // 2:
+            copies[3].wait()
         spectrum = jnp.dot(rows[...], table[tile], preferred_element_type=jnp.float32)
         taps = jnp.dot(tap_rows[...], table[tile], preferred_element_type=jnp.float32)
         sign = 1.0 if tile < tiles // 2 else -1.0
@@ -202,7 +207,7 @@
             pltpu.VMEM(table.shape, jnp.bfloat16),
             pltpu.VMEM((tiles, 3, count, LANES), jnp.float32),
             pltpu.VMEM((tiles, count, pair), jnp.bfloat16),
-            pltpu.SemaphoreType.DMA((3,)),
+            pltpu.SemaphoreType.DMA((4,)),
         ],
         compiler_params=pltpu.CompilerParams(vmem_limit_bytes=CONV_BYTES),
         cost_estimate=pl.CostEstimate(

time: 82.7 us -> 82.8 us (level)
  no operation moved by 1% of the time
where the time goes in v10:
time: 82.8 us; the launch traced here: 82.5 us
  blocking collectives  21.6 us (26%)
  starting transfers between devices  20.6 us (25%)
  Pallas kernels  19.4 us (23%)
  waiting for transfers between devices  19.3 us (23%)
    all_to_all x1, blocking collectives, body(): lax.all_to_all(conv_rows.reshape(ctx, few, length), 'ctx', 0, 0)  21.6 us
    ppermute x8, waiting for transfers between devices, ch_shift(): return lax.ppermute(block, 'ch', route)  11.6 us
    all_to_all x1, starting transfers between devices, body(): long_rows = lax.all_to_all(turned.reshape(ctx, few, length), 'ctx', 0, 0)  11.3 us
    ppermute x8, starting transfers between devices, ch_shift(): return lax.ppermute(block, 'ch', route)  9.34 us
    all_to_all x1, waiting for transfers between devices, body(): long_rows = lax.all_to_all(turned.reshape(ctx, few, length), 'ctx', 0, 0)  7.75 us
    pallas_call x1, Pallas kernels, weight_blocks(): pl.pallas_call(functools.partial(weights_kernel, number), grid_spec=pltpu...  4.87 us
    pallas_call x1, Pallas kernels, convolve(): pl.pallas_call(functools.partial(conv_kernel, few), in_specs=[pl.BlockSpe...  4.23 us
    pallas_call x1, Pallas kernels, turned_taps(): pl.pallas_call(functools.partial(taps_kernel, few), grid_spec=pltpu.Prefe...  3.6 us
  transfers between devices with their start and end apart: 9, of which 7 were waited for; matrix products, arithmetic and copies ran while one was open for 2% of the time, Pallas kernels for 19%

profile of v10, /device:TPU:32, one launch (start us, length us, event | category | flops | bytes accessed | tf_op | source)
XLA Modules:
  0.0 82.5 jit_solution(16691335469642685605)
XLA Ops:
  0.0 2.2 %mix.1 = (bf16[512,512]{1,0:T(8,128)(2,1)}, bf16[512,512]{1,0:T(8,128)(2,1)}) custom-call(bf16[512,512]{1,0:T(8,128)(2,1)} %key_ref.1, bf16[512,512]{1,0:T(8,128)(2,1)} %value_ref.1), custom_call_target="tpu_custom_call" | custom-call | flops 262144 | bytes 2097152 | tf_op jit(solution)/shard_map/mix/pallas_call | solution.py:66
  2.2 11.3 %all-to-all-start = ((bf16[32,16,512]{2,1,0:T(8,128)(2,1)}), bf16[32,16,512]{2,1,0:T(8,128)(2,1)}, u32[]{:S(2)}, u32[]{:S(2)}) async-start(bf16[32,16,512]{2,1,0:T(8,128)(2,1)} %bitcast.18), calls=%async_computation | async-start | bytes 1048576 | tf_op jit(solution)/shard_map/all_to_all | solution.py:377
  13.6 0.6 stack.47.blocks_ref
  14.2 4.9 %weight_blocks.1 = (bf16[4,512,512]{2,1,0:T(8,128)(2,1)}, bf16[4,512,512]{2,1,0:T(8,128)(2,1)}) custom-call(s32[8]{0:T(128)} %stack.47.blocks_ref, bf16[512,4096]{1,0:T(8,128)(2,1)} %weight_ref.1), custom_call_target="tpu_custom_call" | custom-call | bytes 8388608 | tf_op jit(solution)/shard_map/weight_blocks/pallas_call | solution.py:256
  19.2 0.6 pad_add_fusion.place_ref
  19.8 3.6 %turned_taps.1.taps_ref = bf16[512,512]{1,0:T(8,128)(2,1)} custom-call(s32[2]{0:T(128)} %pad_add_fusion.place_ref, f32[4096,512]{1,0:T(8,128)} %taps_ref.1), custom_call_target="tpu_custom_call" | custom-call | flops 16777216 | bytes 2097152 | tf_op jit(solution)/shard_map/turned_taps/pallas_call | solution.py:111
  23.4 7.7 %all-to-all-done = bf16[32,16,512]{2,1,0:T(8,128)(2,1)} async-done(((bf16[32,16,512]{2,1,0:T(8,128)(2,1)}), bf16[32,16,512]{2,1,0:T(8,128)(2,1)}, u32[]{:S(2)}, u32[]{:S(2)}) %all-to-all-start) | async-done | bytes 524320 | tf_op jit(solution)/shard_map/all_to_all | solution.py:377
  31.2 4.2 %convolve.1 = bf16[512,512]{1,0:T(8,128)(2,1)S(1)} custom-call(bf16[512,512]{1,0:T(8,128)(2,1)} %bitcast.1.x_ref, bf16[512,512]{1,0:T(8,128)(2,1)} %turned_taps.1.taps_ref, bf16[4,512,256]{2,1,0:T(8,128)(2,1)} %constant.77.clone.table_ref), custom_call_target="tpu_custom_call" | custom-call | flops 1073741824 | bytes 3145728 | tf_op jit(solution)/shard_map/convolve/pallas_call | solution.py:199
  35.4 21.6 %all_to_all.10 = bf16[32,16,512]{2,1,0:T(8,128)(2,1)S(1)} all-to-all(bf16[32,16,512]{2,1,0:T(8,128)(2,1)S(1)} %bitcast.16), channel_id=1, replica_groups=mesh['ctx'=32,'ch'=8] {'ctx'}, dimensions={0} | all-to-all | bytes 1048576 | tf_op jit(solution)/shard_map/all_to_all | solution.py:379
  57.4 1.3 %own_part.1.part_ref = f32[4,512,512]{2,1,0:T(8,128)S(1)} custom-call(bf16[512,512]{1,0:T(8,128)(2,1)S(1)} %gate.1.gated_ref, bf16[4,512,512]{2,1,0:T(8,128)(2,1)S(1)} %copy-done), custom_call_target="tpu_custom_call" | custom-call | flops 1073741824 | bytes 2097152 | tf_op jit(solution)/shard_map/own_part/pallas_call | solution.py:278
  58.6 0.6 collective-permute-done.other_ref
  59.3 0.4 project.3
  59.7 1.7 %collective-permute-start.6 = (bf16[256,512]{1,0:T(8,128)(2,1)S(1)}, bf16[256,512]{1,0:T(8,128)(2,1)S(1)}, u32[]{:S(2)}, u32[]{:S(2)}) collective-permute-start(bf16[256,512]{1,0:T(8,128)(2,1)S(1)} %get-tuple-element.32), channel_id=1, source_target_pairs={{0,2},{1,3},{2,4},{3,5},{4,6},{5,7},{6,0},{7,1},{8,10},{9,11},{10,... | collective-permute-start | bytes 786440 | tf_op jit(solution)/shard_map/ppermute | solution.py:367
  61.4 1.0 %project.2 = (bf16[256,512]{1,0:T(8,128)(2,1)S(1)}, bf16[256,512]{1,0:T(8,128)(2,1)S(1)}, bf16[256,512]{1,0:T(8,128)(2,1)S(1)}, bf16[256,512]{1,0:T(8,128)(2,1)S...) custom-call(f32[4,512,512]{2,1,0:T(8,128)S(1)} %own_part.1.part_ref, ...), custom_call_target="tpu_custom_call" | custom-call | flops 805306368 | bytes 3145728 | tf_op jit(solution)/shard_map/project/pallas_call | solution.py:303
  62.4 1.7 %collective-permute-start.3 = (bf16[256,512]{1,0:T(8,128)(2,1)S(1)}, bf16[256,512]{1,0:T(8,128)(2,1)S(1)}, u32[]{:S(2)}, u32[]{:S(2)}) collective-permute-start(bf16[256,512]{1,0:T(8,128)(2,1)S(1)} %get-tuple-element.28), channel_id=1, source_target_pairs={{0,6},{1,7},{2,0},{3,1},{4,2},{5,3},{6,4},{7,5},{8,14},{9,15},{10,... | collective-permute-start | bytes 786440 | tf_op jit(solution)/shard_map/ppermute | solution.py:367
  64.1 1.8 %collective-permute-start.5 = (bf16[256,512]{1,0:T(8,128)(2,1)S(1)}, bf16[256,512]{1,0:T(8,128)(2,1)S(1)}, u32[]{:S(2)}, u32[]{:S(2)}) collective-permute-start(bf16[256,512]{1,0:T(8,128)(2,1)S(1)} %get-tuple-element.30), channel_id=1, source_target_pairs={{0,6},{1,7},{2,0},{3,1},{4,2},{5,3},{6,4},{7,5},{8,14},{9,15},{10,... | collective-permute-start | bytes 786440 | tf_op jit(solution)/shard_map/ppermute | solution.py:367
  66.1 3.7 %collective-permute-done.6 = bf16[256,512]{1,0:T(8,128)(2,1)S(1)} collective-permute-done((bf16[256,512]{1,0:T(8,128)(2,1)S(1)}, bf16[256,512]{1,0:T(8,128)(2,1)S(1)}, u32[]{:S(2)}, u32[]{:S(2)}) %collective-permute-start.6) | collective-permute-done | bytes 262176 | tf_op jit(solution)/shard_map/ppermute | solution.py:367
  69.9 0.8 collective-permute-start.7
  70.7 0.9 %collective-permute-done.3 = bf16[256,512]{1,0:T(8,128)(2,1)S(1)} collective-permute-done((bf16[256,512]{1,0:T(8,128)(2,1)S(1)}, bf16[256,512]{1,0:T(8,128)(2,1)S(1)}, u32[]{:S(2)}, u32[]{:S(2)}) %collective-permute-start.3) | collective-permute-done | bytes 262176 | tf_op jit(solution)/shard_map/ppermute | solution.py:367
  71.7 2.9 %collective-permute-start.4 = (bf16[256,512]{1,0:T(8,128)(2,1)S(1)}, bf16[256,512]{1,0:T(8,128)(2,1)S(1)}, u32[]{:S(2)}, u32[]{:S(2)}) collective-permute-start(bf16[256,512]{1,0:T(8,128)(2,1)S(1)} %add_convert_fusion.1), channel_id=1, source_target_pairs={{0,6},{1,7},{2,0},{3,1},{4,2},{5,3},{6,4},{7,5},{8,14},{9,15},{10,... | collective-permute-start | bytes 786440 | tf_op jit(solution)/shard_map/ppermute | solution.py:367
  74.6 2.6 %collective-permute-done.5.two_ref = bf16[256,512]{1,0:T(8,128)(2,1)S(1)} collective-permute-done((bf16[256,512]{1,0:T(8,128)(2,1)S(1)}, bf16[256,512]{1,0:T(8,128)(2,1)S(1)}, u32[]{:S(2)}, u32[]{:S(2)}) %collective-permute-start.5) | collective-permute-done | bytes 262176 | tf_op jit(solution)/shard_map/ppermute | solution.py:367
  77.2 3.4 %collective-permute-done.7.three_ref = bf16[256,512]{1,0:T(8,128)(2,1)S(1)} collective-permute-done((bf16[256,512]{1,0:T(8,128)(2,1)S(1)}, bf16[256,512]{1,0:T(8,128)(2,1)S(1)}, u32[]{:S(2)}, u32[]{:S(2)}) %collective-permute-start.7) | collective-permute-done | bytes 262176 | tf_op jit(solution)/shard_map/ppermute | solution.py:367
  80.6 0.8 finish.2.refs_0_
  81.7 0.8 finish.3
  (17 shorter events, 1.1 us)
Async XLA Ops:
  2.2 28.9 %all-to-all-start = ((bf16[32,16,512]{2,1,0:T(8,128)(2,1)}), bf16[32,16,512]{2,1,0:T(8,128)(2,1)}, u32[]{:S(2)}, u32[]{:S(2)}) async-start(bf16[32,16,512]{2,1,0:T(8,128)(2,1)} %bitcast.18), calls=%async_computation | async-start | bytes 1048576 | tf_op jit(solution)/shard_map/all_to_all | solution.py:377
  19.1 39.6 %collective-permute-start.1 = (bf16[4,512,512]{2,1,0:T(8,128)(2,1)}, bf16[4,512,512]{2,1,0:T(8,128)(2,1)S(1)}, u32[]{:S(2)}, u32[]{:S(2)}) collective-permute-start(bf16[4,512,512]{2,1,0:T(8,128)(2,1)} %get-tuple-element.22), channel_id=1, source_target_pairs={{0,1},{1,0},{2,3},{3,2},{4,5},{5,4},{6,7},{7,6},{8,9},{9,8},{10,11... | collective-permute-start | bytes 6291464 | tf_op jit(solution)/shard_map/ppermute | solution.py:367
  23.4 33.6 %copy-start.1 = (bf16[512,512]{1,0:T(8,128)(2,1)S(1)}, bf16[512,512]{1,0:T(8,128)(2,1)}, u32[]{:S(2)}) copy-start(bf16[512,512]{1,0:T(8,128)(2,1)} %query_ref.1) | copy-start | bytes 1572868
  23.4 33.6 %copy-start.2 = (bf16[512,512]{1,0:T(8,128)(2,1)S(1)}, bf16[512,512]{1,0:T(8,128)(2,1)}, u32[]{:S(2)}) copy-start(bf16[512,512]{1,0:T(8,128)(2,1)} %get-tuple-element.20.mixed_ref) | copy-start | bytes 1572868
  23.4 33.6 %copy-start.3 = (f32[512]{0:T(512)S(1)}, f32[512]{0:T(512)}, u32[]{:S(2)}) copy-start(f32[512]{0:T(512)} %param.11) | copy-start | bytes 6148
  31.2 26.2 %copy-start = (bf16[4,512,512]{2,1,0:T(8,128)(2,1)S(1)}, bf16[4,512,512]{2,1,0:T(8,128)(2,1)}, u32[]{:S(2)}) copy-start(bf16[4,512,512]{2,1,0:T(8,128)(2,1)} %get-tuple-element.21.weight_ref) | copy-start | bytes 6291460
  57.3 2.0 %collective-permute-start = (bf16[512,512]{1,0:T(8,128)(2,1)S(1)}, bf16[512,512]{1,0:T(8,128)(2,1)S(1)}, u32[]{:S(2)}, u32[]{:S(2)}) collective-permute-start(bf16[512,512]{1,0:T(8,128)(2,1)S(1)} %gate.1.gated_ref), channel_id=1, source_target_pairs={{0,1},{1,0},{2,3},{3,2},{4,5},{5,4},{6,7},{7,6},{8,9},{9,8},{10,11... | collective-permute-start | bytes 1572872 | tf_op jit(solution)/shard_map/ppermute | solution.py:367
  59.7 10.1 %collective-permute-start.6 = (bf16[256,512]{1,0:T(8,128)(2,1)S(1)}, bf16[256,512]{1,0:T(8,128)(2,1)S(1)}, u32[]{:S(2)}, u32[]{:S(2)}) collective-permute-start(bf16[256,512]{1,0:T(8,128)(2,1)S(1)} %get-tuple-element.32), channel_id=1, source_target_pairs={{0,2},{1,3},{2,4},{3,5},{4,6},{5,7},{6,0},{7,1},{8,10},{9,11},{10,... | collective-permute-start | bytes 786440 | tf_op jit(solution)/shard_map/ppermute | solution.py:367
  62.4 9.3 %collective-permute-start.3 = (bf16[256,512]{1,0:T(8,128)(2,1)S(1)}, bf16[256,512]{1,0:T(8,128)(2,1)S(1)}, u32[]{:S(2)}, u32[]{:S(2)}) collective-permute-start(bf16[256,512]{1,0:T(8,128)(2,1)S(1)} %get-tuple-element.28), channel_id=1, source_target_pairs={{0,6},{1,7},{2,0},{3,1},{4,2},{5,3},{6,4},{7,5},{8,14},{9,15},{10,... | collective-permute-start | bytes 786440 | tf_op jit(solution)/shard_map/ppermute | solution.py:367
  64.1 13.1 %collective-permute-start.5 = (bf16[256,512]{1,0:T(8,128)(2,1)S(1)}, bf16[256,512]{1,0:T(8,128)(2,1)S(1)}, u32[]{:S(2)}, u32[]{:S(2)}) collective-permute-start(bf16[256,512]{1,0:T(8,128)(2,1)S(1)} %get-tuple-element.30), channel_id=1, source_target_pairs={{0,6},{1,7},{2,0},{3,1},{4,2},{5,3},{6,4},{7,5},{8,14},{9,15},{10,... | collective-permute-start | bytes 786440 | tf_op jit(solution)/shard_map/ppermute | solution.py:367
  65.9 15.5 %collective-permute-start.2 = (bf16[256,512]{1,0:T(8,128)(2,1)S(1)}, bf16[256,512]{1,0:T(8,128)(2,1)S(1)}, u32[]{:S(2)}, u32[]{:S(2)}) collective-permute-start(bf16[256,512]{1,0:T(8,128)(2,1)S(1)} %get-tuple-element.26), channel_id=1, source_target_pairs={{0,2},{1,3},{2,4},{3,5},{4,6},{5,7},{6,0},{7,1},{8,10},{9,11},{10,... | collective-permute-start | bytes 786440 | tf_op jit(solution)/shard_map/ppermute | solution.py:367
  69.9 10.7 %collective-permute-start.7 = (bf16[256,512]{1,0:T(8,128)(2,1)S(1)}, bf16[256,512]{1,0:T(8,128)(2,1)S(1)}, u32[]{:S(2)}, u32[]{:S(2)}) collective-permute-start(bf16[256,512]{1,0:T(8,128)(2,1)S(1)} %add_convert_fusion), channel_id=1, source_target_pairs={{0,2},{1,3},{2,4},{3,5},{4,6},{5,7},{6,0},{7,1},{8,10},{9,11},{10,... | collective-permute-start | bytes 786440 | tf_op jit(solution)/shard_map/ppermute | solution.py:367
  71.7 10.1 %collective-permute-start.4 = (bf16[256,512]{1,0:T(8,128)(2,1)S(1)}, bf16[256,512]{1,0:T(8,128)(2,1)S(1)}, u32[]{:S(2)}, u32[]{:S(2)}) collective-permute-start(bf16[256,512]{1,0:T(8,128)(2,1)S(1)} %add_convert_fusion.1), channel_id=1, source_target_pairs={{0,6},{1,7},{2,0},{3,1},{4,2},{5,3},{6,4},{7,5},{8,14},{9,15},{10,... | collective-permute-start | bytes 786440 | tf_op jit(solution)/shard_map/ppermute | solution.py:367
